TPU v7x, 32 devices: a whole 2x2x4 slice. The times are simulated.
32 devices in a mesh: pose: 4 (over y, core), slab: 8 (over z, x).
Axes of the slice: x: 2, y: 2, z: 4, core: 2. Of those that a mesh axis runs over, the one named last changes fastest.
Arguments:
- coords: float32 [4, 3, 2048], P('pose'), may hold values from -12 to 12, as said below
- atom_types: int32 [4, 2048], P('pose'), may hold values from 0 to 27
- counts: int32 [4], P('pose'), may hold values from 1024 to 2048, as said below
- labels: int32 [4], P('pose'), may hold values from 0 to 1
- receptor_density: bfloat16 [4, 28, 16, 4096], P('pose', None, 'slab'), may hold values from 0 to 1.5
- type_radii: float32 [28], replicated, may hold values from 1.2 to 2.2
- w_stem: bfloat16 [32, 28, 3, 3, 3], replicated, may hold values from -1.25 to 1.25
- w_one: bfloat16 [32, 32, 3, 3, 3], replicated, may hold values from -0.21875 to 0.21875
- w_two: bfloat16 [32, 32, 3, 3, 3], replicated, may hold values from -0.21875 to 0.21875
- w_head: float32 [32], replicated, may hold values from -8 to 8
Outputs:
- scores: float32 [4], P('pose')
- pose_loss: float32 [4], P('pose')
- atom_grad: float32 [4, 3, 2048], P('pose')
- grad_stem: float32 [32, 28, 3, 3, 3], replicated
- grad_one: float32 [32, 32, 3, 3, 3], replicated
- grad_two: float32 [32, 32, 3, 3, 3], replicated
- grad_head: float32 [32], replicated
Inputs may be any that keep to these rules, and one draw needn't show every extreme that they name: The live atoms of a pose are the first counts[p] slots; every pose has 1024 or more of them, and some pose has all 2048. `coords`: every atom lies inside the box of the grid, 0.75 or more from its faces.
All inputs are finite; a program needn't handle non-finite values.
Results may differ from a plain program's by a relative error of at most 0.005.
The roundings to bfloat16 on the way count: a program that leaves them out, or rounds other values in their place, can miss the bound.
Values may be sent and summed in bfloat16 or wider, within the bound.
No kernel may reach another device: no remote copies, remote signals or barrier semaphores. Data moves between devices by JAX's collectives and lax.ppermute only.
A program may use at most 256 MiB of HBM per device.

v0:
```python
import jax
import jax.numpy as jnp
from jax import lax
from jax.sharding import PartitionSpec as P

NXY = 64
CZ = 2


resolution = 0.375
conv_dims = ("NCDHW", "OIDHW", "NCDHW")
grad_dims = ("CNDHW", "IODHW", "NCDHW")


def extended(cells, sides, width):
    for axis, dim in sides:
        count = lax.axis_size(axis)
        ends = count - 1
        head = lax.slice_in_dim(cells, 0, width, axis=dim)
        tail = lax.slice_in_dim(cells, cells.shape[dim] - width, cells.shape[dim], axis=dim)
        cells = jnp.concatenate(
            [
                lax.ppermute(tail, axis, [(i, (i + 1) % count) for i in range(ends)]),
                cells,
                lax.ppermute(head, axis, [((i + 1) % count, i) for i in range(ends)]),
            ],
            axis=dim,
        )
    return cells


def gauss_table(centres, places, inv_sq):
    offset = centres[None, :, None] - places[:, None, :]
    bumps = jnp.exp(-2.0 * offset * offset * inv_sq[:, None, :])
    return (bumps, 4.0 * offset * inv_sq[:, None, :] * bumps)


def spatial(volume):
    return volume.reshape(volume.shape[0], volume.shape[1], volume.shape[2], NXY, NXY)


def flatten(volume):
    return volume.reshape(volume.shape[0], volume.shape[1], volume.shape[2], NXY * NXY)


def conv_valid(padded, kernel):
    result = lax.conv_general_dilated(
        spatial(padded),
        kernel,
        (1, 1, 1),
        [(0, 0), (1, 1), (1, 1)],
        dimension_numbers=conv_dims,
        preferred_element_type=jnp.float32,
    )
    return flatten(result)


def flipped(kernel):
    return jnp.flip(kernel, (2, 3, 4)).transpose(1, 0, 2, 3, 4)


def kernel_grad(padded, upstream):
    result = lax.conv_general_dilated(
        spatial(padded),
        spatial(upstream),
        (1, 1, 1),
        [(0, 0), (1, 1), (1, 1)],
        dimension_numbers=grad_dims,
        preferred_element_type=jnp.float32,
    )
    return result.transpose(1, 0, 2, 3, 4)


def with_rims(volume):
    return extended(volume, (("slab", 2),), 1)


def to_grid(row_cols, plane_count, type_count):
    pose_count = row_cols.shape[0]
    volume = row_cols.reshape(pose_count, plane_count, NXY, type_count, NXY).transpose(
        0, 3, 1, 2, 4
    )
    return volume.reshape(pose_count, type_count, plane_count, NXY * NXY)


def local(
    coords, atom_types, counts, labels, receptor_density, type_radii, w_stem, w_one, w_two, w_head
):
    pose_count = coords.shape[0]
    atom_count = coords.shape[2]
    type_count = type_radii.shape[0]
    slab_count = lax.axis_size("slab")
    total_depth = CZ * slab_count
    cell_count = total_depth * NXY * NXY
    start_plane = lax.axis_index("slab") * CZ
    highest = lax.Precision.HIGHEST
    centres_xy = (jnp.arange(NXY, dtype=jnp.float32) + 0.5 - 0.5 * NXY) * resolution
    kind_ids = jnp.arange(type_count, dtype=jnp.int32)
    type_hits = (atom_types[:, None, :] == kind_ids[None, :, None]).astype(jnp.float32)
    alive = (jnp.arange(atom_count, dtype=jnp.int32)[None, :] < counts[:, None]).astype(jnp.float32)
    live_types = type_hits * alive[:, None, :]
    radius = jnp.sum(type_hits * type_radii[None, :, None], axis=1)
    inv_sq = 1.0 / (radius * radius)
    gauss_x, slope_x = gauss_table(centres_xy, coords[:, 0], inv_sq)
    gauss_y, slope_y = gauss_table(centres_xy, coords[:, 1], inv_sq)
    across_table = (
        (live_types[:, :, None, :] * gauss_y[:, None])
        .reshape(pose_count, type_count * NXY, atom_count)
        .astype(jnp.bfloat16)
    )
    slope_table = (
        (live_types[:, :, None, :] * slope_y[:, None])
        .reshape(pose_count, type_count * NXY, atom_count)
        .astype(jnp.bfloat16)
    )
    plane_count = CZ + 2 * 0
    planes = start_plane - 0 + jnp.arange(plane_count, dtype=jnp.int32)
    inside = ((planes >= 0) & (planes < total_depth)).astype(jnp.float32)
    centres_z = (planes.astype(jnp.float32) + 0.5 - 0.5 * total_depth) * resolution
    gauss_z, slope_z = gauss_table(centres_z, coords[:, 2], inv_sq)
    gauss_z = gauss_z * inside[None, :, None]
    depth_table = (
        (gauss_z[:, :, None, :] * gauss_x[:, None])
        .reshape(pose_count, plane_count * NXY, atom_count)
        .astype(jnp.bfloat16)
    )
    row_cols = jnp.einsum(
        "pra,pqa->prq", depth_table, across_table, preferred_element_type=jnp.float32
    )
    splat, gauss_z, slope_z, inside = (
        to_grid(row_cols, plane_count, type_count),
        gauss_z,
        slope_z,
        inside,
    )
    density = (splat + receptor_density.astype(jnp.float32)).astype(jnp.bfloat16)
    density_pad = with_rims(density)
    stem_pre = conv_valid(density_pad, w_stem)
    hidden_one = jnp.maximum(stem_pre, 0.0).astype(jnp.bfloat16)
    hidden_pad = with_rims(hidden_one)
    second_pre = conv_valid(hidden_pad, w_one)
    hidden_two = jnp.maximum(second_pre, 0.0).astype(jnp.bfloat16)
    two_pad = with_rims(hidden_two)
    summed = hidden_one.astype(jnp.float32) + conv_valid(two_pad, w_two)
    part_pool = jnp.sum(jnp.maximum(summed, 0.0), axis=(2, 3)) / cell_count
    pooled = lax.psum(part_pool, "slab")
    scores = jnp.sum(pooled * w_head[None, :], axis=1)
    label_sign = (2 * labels - 1).astype(jnp.float32)
    pose_loss = jax.nn.softplus(-label_sign * scores)
    score_grad = -label_sign * jax.nn.sigmoid(-label_sign * scores)
    head_term = jnp.sum(score_grad[:, None] * part_pool, axis=0)
    top_grad = jnp.where(
        summed > 0, (score_grad[:, None] * w_head[None, :])[:, :, None, None], 0.0
    ).astype(jnp.bfloat16)
    grad_two_local = kernel_grad(two_pad, top_grad) / cell_count
    back_two = conv_valid(with_rims(top_grad), flipped(w_two))
    mid_grad = jnp.where(second_pre > 0, back_two, 0.0).astype(jnp.bfloat16)
    grad_one_local = kernel_grad(hidden_pad, mid_grad) / cell_count
    back_one = top_grad.astype(jnp.float32) + conv_valid(with_rims(mid_grad), flipped(w_one))
    stem_grad = jnp.where(stem_pre > 0, back_one, 0.0).astype(jnp.bfloat16)
    grad_stem_local = kernel_grad(density_pad, stem_grad) / cell_count
    density_grad = conv_valid(with_rims(stem_grad), flipped(w_stem)).astype(jnp.bfloat16)
    grid_rows = (
        density_grad.reshape(pose_count, type_count, CZ, NXY, NXY)
        .transpose(0, 2, 3, 1, 4)
        .reshape(pose_count, CZ * NXY, type_count * NXY)
    )
    rows_plain = jnp.einsum(
        "prq,pqa->pra", grid_rows, across_table, preferred_element_type=jnp.float32
    ).reshape(pose_count, CZ, NXY, atom_count)
    rows_slope = jnp.einsum(
        "prq,pqa->pra", grid_rows, slope_table, preferred_element_type=jnp.float32
    ).reshape(pose_count, CZ, NXY, atom_count)
    along_x = jnp.einsum("pzxa,pza,pxa->pa", rows_plain, gauss_z, slope_x, precision=highest)
    along_y = jnp.einsum("pzxa,pza,pxa->pa", rows_slope, gauss_z, gauss_x, precision=highest)
    along_z = jnp.einsum("pzxa,pza,pxa->pa", rows_plain, slope_z, gauss_x, precision=highest)
    local_force = jnp.stack([along_x, along_y, along_z], axis=1)
    atom_grad = lax.psum(local_force, "slab")
    grad_stem, grad_one, grad_two, grad_head = lax.psum(
        (grad_stem_local, grad_one_local, grad_two_local, head_term), ("pose", "slab")
    )
    return (scores, pose_loss, atom_grad, grad_stem, grad_one, grad_two, grad_head)


def solution(mesh):
    return jax.shard_map(
        local,
        mesh=mesh,
        in_specs=(
            P("pose", None, None),
            P("pose", None),
            P("pose"),
            P("pose"),
            P("pose", None, "slab", None),
            P(),
            P(),
            P(),
            P(),
            P(),
        ),
        out_specs=(P("pose"), P("pose"), P("pose", None, None), P(), P(), P(), P()),
        check_vma=False,
    )
```

profile of v0, /device:TPU:0, one launch (start us, length us, event | category | flops | bytes accessed | tf_op | source)
XLA Modules:
  0.0 759.1 jit_solution(6189887699078458096)
XLA Ops:
  22.2 6.3 collective-permute-start
  28.5 10.0 %multiply_convert_fusion = (bf16[28,64,2048]{2,1,0:T(8,128)(2,1)}, bf16[28,64,2048]{2,1,0:T(8,128)(2,1)}) fusion(f32[64,2048]{1,0:T(8,128)S(1)} %get-tuple-element.100, f32[28,2048]{1,0:T(8,128)S(1)} %fusion.158, f32[64,2048]{1,0:T(8,128)S(1)} %get-tuple-element.101), kind=kLoop, calls=%fused_computation | loop fusion | flops 14680064 | bytes 15958016 | tf_op jit(solution)/shard_map/convert_element_type | solution.py:114
  62.9 8.6 %copy.334 = bf16[28,4,64,1,8,9]{0,4,5,2,1,3:T(8,128)(2,1)} copy(bf16[28,4,64,1,8,9]{2,1,5,4,0,3:T(4,128)(2,1)} %bitcast.277) | data formatting | bytes 2064384 | tf_op jit(solution)/shard_map/conv_general_dilated | solution.py:47
  73.1 11.6 %maximum_convert_fusion.1 = (bf16[2,64,8,9,32]{4,2,3,1,0:T(8,128)(2,1)}, f32[2,64,8,9,32]{4,2,3,1,0:T(8,128)}) fusion(pred[8,9]{0,1:T(8,128)(4,1)S(1)} %copy-done.10, bf16[32,28,3,3,3]{1,0,4,3,2:T(8,128)(2,1)S(1)} %copy-done.13, bf16[28,4,64,1,7,2]{0,4,5,2,1,3:T(8,128)(2,1)S(1)} %slice.89, bf16[28,4,64,1,8,9]{0,4,5,2,1,3:T(8,128)(2,1)} %copy.334), kind=kOutput, calls=%fused_computation.94 | convolution fusion | flops 446226432 | bytes 3050824 | tf_op jit(solution)/shard_map/conv_general_dilated | solution.py:47
  97.8 5.8 collective-permute-start.2
  105.7 8.1 %copy.434 = bf16[28,4,64,1,8,8]{0,4,5,2,1,3:T(8,128)(2,1)} copy(bf16[28,4,64,1,8,8]{2,1,5,4,0,3:T(4,128)(2,1)} %get-tuple-element.78) | data formatting | bytes 1835008
  113.9 7.7 %copy.433 = bf16[28,4,64,1,8,8]{0,4,5,2,1,3:T(8,128)(2,1)} copy(bf16[28,4,64,1,8,8]{2,1,5,4,0,3:T(4,128)(2,1)} %get-tuple-element.77) | data formatting | bytes 1835008
  122.7 9.0 %fusion.75 = (bf16[28,4,64,8,9,1]{0,3,5,4,2,1:T(8,128)(2,1)}, bf16[28,4,64,8,9,1]{0,3,5,4,2,1:T(8,128)(2,1)}) fusion(bf16[28,4,64,1,7,1]{0,4,5,2,1,3:T(8,128)(2,1)} %copy.435, bf16[28,4,64,1,8,8]{0,4,5,2,1,3:T(8,128)(2,1)} %copy.434, bf16[28,4,64,1,8,8]{0,4,5,2,1,3:T(8,128)(2,1)} %copy.433, bf16[28,4,64,1,7,1]{0,4,5,2,1,3:T(8,128)(2,1)} %copy.432), kind=kLoop, calls=%fused_computation.77 | loop fusion | flops 6193152 | bytes 4100096 | tf_op jit(solution)/shard_map/reshape | solution.py:39
  131.7 6.8 copy.377
  149.3 6.7 copy.340
  157.5 10.4 %maximum_convert_fusion = (bf16[2,64,8,9,32]{4,2,3,1,0:T(8,128)(2,1)}, f32[2,64,8,9,32]{4,2,3,1,0:T(8,128)}) fusion(pred[8,9]{0,1:T(8,128)(4,1)S(1)} %copy-done.10, bf16[32,32,3,3,3]{1,0,4,3,2:T(8,128)(2,1)S(1)} %copy-done, bf16[32,4,64,1,7,2]{0,4,5,2,1,3:T(8,128)(2,1)S(1)} %slice.93, bf16[32,4,64,1,8,9]{0,4,5,2,1,3:T(8,128)(2,1)} %copy.340), kind=kOutput, calls=%fused_computation.92 | convolution fusion | flops 509804544 | bytes 3233864 | tf_op jit(solution)/shard_map/conv_general_dilated | solution.py:47
  188.3 7.7 %copy.437 = bf16[32,4,64,1,8,8]{0,4,5,2,1,3:T(8,128)(2,1)} copy(bf16[32,4,64,1,8,8]{2,0,5,4,1,3:T(8,128)(2,1)} %get-tuple-element.69) | data formatting | bytes 2097152
  197.0 7.6 %copy.438 = bf16[32,4,64,1,8,8]{0,4,5,2,1,3:T(8,128)(2,1)} copy(bf16[32,4,64,1,8,8]{2,0,5,4,1,3:T(8,128)(2,1)} %get-tuple-element.70) | data formatting | bytes 2097152
  204.7 8.8 %fusion.79 = (bf16[32,4,64,8,9,1]{0,3,5,4,2,1:T(8,128)(2,1)}, bf16[32,4,64,8,9,1]{0,3,5,4,2,1:T(8,128)(2,1)}) fusion(bf16[32,4,64,1,7,1]{0,4,5,2,1,3:T(8,128)(2,1)S(1)} %copy.436, bf16[32,4,64,1,8,8]{0,4,5,2,1,3:T(8,128)(2,1)} %copy.437, bf16[32,4,64,1,7,1]{0,4,5,2,1,3:T(8,128)(2,1)} %copy.439, bf16[32,4,64,1,8,8]{0,4,5,2,1,3:T(8,128)(2,1)} %copy.438), kind=kLoop, calls=%fused_computation.81 | loop fusion | flops 7077888 | bytes 4685824 | tf_op jit(solution)/shard_map/concatenate | solution.py:21
  213.4 5.5 copy.383
  227.5 6.8 copy.346
  235.8 11.3 %select_reduce_fusion = (f32[32]{0:T(128)S(1)}, f32[2,64,8,9,32]{4,2,3,1,0:T(8,128)}) fusion(bf16[2,64,8,9,32]{4,2,3,1,0:T(8,128)(2,1)} %get-tuple-element.109, pred[8,9]{0,1:T(8,128)(4,1)S(1)} %copy-done.10, bf16[32,32,3,3,3]{1,0,4,3,2:T(8,128)(2,1)S(1)} %copy-done.11, bf16[32,4,64,1,7,2]{0,4,5,2,1,3:T(8,128)(2,1)S(1)} %slice.97, ...), kind=kOutput, calls=%fused_computation.91 | convolution fusion | flops 510394336 | bytes 3233992 | tf_op jit(solution)/shard_map/conv_general_dilated | solution.py:47
  247.1 19.5 %psum.42 = f32[1,32]{1,0:T(1,128)S(1)} all-reduce(f32[1,32]{1,0:T(1,128)S(1)} %multiply_bitcast_fusion), channel_id=1, replica_groups=mesh['pose'=4,'slab'=8] {'slab'}, use_global_device_ids=true, to_apply=%region_2.0 | all-reduce | flops 32 | bytes 256 | tf_op jit(solution)/shard_map/psum | solution.py:146
  305.1 7.7 %copy.441 = bf16[32,4,64,1,8,8]{0,4,5,2,1,3:T(8,128)(2,1)} copy(bf16[32,4,64,1,8,8]{2,0,5,4,1,3:T(8,128)(2,1)} %get-tuple-element.65) | data formatting | bytes 2097152
  313.8 7.7 %copy.442 = bf16[32,4,64,1,8,8]{0,4,5,2,1,3:T(8,128)(2,1)} copy(bf16[32,4,64,1,8,8]{2,0,5,4,1,3:T(8,128)(2,1)} %get-tuple-element.66) | data formatting | bytes 2097152
  326.9 36.8 %psum.47 = f32[32]{0:T(128)} all-reduce(f32[32]{0:T(128)S(1)} %broadcast_multiply_fusion.2), channel_id=1, replica_groups=mesh['pose'=4,'slab'=8] {'pose','slab'}, use_global_device_ids=true, to_apply=%region_8.9 | all-reduce | flops 32 | bytes 256 | tf_op jit(solution)/shard_map/psum | solution.py:179
  363.7 9.1 %fusion.81 = (bf16[32,4,64,8,9,1]{0,3,5,4,2,1:T(8,128)(2,1)}, bf16[32,4,64,8,9,1]{0,3,5,4,2,1:T(8,128)(2,1)}) fusion(bf16[32,4,64,1,7,1]{0,4,5,2,1,3:T(8,128)(2,1)S(1)} %copy.440, bf16[32,4,64,1,8,8]{0,4,5,2,1,3:T(8,128)(2,1)} %copy.441, bf16[32,4,64,1,7,1]{0,4,5,2,1,3:T(8,128)(2,1)} %copy.443, bf16[32,4,64,1,8,8]{0,4,5,2,1,3:T(8,128)(2,1)} %copy.442), kind=kLoop, calls=%fused_computation.83 | loop fusion | flops 7077888 | bytes 4685824 | tf_op jit(solution)/shard_map/concatenate | solution.py:21
  372.8 22.9 %fusion.117 = f32[32,32,3,3,3]{0,1,4,3,2:T(8,128)} fusion(bf16[2,64,8,9,32]{4,2,3,1,0:T(8,128)(2,1)S(1)} %copy-done.1, pred[8,9]{0,1:T(8,128)(4,1)S(1)} %copy-done.10, bf16[32,4,64,8,9,1]{0,3,5,4,2,1:T(8,128)(2,1)} %get-tuple-element.121, bf16[32,4,64,8,9,1]{0,3,5,4,2,1:T(8,128)(2,1)} %copy.389, bf16[32,4,64,8,9,1]{0,3,5,4,2,1:T(8,128)(2,1)} %get-tuple-element.120), kind=kOutput, calls=%fused_computation.128 | convolution fusion | flops 515238912 | bytes 4239432 | tf_op jit(solution)/shard_map/transpose | solution.py:71
  408.2 12.1 %select_convert_fusion.1 = bf16[2,64,8,9,32]{4,2,3,1,0:T(8,128)(2,1)} fusion(f32[2,64,8,9,32]{4,2,3,1,0:T(8,128)} %get-tuple-element.112, pred[8,9]{0,1:T(8,128)(4,1)S(1)} %copy-done.10, bf16[32,32,3,3,3]{1,0,4,3,2:T(8,128)(2,1)S(1)} %copy-done.12, bf16[32,4,64,1,7,2]{0,4,5,2,1,3:T(8,128)(2,1)S(1)} %slice.103, bf16[32,4,64,1,8,9]{0,4,5,2,1,3:T(8,128)(2,1)} %copy.355), kind=kOutput, calls=%fused_computation.89 | convolution fusion | flops 510099456 | bytes 3233864 | tf_op jit(solution)/shard_map/conv_general_dilated | solution.py:47
  432.0 23.5 %fusion.127 = f32[32,32,3,3,3]{0,1,4,3,2:T(8,128)} fusion(bf16[2,64,8,9,32]{4,2,3,1,0:T(8,128)(2,1)} %select_convert_fusion.1, pred[8,9]{0,1:T(8,128)(4,1)S(1)} %copy-done.10, bf16[32,4,64,8,9,1]{0,3,5,4,2,1:T(8,128)(2,1)} %get-tuple-element.119, bf16[32,4,64,8,9,1]{0,3,5,4,2,1:T(8,128)(2,1)} %copy.383, bf16[32,4,64,8,9,1]{0,3,5,4,2,1:T(8,128)(2,1)} %get-tuple-element.118), kind=kOutput, calls=%fused_computation.130 | convolution fusion | flops 515238912 | bytes 4239432 | tf_op jit(solution)/shard_map/transpose | solution.py:71
  459.2 5.5 copy.361
  466.2 12.4 %select_convert_fusion = (bf16[2,64,8,9,32]{4,2,3,1,0:T(8,128)(2,1)}, pred[2,64,8,9,32]{4,2,3,1,0:T(8,128)(4,1)S(1)}, f32[2,64,8,9,32]{4,2,3,1,0:T(8,128)}) fusion(bf16[2,64,8,9,32]{4,2,3,1,0:T(8,128)(2,1)} %select_convert_fusion.2, f32[2,64,8,9,32]{4,2,3,1,0:T(8,128)} %get-tuple-element.110, pred[8,9]{0,1:T(8,128)(4,1)S(1)} %copy-done.10, ...), kind=kOutput, calls=%fused_computation.88 | convolution fusion | flops 510689280 | bytes 5298248 | tf_op jit(solution)/shard_map/conv_general_dilated | solution.py:47
  498.5 5.6 collective-permute-start.10
  504.2 23.3 %fusion.137 = f32[32,28,3,3,3]{0,1,4,3,2:T(8,128)} fusion(bf16[2,64,8,9,32]{4,2,3,1,0:T(8,128)(2,1)} %get-tuple-element.63, pred[8,9]{0,1:T(8,128)(4,1)S(1)} %copy-done.10, bf16[28,4,64,8,9,1]{0,3,5,4,2,1:T(8,128)(2,1)} %get-tuple-element.116, bf16[28,4,64,8,9,1]{0,3,5,4,2,1:T(8,128)(2,1)} %copy.377, bf16[28,4,64,8,9,1]{0,3,5,4,2,1:T(8,128)(2,1)} %get-tuple-element.117), kind=kOutput, calls=%fused_computation.132 | convolution fusion | flops 450870912 | bytes 3783240 | tf_op jit(solution)/shard_map/transpose | solution.py:71
  527.6 134.7 %all-reduce.3.cloned.1.call-done = (f32[32,28,3,3,3]{0,1,4,3,2:T(8,128)}, f32[32,32,3,3,3]{0,1,4,3,2:T(8,128)}, f32[32,32,3,3,3]{0,1,4,3,2:T(8,128)}) async-done(((f32[32,28,3,3,3]{0,1,4,3,2:T(8,128)}, f32[32,32,3,3,3]{0,1,4,3,2:T(8,128)}, f32[32,32,3,3,3]{0,1,4,3,2:T(8,128)}), (f32[32,28,3,3,3]{0,1,4,3,2:T(8,128)}, f32[32,32,3,3,3]{0,1,4,3,2:T(8,128)}, ...) | async-done | bytes 317968 | tf_op jit(solution)/shard_map/psum | solution.py:179
  678.9 10.3 %fusion.54 = bf16[2,64,8,9,28]{4,2,3,1,0:T(8,128)(2,1)} fusion(bf16[32,28,3,3,3]{1,0,4,3,2:T(8,128)(2,1)S(1)} %copy-done.14, bf16[32,4,64,1,7,2]{0,4,5,2,1,3:T(8,128)(2,1)S(1)} %slice.112, bf16[32,4,64,1,8,9]{0,4,5,2,1,3:T(8,128)(2,1)} %copy.368), kind=kOutput, calls=%fused_computation.57 | convolution fusion | flops 445587456 | bytes 1973504 | tf_op jit(solution)/shard_map/conv_general_dilated | solution.py:47
  713.1 37.6 %psum.43 = f32[1,3,2048]{2,0,1:T(1,128)} all-reduce(f32[1,3,2048]{2,0,1:T(1,128)S(1)} %pad_maximum_fusion.1), channel_id=1, replica_groups=mesh['pose'=4,'slab'=8] {'slab'}, use_global_device_ids=true, to_apply=%region_4.5 | all-reduce | flops 6144 | bytes 49152 | tf_op jit(solution)/shard_map/psum | solution.py:178
  (183 shorter events, 233.2 us)
Async XLA Ops:
  7.2 150.3 %copy-start = (bf16[32,32,3,3,3]{1,0,4,3,2:T(8,128)(2,1)S(1)}, bf16[32,32,3,3,3]{1,0,4,3,2:T(8,128)(2,1)}, u32[]{:S(2)}) copy-start(bf16[32,32,3,3,3]{1,0,4,3,2:T(8,128)(2,1)} %param.17) | copy-start | bytes 165892
  7.2 655.1 %all-reduce.3.cloned.1.call-start = ((), (), s32[]{:S(2)}) async-start(), calls=%async_computation | async-start | bytes 2654208 | tf_op jit(solution)/shard_map/psum | solution.py:179
  11.9 7.0 copy-start.9
  20.9 21.1 %collective-permute-start.1 = (bf16[1,28,1,4096]{3,2,1,0:T(2,128)(2,1)S(1)}, bf16[1,28,1,4096]{3,2,1,0:T(2,128)(2,1)S(1)}, u32[]{:S(2)}, u32[]{:S(2)}) collective-permute-start(bf16[1,28,1,4096]{3,2,1,0:T(2,128)(2,1)S(1)} %get-tuple-element.94), channel_id=1, source_target_pairs={{1,0},{2,1},{3,2},{4,3},{5,4},{6,5},{7,6},{9,8},{10,9},{11,10},{12... | collective-permute-start | bytes 688136 | tf_op jit(solution)/shard_map/ppermute | solution.py:25
  22.2 24.1 %collective-permute-start = (bf16[1,28,1,4096]{3,2,1,0:T(2,128)(2,1)S(1)}, bf16[1,28,1,4096]{3,2,1,0:T(2,128)(2,1)}, u32[]{:S(2)}, u32[]{:S(2)}) collective-permute-start(bf16[1,28,1,4096]{3,2,1,0:T(2,128)(2,1)S(1)} %get-tuple-element.93), channel_id=1, source_target_pairs={{0,1},{1,2},{2,3},{3,4},{4,5},{5,6},{6,7},{8,9},{9,10},{10,11},{11... | collective-permute-start | bytes 688136 | tf_op jit(solution)/shard_map/ppermute | solution.py:23
  62.9 10.1 %copy-start.10 = (pred[8,9]{0,1:T(8,128)(4,1)S(1)}, pred[8,9]{0,1:T(8,128)(4,1)}, u32[]{:S(2)}) copy-start(pred[8,9]{0,1:T(8,128)(4,1)} %constant.99) | copy-start | bytes 220
  62.9 10.1 %copy-start.13 = (bf16[32,28,3,3,3]{1,0,4,3,2:T(8,128)(2,1)S(1)}, bf16[32,28,3,3,3]{1,0,4,3,2:T(8,128)(2,1)}, u32[]{:S(2)}) copy-start(bf16[32,28,3,3,3]{1,0,4,3,2:T(8,128)(2,1)} %param.16) | copy-start | bytes 145156
  96.5 42.0 %collective-permute-start.3 = (bf16[1,32,1,4096]{3,1,2,0:T(8,128)(2,1)}, bf16[1,32,1,4096]{3,1,2,0:T(8,128)(2,1)}, u32[]{:S(2)}, u32[]{:S(2)}) collective-permute-start(bf16[1,32,1,4096]{3,1,2,0:T(8,128)(2,1)} %get-tuple-element.92), channel_id=1, source_target_pairs={{1,0},{2,1},{3,2},{4,3},{5,4},{6,5},{7,6},{9,8},{10,9},{11,10},{12... | collective-permute-start | bytes 786440 | tf_op jit(solution)/shard_map/ppermute | solution.py:25
  97.8 42.9 %collective-permute-start.2 = (bf16[1,32,1,4096]{3,1,2,0:T(8,128)(2,1)}, bf16[1,32,1,4096]{3,1,2,0:T(8,128)(2,1)}, u32[]{:S(2)}, u32[]{:S(2)}) collective-permute-start(bf16[1,32,1,4096]{3,1,2,0:T(8,128)(2,1)} %get-tuple-element.91), channel_id=1, source_target_pairs={{0,1},{1,2},{2,3},{3,4},{4,5},{5,6},{6,7},{8,9},{9,10},{10,11},{11... | collective-permute-start | bytes 786440 | tf_op jit(solution)/shard_map/ppermute | solution.py:23
  180.3 38.7 %collective-permute-start.5 = (bf16[1,32,1,4096]{3,1,2,0:T(8,128)(2,1)}, bf16[1,32,1,4096]{3,1,2,0:T(8,128)(2,1)}, u32[]{:S(2)}, u32[]{:S(2)}) collective-permute-start(bf16[1,32,1,4096]{3,1,2,0:T(8,128)(2,1)} %get-tuple-element.90), channel_id=1, source_target_pairs={{1,0},{2,1},{3,2},{4,3},{5,4},{6,5},{7,6},{9,8},{10,9},{11,10},{12... | collective-permute-start | bytes 786440 | tf_op jit(solution)/shard_map/ppermute | solution.py:25
  181.6 39.7 %collective-permute-start.4 = (bf16[1,32,1,4096]{3,1,2,0:T(8,128)(2,1)}, bf16[1,32,1,4096]{3,1,2,0:T(8,128)(2,1)}, u32[]{:S(2)}, u32[]{:S(2)}) collective-permute-start(bf16[1,32,1,4096]{3,1,2,0:T(8,128)(2,1)} %get-tuple-element.89), channel_id=1, source_target_pairs={{0,1},{1,2},{2,3},{3,4},{4,5},{5,6},{6,7},{8,9},{9,10},{10,11},{11... | collective-permute-start | bytes 786440 | tf_op jit(solution)/shard_map/ppermute | solution.py:23
  227.5 8.3 %copy-start.11 = (bf16[32,32,3,3,3]{1,0,4,3,2:T(8,128)(2,1)S(1)}, bf16[32,32,3,3,3]{1,0,4,3,2:T(8,128)(2,1)}, u32[]{:S(2)}) copy-start(bf16[32,32,3,3,3]{1,0,4,3,2:T(8,128)(2,1)} %param.18) | copy-start | bytes 165892
  235.8 30.8 %copy-start.15 = (f32[32]{0:T(128)S(1)}, f32[32]{0:T(128)}, u32[]{:S(2)}) copy-start(f32[32]{0:T(128)} %param.19) | copy-start | bytes 388
  276.9 5.4 copy-start.2
  283.9 6.3 copy-start.3
  291.6 0.8 copy-start.4
  293.2 102.6 %collective-permute-start.7 = (bf16[1,32,1,4096]{3,1,2,0:T(8,128)(2,1)}, bf16[1,32,1,4096]{3,1,2,0:T(8,128)(2,1)}, u32[]{:S(2)}, u32[]{:S(2)}) collective-permute-start(bf16[1,32,1,4096]{3,1,2,0:T(8,128)(2,1)} %get-tuple-element.88), channel_id=1, source_target_pairs={{1,0},{2,1},{3,2},{4,3},{5,4},{6,5},{7,6},{9,8},{10,9},{11,10},{12... | collective-permute-start | bytes 786440 | tf_op jit(solution)/shard_map/ppermute | solution.py:25
  298.6 99.5 %collective-permute-start.6 = (bf16[1,32,1,4096]{3,1,2,0:T(8,128)(2,1)}, bf16[1,32,1,4096]{3,1,2,0:T(8,128)(2,1)}, u32[]{:S(2)}, u32[]{:S(2)}) collective-permute-start(bf16[1,32,1,4096]{3,1,2,0:T(8,128)(2,1)} %get-tuple-element.87), channel_id=1, source_target_pairs={{0,1},{1,2},{2,3},{3,4},{4,5},{5,6},{6,7},{8,9},{9,10},{10,11},{11... | collective-permute-start | bytes 786440 | tf_op jit(solution)/shard_map/ppermute | solution.py:23
  363.7 9.1 %copy-start.1 = (bf16[2,64,8,9,32]{4,2,3,1,0:T(8,128)(2,1)S(1)}, bf16[2,64,8,9,32]{4,2,3,1,0:T(8,128)(2,1)}, u32[]{:S(2)}) copy-start(bf16[2,64,8,9,32]{4,2,3,1,0:T(8,128)(2,1)} %select_convert_fusion.2) | copy-start | bytes 1769476
  372.8 23.0 %copy-start.7 = (bf16[2,64,8,9,32]{1,4,3,2,0:T(8,128)(2,1)S(1)}, bf16[2,64,8,9,32]{1,4,3,2,0:T(8,128)(2,1)}, u32[]{:S(2)}) copy-start(bf16[2,64,8,9,32]{1,4,3,2,0:T(8,128)(2,1)} %copy.351) | copy-start | bytes 1769476
  401.3 6.9 copy-start.12
  425.7 29.8 %collective-permute-start.9 = (bf16[1,32,1,4096]{3,1,2,0:T(8,128)(2,1)S(1)}, bf16[1,32,1,4096]{3,1,2,0:T(8,128)(2,1)S(1)}, u32[]{:S(2)}, u32[]{:S(2)}) collective-permute-start(bf16[1,32,1,4096]{3,1,2,0:T(8,128)(2,1)S(1)} %get-tuple-element.86), channel_id=1, source_target_pairs={{1,0},{2,1},{3,2},{4,3},{5,4},{6,5},{7,6},{9,8},{10,9},{11,10},{12... | collective-permute-start | bytes 786440 | tf_op jit(solution)/shard_map/ppermute | solution.py:25
  427.0 29.9 %collective-permute-start.8 = (bf16[1,32,1,4096]{3,1,2,0:T(8,128)(2,1)S(1)}, bf16[1,32,1,4096]{3,1,2,0:T(8,128)(2,1)S(1)}, u32[]{:S(2)}, u32[]{:S(2)}) collective-permute-start(bf16[1,32,1,4096]{3,1,2,0:T(8,128)(2,1)S(1)} %get-tuple-element.85), channel_id=1, source_target_pairs={{0,1},{1,2},{2,3},{3,4},{4,5},{5,6},{6,7},{8,9},{9,10},{10,11},{11... | collective-permute-start | bytes 786440 | tf_op jit(solution)/shard_map/ppermute | solution.py:23
  487.1 5.5 copy-start.5
  494.0 174.2 %collective-permute-start.11 = (bf16[1,32,1,4096]{3,1,2,0:T(8,128)(2,1)S(1)}, bf16[1,32,1,4096]{3,1,2,0:T(8,128)(2,1)S(1)}, u32[]{:S(2)}, u32[]{:S(2)}) collective-permute-start(bf16[1,32,1,4096]{3,1,2,0:T(8,128)(2,1)S(1)} %get-tuple-element.84), channel_id=1, source_target_pairs={{1,0},{2,1},{3,2},{4,3},{5,4},{6,5},{7,6},{9,8},{10,9},{11,10},{12... | collective-permute-start | bytes 786440 | tf_op jit(solution)/shard_map/ppermute | solution.py:25
  498.5 171.1 %collective-permute-start.10 = (bf16[1,32,1,4096]{3,1,2,0:T(8,128)(2,1)S(1)}, bf16[1,32,1,4096]{3,1,2,0:T(8,128)(2,1)S(1)}, u32[]{:S(2)}, u32[]{:S(2)}) collective-permute-start(bf16[1,32,1,4096]{3,1,2,0:T(8,128)(2,1)S(1)} %get-tuple-element.83), channel_id=1, source_target_pairs={{0,1},{1,2},{2,3},{3,4},{4,5},{5,6},{6,7},{8,9},{9,10},{10,11},{11... | collective-permute-start | bytes 786440 | tf_op jit(solution)/shard_map/ppermute | solution.py:23
  671.9 7.0 copy-start.14
  692.8 4.3 copy-start.6
  703.5 7.7 %copy-start.8 = (f32[2048,2]{1,0:T(8,128)S(1)}, f32[2048,2]{1,0:T(8,128)}, u32[]{:S(2)}) copy-start(f32[2048,2]{1,0:T(8,128)} %copy.406) | copy-start | bytes 49156
Sparse Core Ops, SparseCore 0:
  527.6 134.6 all-reduce.2
where the time goes:
time: 770 us; the launch traced here: 759 us
  local copies, waits for them, and re-layouts  254 us (33%)
  matrix products  152 us (20%)
  waiting for transfers between devices  139 us (18%)
  blocking collectives  93.9 us (12%)
  other arithmetic  60.3 us (8%)
  starting transfers between devices  41.2 us (5%)
  between operations  18.6 us (2%)
    psum x1, waiting for transfers between devices, local(): lax.psum((grad_stem_local, grad_one_local, grad_two_local, head_term), ('...  135 us
    transpose x3, matrix products, kernel_grad(): return result.transpose(1, 0, 2, 3, 4)  69.8 us
    conv_general_dilated x19, local copies, waits for them, and re-layouts, conv_valid(): lax.conv_general_dilated(spatial(padded), kernel, (1, 1, 1), [(0, 0), (1,...  69 us
    conv_general_dilated x6, matrix products, conv_valid(): lax.conv_general_dilated(spatial(padded), kernel, (1, 1, 1), [(0, 0), (1,...  68.2 us
    unnamed x49, local copies, waits for them, and re-layouts  64 us
    concatenate x31, local copies, waits for them, and re-layouts, extended(): jnp.concatenate([lax.ppermute(tail, axis, [(i, (i + 1) % count) for i in...  42.7 us
    psum x1, blocking collectives, local(): atom_grad = lax.psum(local_force, 'slab')  37.6 us
    psum x1, blocking collectives, local(): lax.psum((grad_stem_local, grad_one_local, grad_two_local, head_term), ('...  36.8 us
  transfers between devices with their start and end apart: 13, of which 2 were waited for; matrix products, arithmetic and copies ran while one was open for 27% of the time, Pallas kernels for 0%

commit v1 on v0

v1 whole, which is shorter than its diff:
```python
import functools

import jax
import jax.numpy as jnp
from jax import lax
from jax.experimental import pallas as pl
from jax.experimental.pallas import tpu as pltpu
from jax.sharding import PartitionSpec as P

NXY = 64
resolution = 0.375
f32 = jnp.float32
bf16 = jnp.bfloat16

JB = 16
OWN = 32
RD, RS, R2, R3, RM, RG = 38, 37, 36, 35, 34, 33
BR = 41 * JB
CH = 128
NCH = 5
NT = (((1,), (1,)), ((), ()))
NN = (((1,), (0,)), ((), ()))


def dotf(a, b, dims):
    return lax.dot_general(a, b, dims, preferred_element_type=f32)


def lane_block(shape):
    return lax.broadcasted_iota(jnp.int32, shape, 1) // 32


def spread(block, turn):
    if turn == 1:
        return block
    out = pltpu.roll(block, ((turn - 1) * 32) % 128, 1)
    lanes = lane_block(block.shape)
    if turn == 0:
        return jnp.where(lanes == 3, 0.0, out)
    if turn == 3:
        return jnp.where(lanes == 0, 0.0, out)
    return out


def one_block(block, source, target):
    out = pltpu.roll(block, ((target - source) * 32) % 128, 1)
    return jnp.where(lane_block(block.shape) == target, out, 0.0)


def build_forward(u_ref, conv, flip, w_ref):
    zero = jnp.zeros((32, 128), f32)

    def body(f, carry):
        fe = jnp.where(flip == 0, f, 2 - f)
        for p in range(2):
            for jo in range(4):
                rows = pl.ds(p * 128 + jo * 32, 32)
                for half in range(2):
                    edge = zero
                    for q in (2 * half, 2 * half + 1):
                        e = q - p
                        main = zero
                        if 0 <= e <= 2:
                            u = u_ref[conv * 9 + e * 3 + fe]
                            main = spread(u, jo)
                            if jo == 0:
                                edge = edge + one_block(u, 0, 2 * (q % 2))
                            if jo == 3:
                                edge = edge + one_block(u, 2, 2 * (q % 2) + 1)
                        w_ref[f, rows, pl.ds(q * 128, 128)] = main.astype(bf16)
                    w_ref[f, rows, pl.ds(512 + half * 128, 128)] = edge.astype(bf16)
        return carry

    lax.fori_loop(0, 3, body, 0)


def build_backward(u_ref, conv, flip, w_ref):
    zero = jnp.zeros((32, 128), f32)

    def body(f, carry):
        fe = jnp.where(flip == 0, 2 - f, f)
        for q in range(4):
            for p in range(2):
                e = 2 - (q - p)
                lanes = pl.ds(p * 128, 128)
                ok = 0 <= e <= 2
                u = u_ref[conv * 9 + e * 3 + fe] if ok else None
                for jc in range(4):
                    w_ref[f, pl.ds(q * 128 + jc * 32, 32), lanes] = (spread(u, jc) if ok else zero).astype(bf16)
                low = one_block(u, 2, 0) if ok else zero
                high = one_block(u, 0, 3) if ok else zero
                w_ref[f, pl.ds(512 + q * 64, 32), lanes] = low.astype(bf16)
                w_ref[f, pl.ds(512 + q * 64 + 32, 32), lanes] = high.astype(bf16)
        return carry

    lax.fori_loop(0, 3, body, 0)


def edges(a, b):
    n = a.shape[0]
    lanes = lane_block((n, 128))
    mixed = jnp.where(lanes < 2, pltpu.roll(a, 32, 1), pltpu.roll(b, 96, 1))
    down = pltpu.roll(mixed, 1, 0)
    up = pltpu.roll(mixed, n - 1, 0)
    jb = lax.broadcasted_iota(jnp.int32, (n, 128), 0) % JB
    low = jnp.where(jb == 0, 0.0, down)
    high = jnp.where(jb == JB - 1, 0.0, up)
    return jnp.where(lanes % 2 == 0, low, high)


def patch(x_ref, e_ref, plane, pair, f, n):
    sl = pl.ds(f * JB, n)
    return [x_ref[plane + k, sl, :] for k in range(4)] + [e_ref[pair + k, sl, :] for k in range(2)]


def conv_pair(x_ref, e_ref, plane, pair, rows, w_ref, acc_ref, dims):
    n = rows * JB
    total = None
    for f in range(3):
        lhs = jnp.concatenate(patch(x_ref, e_ref, plane, pair, f, n), axis=1)
        part = dotf(lhs, w_ref[f], dims)
        total = part if total is None else total + part
    acc_ref[pl.ds(0, n), :] = total


def put_pair(main_ref, e_ref, plane, pair, at, va, vb):
    main_ref[plane, pl.ds(at, va.shape[0]), :] = va.astype(bf16)
    main_ref[plane + 1, pl.ds(at, va.shape[0]), :] = vb.astype(bf16)
    if e_ref is not None:
        e_ref[pair, pl.ds(at, va.shape[0]), :] = edges(va, vb).astype(bf16)


def rounded(v):
    return v.astype(bf16).astype(f32)


def clear_pad(ref):
    for k in range(ref.shape[0]):
        ref[k, pl.ds(0, JB), :] = jnp.zeros((JB, 128), ref.dtype)


def pack_kernel(meta, raw_ref, self_ref, part_ref):
    h = meta[1]
    row = lax.broadcasted_iota(jnp.int32, (256, 256), 0)
    col = lax.broadcasted_iota(jnp.int32, (256, 256), 1)
    mask = jnp.where((row // 32) % 4 == col % 4, 1.0, 0.0).astype(bf16)
    srow = lax.broadcasted_iota(jnp.int32, (64, 256), 0)
    scol = lax.broadcasted_iota(jnp.int32, (64, 256), 1)
    same = srow % JB == (scol // 4) % JB
    for v in range(2):
        a = srow // JB if v == 0 else 3 - srow // JB
        pick = jnp.where(same & (scol // 64 == a), 1.0, 0.0).astype(bf16)
        for ch in range(10):
            at = (ch if v == 0 else 15 - ch) * 256
            x0 = raw_ref[0, :, pl.ds(at, 256)]
            x1 = raw_ref[1, :, pl.ds(at, 256)]
            wide = jnp.concatenate([x0] * 4 + [x1] * 4, axis=0) * mask
            out = dotf(pick, wide, NT).astype(bf16)
            n = 64 if ch < 9 else 32
            for p in range(2):
                val = out[:n, p * 128 : (p + 1) * 128]

                @pl.when(h == v)
                def _():
                    self_ref[p, pl.ds(ch * 64, n), :] = val

                @pl.when(h != v)
                def _():
                    part_ref[p, pl.ds(ch * 64, n), :] = val


def atom_terms(meta, radii, types, count_at):
    radius = jnp.zeros(types.shape, f32)
    for c in range(radii.shape[0]):
        radius = radius + jnp.where(types == c, radii[c], 0.0)
    return 1.0 / (radius * radius)


def centre_rows(n, first, step, half):
    row = lax.broadcasted_iota(jnp.int32, (n, 1), 0)
    return ((first + step * row).astype(f32) + 0.5 - half) * resolution


def bump(centre, place, inv_sq):
    offset = centre - place
    return jnp.exp(-2.0 * offset * offset * inv_sq), offset


def first_row(meta):
    return jnp.where(meta[1] == 0, 0, NXY - 1), jnp.where(meta[1] == 0, 1, -1)


def splat_kernel(meta, radii, coords_ref, types_ref, out_ref, z_ref, gy_ref, live_ref, y_ref):
    atoms = types_ref.shape[1]
    types = types_ref[...]
    inv_sq = atom_terms(meta, radii, types, 2)
    top, step = first_row(meta)
    gx = bump(centre_rows(40, top, step, 0.5 * NXY), coords_ref[0:1, :], inv_sq)[0]
    half_z = 0.5 * meta[3].astype(f32)
    gz = bump(centre_rows(16, 4 * meta[0] - 3, 1, half_z), coords_ref[2:3, :], inv_sq)[0]
    for q in range(10):
        z_ref[pl.ds(q * 40, 40), :] = (gz[q : q + 1, :] * gx).astype(bf16)
    gy_ref[...] = bump(centre_rows(NXY, 0, 1, 0.5 * NXY), coords_ref[1:2, :], inv_sq)[0]
    kind = lax.broadcasted_iota(jnp.int32, (32, atoms), 0)
    slot = lax.broadcasted_iota(jnp.int32, (32, atoms), 1)
    live_ref[...] = jnp.where((types == kind) & (slot < meta[2]), 1.0, 0.0)

    def body(step8, carry):
        for t in range(8):
            y = gy_ref[pl.ds(step8 * 8 + t, 1), :]
            y_ref[pl.ds(t * 32, 32), :] = (live_ref[...] * y).astype(bf16)
        out = dotf(z_ref[...], y_ref[...], NT)
        out_ref[pl.ds(2 * step8, 400, stride=JB), :] = out[:, :128]
        out_ref[pl.ds(2 * step8 + 1, 400, stride=JB), :] = out[:, 128:]
        return carry

    lax.fori_loop(0, 8, body, 0)


def forward_kernel(
    meta, splat_ref, lo_ref, own_ref, hi_ref, u_ref,
    x_ref, ex_ref, h1_ref, e1_ref, h2_ref, e2_ref, m3_ref, up_ref, dn_ref, pool_ref,
    w_ref, acc_ref,
):
    first = 4 * meta[0] - 3
    depth = meta[3]
    flip = meta[1]
    for ref in (x_ref, ex_ref, h1_ref, e1_ref, h2_ref, e2_ref):
        clear_pad(ref)

    def inside(q):
        z = first + q
        return jnp.where((z >= 0) & (z < depth), 1.0, 0.0)

    def receptor(q, sl):
        if q < 3:
            return lo_ref[q, sl, :]
        if q < 7:
            return own_ref[q - 3, sl, :]
        return hi_ref[q - 7, sl, :]

    for m in range(5):
        def density(c, carry):
            at = c * 304
            sl = pl.ds(pl.multiple_of(at, 16), 304)
            vals = []
            for q in (2 * m, 2 * m + 1):
                v = splat_ref[pl.ds(pl.multiple_of(q * 640 + at, 16), 304), :] + receptor(q, sl).astype(f32)
                vals.append(rounded(v * inside(q)))
            put_pair(x_ref, ex_ref, 2 * m, m, pl.multiple_of(JB + at, 16), *vals)
            return carry

        lax.fori_loop(0, 2, density, 0)

    build_forward(u_ref, 0, flip, w_ref)

    def stem(m, carry):
        conv_pair(x_ref, ex_ref, 2 * m, m, RS, w_ref, acc_ref, NT)
        ia, ib = inside(2 * m + 1), inside(2 * m + 2)
        for c in range(NCH):
            acc = jnp.maximum(acc_ref[pl.ds(c * CH, CH), :], 0.0)
            put_pair(h1_ref, e1_ref, 2 * m, m, JB + c * CH, rounded(acc[:, :128] * ia), rounded(acc[:, 128:] * ib))
        return carry

    lax.fori_loop(0, 4, stem, 0)
    build_forward(u_ref, 1, flip, w_ref)

    def second(m, carry):
        conv_pair(h1_ref, e1_ref, 2 * m, m, R2, w_ref, acc_ref, NT)
        ia, ib = inside(2 * m + 2), inside(2 * m + 3)
        for c in range(NCH):
            acc = jnp.maximum(acc_ref[pl.ds(c * CH, CH), :], 0.0)
            put_pair(h2_ref, e2_ref, 2 * m, m, JB + c * CH, rounded(acc[:, :128] * ia), rounded(acc[:, 128:] * ib))
        return carry

    lax.fori_loop(0, 3, second, 0)
    build_forward(u_ref, 2, flip, w_ref)

    def third(m, pool):
        conv_pair(h2_ref, e2_ref, 2 * m, m, R3, w_ref, acc_ref, NT)
        for c in range(7):
            sl = pl.ds(c * 80, 80)
            src = pl.ds(JB + c * 80, 80)
            for k in range(2):
                keep = h1_ref[2 * m + 2 + k, src, :].astype(f32)
                summed = keep + acc_ref[sl, pl.ds(128 * k, 128)]
                top = jnp.maximum(summed, 0.0)
                if (c + 1) * 80 > OWN * JB:
                    row = lax.broadcasted_iota(jnp.int32, (80, 128), 0) + c * 80
                    top = jnp.where(row < OWN * JB, top, 0.0)
                pool = pool + jnp.sum(top, axis=0, keepdims=True)
                m3_ref[2 * m + k, sl, :] = jnp.where(summed > 0.0, 1.0, 0.0).astype(bf16)
        return pool

    pool = lax.fori_loop(0, 2, third, jnp.zeros((1, 128), f32))
    pool = pool + pltpu.roll(pool, 64, 1)
    pool = pool + pltpu.roll(pool, 32, 1)
    pool_ref[...] = jnp.broadcast_to(pool, (8, 128))
    for k in range(3):
        up_ref[k] = m3_ref[k + 1]
        dn_ref[k] = m3_ref[k]
    up_ref[3] = h2_ref[3, pl.ds(JB, R3 * JB), :]
    dn_ref[3] = h2_ref[2, pl.ds(JB, R3 * JB), :]


def weight_grad(x_ref, e_ref, plane, pair, grads, g_ref, first):
    ut = jnp.transpose(grads).astype(bf16)
    for f in range(3):
        rhs = jnp.concatenate(patch(x_ref, e_ref, plane, pair, f, OWN * JB), axis=1)
        part = dotf(ut, rhs, NN)
        g_ref[f] = part if first else g_ref[f] + part


def extract(g_ref, conv, flip, scale, out_ref):
    lanes = lane_block((32, 128))

    def body(f, carry):
        fe = jnp.where(flip == 0, f, 2 - f)
        for e in range(3):
            total = jnp.zeros((32, 128), f32)
            for p in range(2):
                q = p + e
                for jo in range(4):
                    rows = pl.ds(p * 128 + jo * 32, 32)
                    block = g_ref[f, rows, pl.ds(q * 128, 128)]
                    if jo != 1:
                        block = pltpu.roll(block, ((1 - jo) * 32) % 128, 1)
                    if jo == 0:
                        block = jnp.where((lanes == 1) | (lanes == 2), block, 0.0)
                    elif jo == 3:
                        block = jnp.where(lanes < 2, block, 0.0)
                    else:
                        block = jnp.where(lanes < 3, block, 0.0)
                    total = total + block
                    if jo in (0, 3):
                        side = g_ref[f, rows, pl.ds(512 + (q // 2) * 128, 128)]
                        at = 2 * (q % 2)
                        total = total + (one_block(side, at, 0) if jo == 0 else one_block(side, at + 1, 2))
            out_ref[conv * 9 + e * 3 + fe] = total * scale
        return carry

    lax.fori_loop(0, 3, body, 0)


def backward_kernel(
    meta, radii, coords_ref, types_ref, parts_ref, mine_ref, head_ref,
    x_ref, ex_ref, h1_ref, e1_ref, h2_ref, e2_ref, m3_ref, lo_ref, hi_ref, u_ref,
    gw_ref, force_ref, info_ref,
    t_ref, et_ref, mg_ref, em_ref, sg_ref, es_ref, hm_ref, w_ref, acc_ref, g_ref, dg_ref, dk_ref,
    gy_ref, sy_ref, live_ref, y_ref, dy_ref,
):
    flip = meta[1]
    cells = meta[3].astype(f32) * (NXY * NXY)
    head = head_ref[...]
    pooled = jnp.sum(parts_ref[...], axis=0, keepdims=True) / cells
    lane = lax.broadcasted_iota(jnp.int32, (1, 128), 1)
    score = jnp.sum(jnp.where(lane < 32, pooled * head, 0.0), axis=1, keepdims=True)
    sign = (2 * meta[4] - 1).astype(f32)
    score_grad = -sign / (1.0 + jnp.exp(sign * score))
    info_ref[0:1, :] = jnp.broadcast_to(score, (1, 128))
    info_ref[1:2, :] = score_grad * mine_ref[0:1, :] / cells
    info_ref[2:8, :] = jnp.zeros((6, 128), f32)
    tone = rounded(score_grad * head)

    for ref in (t_ref, et_ref, mg_ref, em_ref, sg_ref, es_ref):
        clear_pad(ref)
    mask_of = lambda q: (lo_ref.at[q] if q < 3 else m3_ref.at[q - 3] if q < 7 else hi_ref.at[q - 7])
    for m in range(5):
        for c in range(5):
            sl = pl.ds(c * 112, 112)
            vals = [jnp.where(mask_of(q)[sl, :].astype(f32) > 0.0, tone, 0.0) for q in (2 * m, 2 * m + 1)]
            put_pair(t_ref, et_ref, 2 * m, m, JB + c * 112, *vals)
    hm_ref[0] = lo_ref[3]
    hm_ref[7] = hi_ref[3]
    for k in range(6):
        hm_ref[k + 1] = h2_ref[k, pl.ds(JB, R3 * JB), :]

    scale = 1.0 / cells
    own_rows = pl.ds(JB, OWN * JB)
    for m in range(2):
        grads = jnp.concatenate([t_ref[3 + 2 * m, own_rows, :], t_ref[4 + 2 * m, own_rows, :]], axis=1)
        weight_grad(h2_ref, e2_ref, 2 * m, m, grads, g_ref, m == 0)
    extract(g_ref, 2, flip, scale, gw_ref)

    build_backward(u_ref, 2, flip, w_ref)

    def mid(m, carry):
        conv_pair(t_ref, et_ref, 2 * m, m, RM, w_ref, acc_ref, NN)
        for c in range(NCH):
            sl = pl.ds(c * 112, 112)
            vals = [
                rounded(jnp.where(hm_ref[2 * m + k, sl, :].astype(f32) > 0.0, acc_ref[sl, pl.ds(128 * k, 128)], 0.0))
                for k in range(2)
            ]
            put_pair(mg_ref, em_ref, 2 * m, m, JB + c * 112, *vals)
        return carry

    lax.fori_loop(0, 4, mid, 0)

    for m in range(3):
        ga = mg_ref[1 + 2 * m, own_rows, :]
        gb = mg_ref[2 + 2 * m, own_rows, :]
        if m == 0:
            ga = jnp.zeros_like(ga)
        if m == 2:
            gb = jnp.zeros_like(gb)
        weight_grad(h1_ref, e1_ref, 2 * m, m, jnp.concatenate([ga, gb], axis=1), g_ref, m == 0)
    extract(g_ref, 1, flip, scale, gw_ref)

    build_backward(u_ref, 1, flip, w_ref)

    def low(m, carry):
        conv_pair(mg_ref, em_ref, 2 * m, m, RG, w_ref, acc_ref, NN)
        for c in range(NCH):
            sl = pl.ds(c * 112, 112)
            src = pl.ds(JB + c * 112, 112)
            vals = []
            for k in range(2):
                back = t_ref[2 * m + 2 + k, src, :].astype(f32) + acc_ref[sl, pl.ds(128 * k, 128)]
                vals.append(rounded(jnp.where(h1_ref[2 * m + 1 + k, src, :].astype(f32) > 0.0, back, 0.0)))
            put_pair(sg_ref, es_ref, 2 * m, m, JB + c * 112, *vals)
        return carry

    lax.fori_loop(0, 3, low, 0)

    for m in range(2):
        grads = jnp.concatenate([sg_ref[1 + 2 * m, own_rows, :], sg_ref[2 + 2 * m, own_rows, :]], axis=1)
        weight_grad(x_ref, ex_ref, 2 + 2 * m, 1 + m, grads, g_ref, m == 0)
    extract(g_ref, 0, flip, scale, gw_ref)

    build_backward(u_ref, 0, flip, w_ref)

    def last(m, carry):
        conv_pair(sg_ref, es_ref, 2 * m, m, OWN, w_ref, acc_ref, NN)
        for k in range(2):
            at = pl.ds(pl.multiple_of((2 * m + k) * OWN * JB, 16), OWN * JB)
            dg_ref[at, :] = rounded(acc_ref[pl.ds(0, OWN * JB), pl.ds(128 * k, 128)])
        return carry

    lax.fori_loop(0, 2, last, 0)
    for jb in range(JB):
        dk_ref[:, pl.ds(jb * 128, 128)] = dg_ref[pl.ds(jb, 4 * OWN, stride=JB), :].astype(bf16)

    types = types_ref[...]
    inv_sq = atom_terms(meta, radii, types, 2)
    atoms = types.shape[1]
    gy, off = bump(centre_rows(NXY, 0, 1, 0.5 * NXY), coords_ref[1:2, :], inv_sq)
    gy_ref[...] = gy
    sy_ref[...] = 4.0 * off * inv_sq * gy
    kind = lax.broadcasted_iota(jnp.int32, (32, atoms), 0)
    slot = lax.broadcasted_iota(jnp.int32, (32, atoms), 1)
    live_ref[...] = jnp.where((types == kind) & (slot < meta[2]), 1.0, 0.0)
    top, step = first_row(meta)
    half_z = 0.5 * meta[3].astype(f32)
    wide = 256
    for b in range(atoms // wide):
        sl = pl.ds(b * wide, wide)

        def table(j, carry):
            live = live_ref[:, sl]
            at = pl.ds(pl.multiple_of(j * 32, 32), 32)
            y_ref[at, :] = (live * gy_ref[pl.ds(j, 1), sl]).astype(bf16)
            dy_ref[at, :] = (live * sy_ref[pl.ds(j, 1), sl]).astype(bf16)
            return carry

        lax.fori_loop(0, NXY, table, 0, unroll=4)
        plain = dotf(dk_ref[...], y_ref[...], NN)
        slope = dotf(dk_ref[...], dy_ref[...], NN)
        inv = inv_sq[:, b * wide : (b + 1) * wide]
        gx, off_x = bump(centre_rows(OWN, top, step, 0.5 * NXY), coords_ref[0:1, sl], inv)
        dgx = 4.0 * off_x * inv * gx
        gz, off_z = bump(centre_rows(8, 4 * meta[0], 1, half_z), coords_ref[2:3, sl], inv)
        dgz = 4.0 * off_z * inv * gz
        fx = jnp.zeros((1, wide), f32)
        fy = jnp.zeros((1, wide), f32)
        fz = jnp.zeros((1, wide), f32)
        for k in range(4):
            pk = plain[k * OWN : (k + 1) * OWN, :]
            sk = slope[k * OWN : (k + 1) * OWN, :]
            fx = fx + gz[k : k + 1, :] * jnp.sum(pk * dgx, axis=0, keepdims=True)
            fy = fy + gz[k : k + 1, :] * jnp.sum(sk * gx, axis=0, keepdims=True)
            fz = fz + dgz[k : k + 1, :] * jnp.sum(pk * gx, axis=0, keepdims=True)
        force_ref[0:1, sl] = fx
        force_ref[1:2, sl] = fy
        force_ref[2:3, sl] = fz


def smem():
    return pl.BlockSpec(memory_space=pltpu.SMEM)


def vmem():
    return pl.BlockSpec(memory_space=pltpu.VMEM)


def lane_rows(w):
    o, c = w.shape[:2]
    moved = jnp.transpose(w, (2, 3, 0, 4, 1)).astype(f32)
    moved = jnp.pad(moved, ((0, 0), (0, 0), (0, 0), (0, 1), (0, 32 - c)))
    return moved.reshape(9, o, 128)


def local(coords, atom_types, counts, labels, receptor, radii, w_stem, w_one, w_two, w_head):
    slab_count = lax.axis_size("slab")
    pose_count = lax.axis_size("pose")
    atoms = coords.shape[2]
    s = lax.axis_index("slab")
    group, half = s // 2, s % 2
    depth = receptor.shape[2] * slab_count
    meta = jnp.stack([group, half, counts[0], jnp.int32(depth), labels[0]]).astype(jnp.int32)
    bh = (RD * JB, 128)

    raw = jnp.pad(jnp.transpose(receptor[0], (1, 0, 2)), ((0, 0), (0, 4), (0, 0)))
    mine, theirs = pl.pallas_call(
        pack_kernel,
        out_shape=[jax.ShapeDtypeStruct((2,) + bh, bf16)] * 2,
        in_specs=[smem(), vmem()],
        out_specs=[vmem(), vmem()],
        name="pack",
    )(meta, raw)
    other = lax.ppermute(theirs, "slab", [(i, i ^ 1) for i in range(slab_count)])
    lower = jnp.where(half == 0, mine, other)
    upper = jnp.where(half == 0, other, mine)
    own = jnp.concatenate([lower, upper], axis=0)
    ups = [(i, i + 2) for i in range(slab_count - 2)]
    downs = [(i + 2, i) for i in range(slab_count - 2)]
    lo = lax.ppermute(own[1:4], "slab", ups)
    hi = lax.ppermute(own[0:3], "slab", downs)

    types = atom_types
    splat = pl.pallas_call(
        splat_kernel,
        out_shape=jax.ShapeDtypeStruct((6400, 128), f32),
        in_specs=[smem(), smem(), vmem(), vmem()],
        out_specs=vmem(),
        scratch_shapes=[
            pltpu.VMEM((400, atoms), bf16),
            pltpu.VMEM((NXY, atoms), f32),
            pltpu.VMEM((32, atoms), f32),
            pltpu.VMEM((256, atoms), bf16),
        ],
        cost_estimate=pl.CostEstimate(flops=2 * 400 * 2048 * atoms, bytes_accessed=4_000_000, transcendentals=0),
        name="splat",
    )(meta, radii, coords[0], types)

    u = jnp.concatenate([lane_rows(w_stem), lane_rows(w_one), lane_rows(w_two)], axis=0)

    big = lambda n: jax.ShapeDtypeStruct((n, BR, 128), bf16)
    thin = lambda n: jax.ShapeDtypeStruct((n, R3 * JB, 128), bf16)
    x, ex, h1, e1, h2, e2, m3, up, dn, pool = pl.pallas_call(
        forward_kernel,
        out_shape=[big(10), big(5), big(8), big(4), big(6), big(3), thin(4), thin(4), thin(4),
                   jax.ShapeDtypeStruct((8, 128), f32)],
        in_specs=[smem()] + [vmem()] * 5,
        out_specs=[vmem()] * 10,
        scratch_shapes=[pltpu.VMEM((3, 256, 768), bf16), pltpu.VMEM((BR, 256), f32)],
        name="forward",
    )(meta, splat, lo, own, hi, u)

    from_lo = lax.ppermute(up, "slab", ups)
    from_hi = lax.ppermute(dn, "slab", downs)
    parts = lax.all_to_all(jnp.broadcast_to(pool[:1][None], (slab_count, 1, 128)), "slab", 0, 0)
    parts = parts.reshape(slab_count, 128)
    head = jnp.tile(w_head, 4)[None, :]

    gw, force, info = pl.pallas_call(
        backward_kernel,
        out_shape=[
            jax.ShapeDtypeStruct((27, 32, 128), f32),
            jax.ShapeDtypeStruct((3, atoms), f32),
            jax.ShapeDtypeStruct((8, 128), f32),
        ],
        in_specs=[smem(), smem()] + [vmem()] * 15,
        out_specs=[vmem()] * 3,
        scratch_shapes=[
            pltpu.VMEM((10, BR, 128), bf16), pltpu.VMEM((5, BR, 128), bf16),
            pltpu.VMEM((8, BR, 128), bf16), pltpu.VMEM((4, BR, 128), bf16),
            pltpu.VMEM((6, BR, 128), bf16), pltpu.VMEM((3, BR, 128), bf16),
            pltpu.VMEM((8, R3 * JB, 128), bf16),
            pltpu.VMEM((3, 768, 256), bf16), pltpu.VMEM((BR, 256), f32), pltpu.VMEM((3, 256, 768), f32),
            pltpu.VMEM((4 * OWN * JB, 128), f32), pltpu.VMEM((4 * OWN, 2048), bf16),
            pltpu.VMEM((NXY, atoms), f32), pltpu.VMEM((NXY, atoms), f32), pltpu.VMEM((32, atoms), f32),
            pltpu.VMEM((2048, 256), bf16), pltpu.VMEM((2048, 256), bf16),
        ],
        name="backward",
    )(meta, radii, coords[0], types, parts, pool, head, x, ex, h1, e1, h2, e2, m3, from_lo, from_hi, u)

    count = pose_count * slab_count
    flat = jnp.concatenate([gw.reshape(27 * 32, 128), info[1:2]], axis=0)
    each = -(-flat.shape[0] // count)
    flat = jnp.pad(flat, ((0, each * count - flat.shape[0]), (0, 0))).reshape(pose_count, slab_count, each, 128)
    share = -(-3 * atoms // (slab_count * 128))
    atom_part = jnp.pad(force.reshape(3 * atoms), (0, share * slab_count * 128 - 3 * atoms))
    atom_part = atom_part.reshape(1, slab_count, share, 128)
    same = (lax.axis_index("pose") == jnp.arange(pose_count))[:, None, None, None]
    atom_part = jnp.where(same, atom_part, 0.0)
    message = jnp.concatenate([flat, atom_part], axis=2).reshape(count, each + share, 128)
    got = lax.all_to_all(message, ("pose", "slab"), 0, 0)
    total = jnp.sum(got, axis=0)
    full = lax.all_to_all(jnp.broadcast_to(total[None], (count, each + share, 128)), ("pose", "slab"), 0, 0)
    rows = full[:, :each].reshape(count * each, 128)
    grads = rows[: 27 * 32].reshape(3, 3, 3, 32, 128)[..., :96].reshape(3, 3, 3, 32, 3, 32)
    grads = grads.transpose(0, 3, 5, 1, 2, 4)
    grad_head = rows[27 * 32, :32]
    atom = lax.dynamic_slice_in_dim(
        full.reshape(pose_count, slab_count, each + share, 128), lax.axis_index("pose"), 1, 0
    )[:, :, each:]
    atom_grad = atom.reshape(-1)[: 3 * atoms].reshape(1, 3, atoms)
    scores = info[0, :1]
    label_sign = (2 * labels - 1).astype(f32)
    pose_loss = jax.nn.softplus(-label_sign * scores)
    return scores, pose_loss, atom_grad, grads[0][:, :28], grads[1], grads[2], grad_head


def solution(mesh):
    return jax.shard_map(
        local,
        mesh=mesh,
        in_specs=(
            P("pose", None, None),
            P("pose", None),
            P("pose"),
            P("pose"),
            P("pose", None, "slab", None),
            P(),
            P(),
            P(),
            P(),
            P(),
        ),
        out_specs=(P("pose"), P("pose"), P("pose", None, None), P(), P(), P(), P()),
        check_vma=False,
    )
```

time: 770 us -> 158 us (0.21); the launches traced: 759 us -> 157 us
  local copies, waits for them, and re-layouts: 254 us -> 16.2 us
  matrix products: 152 us -> 0 us
  waiting for transfers between devices: 139 us -> 32 us
  blocking collectives: 93.9 us -> 20.8 us
  Pallas kernels: 0 us -> 57.8 us
  other arithmetic: 60.3 us -> 3.07 us
  starting transfers between devices: 41.2 us -> 23.1 us
  between operations: 18.6 us -> 4.19 us
    psum x1 -> x0, waiting for transfers between devices: 135 us -> none  [local(): lax.psum((grad_stem_local, grad_one_local, grad_two_local, head_term), ('...]
    psum x3 -> x0, blocking collectives: 93.9 us -> none  [the longest x1 37.6 us: local(): atom_grad = lax.psum(local_force, 'slab')]
    transpose x3 -> x0, matrix products: 69.8 us -> none  [kernel_grad(): return result.transpose(1, 0, 2, 3, 4)]
    conv_general_dilated x19 -> x0, local copies, waits for them, and re-layouts: 69 us -> none  [conv_valid(): lax.conv_general_dilated(spatial(padded), kernel, (1, 1, 1), [(0, 0), (1,...]
    conv_general_dilated x6 -> x0, matrix products: 68.2 us -> none  [conv_valid(): lax.conv_general_dilated(spatial(padded), kernel, (1, 1, 1), [(0, 0), (1,...]
    pallas_call x0 -> x4, Pallas kernels: none -> 57.8 us  [the longest x1 27 us: local(): pl.pallas_call(backward_kernel, out_shape=[jax.ShapeDtypeStruct((27, 32,...]
    unnamed x49 -> x32, local copies, waits for them, and re-layouts: 64 us -> 6.64 us
    concatenate x31 -> x1, local copies, waits for them, and re-layouts: 42.7 us -> 0.04 us  [local(): jnp.concatenate([flat, atom_part], axis=2).reshape(count, each + share, 128)]
  transfers between devices with their start and end apart: 13 -> 7, of which waited for: 2 -> 4; matrix products, arithmetic and copies ran while one was open for 27% -> 4% of each run, Pallas kernels for 0% -> 5%
where the time goes in v1:
time: 158 us; the launch traced here: 157 us
  Pallas kernels  57.8 us (37%)
  waiting for transfers between devices  32 us (20%)
  starting transfers between devices  23.1 us (15%)
  blocking collectives  20.8 us (13%)
  local copies, waits for them, and re-layouts  16.2 us (10%)
  between operations  4.19 us (3%)
  other arithmetic  3.07 us (2%)
    pallas_call x1, Pallas kernels, local(): pl.pallas_call(backward_kernel, out_shape=[jax.ShapeDtypeStruct((27, 32,...  27 us
    all_to_all x1, blocking collectives, local(): got = lax.all_to_all(message, ('pose', 'slab'), 0, 0)  20.8 us
    all_to_all x1, waiting for transfers between devices, local(): lax.all_to_all(jnp.broadcast_to(total[None], (count, each + share, 128)),...  17.1 us
    pallas_call x1, Pallas kernels, local(): pl.pallas_call(forward_kernel, out_shape=[big(10), big(5), big(8), big(4)...  16.3 us
    pallas_call x1, Pallas kernels, local(): pl.pallas_call(splat_kernel, out_shape=jax.ShapeDtypeStruct((6400, 128),...  8.54 us
    all_to_all x1, waiting for transfers between devices, local(): lax.all_to_all(jnp.broadcast_to(pool[:1][None], (slab_count, 1, 128)), 's...  7.85 us
    all_to_all x1, starting transfers between devices, local(): lax.all_to_all(jnp.broadcast_to(pool[:1][None], (slab_count, 1, 128)), 's...  6.87 us
    unnamed x32, local copies, waits for them, and re-layouts  6.64 us
  transfers between devices with their start and end apart: 7, of which 4 were waited for; matrix products, arithmetic and copies ran while one was open for 4% of the time, Pallas kernels for 5%

profile of v1, /device:TPU:0, one launch (start us, length us, event | category | flops | bytes accessed | tf_op | source)
XLA Modules:
  0.0 157.1 jit_solution(14407461491879231309)
XLA Ops:
  2.0 1.3 copy.43
  3.3 0.9 pad.22.raw_ref
  4.8 5.9 %pack.1 = (bf16[2,608,128]{2,1,0:T(8,128)(2,1)}, bf16[2,608,128]{2,1,0:T(8,128)(2,1)}) custom-call(s32[5]{0:T(128)} %stack.11.meta, bf16[2,32,4096]{2,1,0:T(8,128)(2,1)} %pad.22.raw_ref), custom_call_target="tpu_custom_call" | custom-call | tf_op jit(solution)/shard_map/pack/pallas_call | solution.py:514
  10.7 3.0 %collective-permute-start = (bf16[2,608,128]{2,1,0:T(8,128)(2,1)}, bf16[2,608,128]{2,1,0:T(8,128)(2,1)S(1)}, u32[]{:S(2)}, u32[]{:S(2)}) collective-permute-start(bf16[2,608,128]{2,1,0:T(8,128)(2,1)} %get-tuple-element.23), channel_id=1, source_target_pairs={{0,1},{1,0},{2,3},{3,2},{4,5},{5,4},{6,7},{7,6},{8,9},{9,8},{10,11... | collective-permute-start | bytes 933896 | tf_op jit(solution)/shard_map/ppermute | solution.py:521
  15.2 6.0 %collective-permute-done = bf16[2,608,128]{2,1,0:T(8,128)(2,1)S(1)} collective-permute-done((bf16[2,608,128]{2,1,0:T(8,128)(2,1)}, bf16[2,608,128]{2,1,0:T(8,128)(2,1)S(1)}, u32[]{:S(2)}, u32[]{:S(2)}) %collective-permute-start) | collective-permute-done | bytes 311328 | tf_op jit(solution)/shard_map/ppermute | solution.py:521
  21.3 3.8 %collective-permute-start.1 = (bf16[3,608,128]{2,1,0:T(8,128)(2,1)S(1)}, bf16[3,608,128]{2,1,0:T(8,128)(2,1)S(1)}, u32[]{:S(2)}, u32[]{:S(2)}) collective-permute-start(bf16[3,608,128]{2,1,0:T(8,128)(2,1)S(1)} %get-tuple-element.55), channel_id=1, source_target_pairs={{0,2},{1,3},{2,4},{3,5},{4,6},{5,7},{8,10},{9,11},{10,12},{11,13},... | collective-permute-start | bytes 1400840 | tf_op jit(solution)/shard_map/ppermute | solution.py:527
  25.1 1.3 collective-permute-start.2
  26.4 0.8 maximum_convert_fusion.u_ref
  27.2 0.6 copy.44
  27.8 8.5 %splat.1.splat_ref = f32[6400,128]{1,0:T(8,128)} custom-call(s32[5]{0:T(128)} %stack.11.meta, f32[28]{0:T(128)} %radii.3, f32[3,2048]{1,0:T(4,128)} %bitcast.44, s32[1,2048]{1,0:T(1,128)} %types_ref.3), custom_call_target="tpu_custom_call" | custom-call | flops 3355443200 | bytes 4000000 | tf_op jit(solution)/shard_map/splat/pallas_call | solution.py:531
  36.4 0.9 pad_maximum_fusion.own_ref
  37.3 1.0 collective-permute-done.2.hi_ref
  38.3 0.8 copy-done.3
  39.1 16.3 %forward.1 = (bf16[10,656,128]{2,1,0:T(8,128)(2,1)}, bf16[5,656,128]{2,1,0:T(8,128)(2,1)}, bf16[8,656,128]{2,1,0:T(8,128)(2,1)}, bf16[4,656,128]{2,1,0:T(8,128)(...) custom-call(s32[5]{0:T(128)} %stack.11.meta, ...), custom_call_target="tpu_custom_call" | custom-call | tf_op jit(solution)/shard_map/forward/pallas_call | solution.py:550
  55.4 4.3 %collective-permute-start.3 = (bf16[4,560,128]{2,1,0:T(8,128)(2,1)}, bf16[4,560,128]{2,1,0:T(8,128)(2,1)S(1)}, u32[]{:S(2)}, u32[]{:S(2)}) collective-permute-start(bf16[4,560,128]{2,1,0:T(8,128)(2,1)} %get-tuple-element.32), channel_id=1, source_target_pairs={{0,2},{1,3},{2,4},{3,5},{4,6},{5,7},{8,10},{9,11},{10,12},{11,13},... | collective-permute-start | bytes 1720328 | tf_op jit(solution)/shard_map/ppermute | solution.py:560
  59.7 1.3 collective-permute-start.4
  61.0 0.7 slice_bitcast_fusion.4
  62.3 6.9 %all-to-all-start = ((f32[8,1,128]{2,1,0:T(1,128)}), f32[8,1,128]{2,1,0:T(1,128)S(1)}, u32[]{:S(2)}, u32[]{:S(2)}) async-start(f32[8,1,128]{2,1,0:T(1,128)} %broadcast_in_dim.44), calls=%async_computation | async-start | bytes 8192 | tf_op jit(solution)/shard_map/all_to_all | solution.py:562
  70.0 7.9 %all-to-all-done = f32[8,1,128]{2,1,0:T(1,128)S(1)} async-done(((f32[8,1,128]{2,1,0:T(1,128)}), f32[8,1,128]{2,1,0:T(1,128)S(1)}, u32[]{:S(2)}, u32[]{:S(2)}) %all-to-all-start) | async-done | bytes 4128 | tf_op jit(solution)/shard_map/all_to_all | solution.py:562
  78.9 27.0 %backward.1 = (f32[27,32,128]{2,1,0:T(8,128)}, f32[3,2048]{1,0:T(4,128)}, f32[8,128]{1,0:T(8,128)}) custom-call(s32[5]{0:T(128)} %stack.11.meta, f32[28]{0:T(128)} %radii.3, f32[3,2048]{1,0:T(4,128)} %bitcast.45, s32[1,2048]{1,0:T(1,128)} %types_ref.3, f32[8,128]{1,0:T(8,128)} %bitcast.46, f32[8,128]{1,0:T(8,128)} %get-tuple-element.24.mine_ref, ...), custom_call_target="tpu_custom_call" | custom-call | tf_op jit(solution)/shard_map/backward/pallas_call | solution.py:566
  105.9 0.7 slice.46
  106.6 1.0 select_maximum_fusion
  107.9 20.8 %all_to_all.15 = f32[32,34,128]{2,1,0:T(8,128)S(1)} all-to-all(f32[32,34,128]{2,1,0:T(8,128)S(1)} %pad_maximum_fusion.1), channel_id=1, replica_groups=mesh['pose'=4,'slab'=8] {'pose','slab'}, dimensions={0} | all-to-all | bytes 1114112 | tf_op jit(solution)/shard_map/all_to_all | solution.py:598
  128.7 0.9 broadcast_in_dim.52
  129.7 2.6 %all-to-all-start.2 = ((f32[32,34,128]{2,1,0:T(8,128)}), f32[32,34,128]{2,1,0:T(8,128)S(1)}, u32[]{:S(2)}, u32[]{:S(2)}) async-start(f32[32,34,128]{2,1,0:T(8,128)} %broadcast_in_dim.52), calls=%async_computation.2 | async-start | bytes 1310720 | tf_op jit(solution)/shard_map/all_to_all | solution.py:600
  132.3 1.2 slice.45
  134.2 17.1 %all-to-all-done.2 = f32[32,34,128]{2,1,0:T(8,128)S(1)} async-done(((f32[32,34,128]{2,1,0:T(8,128)}), f32[32,34,128]{2,1,0:T(8,128)S(1)}, u32[]{:S(2)}, u32[]{:S(2)}) %all-to-all-start.2) | async-done | bytes 557088 | tf_op jit(solution)/shard_map/all_to_all | solution.py:600
  152.0 0.6 reshape.72
  152.9 0.8 copy.34
  153.7 0.8 copy.35
  154.6 0.8 copy.36
  155.4 0.6 reshape_reshape.4
  (55 shorter events, 5.8 us)
Async XLA Ops:
  0.6 13.0 %copy-start.5 = (bf16[32,28,3,3,3]{1,0,4,3,2:T(8,128)(2,1)S(1)}, bf16[32,28,3,3,3]{1,0,4,3,2:T(8,128)(2,1)}, u32[]{:S(2)}) copy-start(bf16[32,28,3,3,3]{1,0,4,3,2:T(8,128)(2,1)} %param.16) | copy-start | bytes 145156
  3.3 10.9 %copy-start.6 = (bf16[32,32,3,3,3]{1,0,4,3,2:T(8,128)(2,1)S(1)}, bf16[32,32,3,3,3]{1,0,4,3,2:T(8,128)(2,1)}, u32[]{:S(2)}) copy-start(bf16[32,32,3,3,3]{1,0,4,3,2:T(8,128)(2,1)} %param.17) | copy-start | bytes 165892
  4.2 10.5 %copy-start.7 = (bf16[32,32,3,3,3]{1,0,4,3,2:T(8,128)(2,1)S(1)}, bf16[32,32,3,3,3]{1,0,4,3,2:T(8,128)(2,1)}, u32[]{:S(2)}) copy-start(bf16[32,32,3,3,3]{1,0,4,3,2:T(8,128)(2,1)} %param.18) | copy-start | bytes 165892
  10.7 10.5 %collective-permute-start = (bf16[2,608,128]{2,1,0:T(8,128)(2,1)}, bf16[2,608,128]{2,1,0:T(8,128)(2,1)S(1)}, u32[]{:S(2)}, u32[]{:S(2)}) collective-permute-start(bf16[2,608,128]{2,1,0:T(8,128)(2,1)} %get-tuple-element.23), channel_id=1, source_target_pairs={{0,1},{1,0},{2,3},{3,2},{4,5},{5,4},{6,7},{7,6},{8,9},{9,8},{10,11... | collective-permute-start | bytes 933896 | tf_op jit(solution)/shard_map/ppermute | solution.py:521
  14.0 7.2 %copy-start.4 = (bf16[2,608,128]{2,1,0:T(8,128)(2,1)S(1)}, bf16[2,608,128]{2,1,0:T(8,128)(2,1)}, u32[]{:S(2)}) copy-start(bf16[2,608,128]{2,1,0:T(8,128)(2,1)} %get-tuple-element.22) | copy-start | bytes 933892
  15.2 12.0 %copy-start.9 = (f32[1,3,2048]{2,0,1:T(1,128)S(1)}, f32[1,3,2048]{2,0,1:T(1,128)}, u32[]{:S(2)}) copy-start(f32[1,3,2048]{2,0,1:T(1,128)} %param.10) | copy-start | bytes 73732
  21.3 15.9 %collective-permute-start.1 = (bf16[3,608,128]{2,1,0:T(8,128)(2,1)S(1)}, bf16[3,608,128]{2,1,0:T(8,128)(2,1)S(1)}, u32[]{:S(2)}, u32[]{:S(2)}) collective-permute-start(bf16[3,608,128]{2,1,0:T(8,128)(2,1)S(1)} %get-tuple-element.55), channel_id=1, source_target_pairs={{0,2},{1,3},{2,4},{3,5},{4,6},{5,7},{8,10},{9,11},{10,12},{11,13},... | collective-permute-start | bytes 1400840 | tf_op jit(solution)/shard_map/ppermute | solution.py:527
  25.1 13.2 %collective-permute-start.2 = (bf16[3,608,128]{2,1,0:T(8,128)(2,1)S(1)}, bf16[3,608,128]{2,1,0:T(8,128)(2,1)S(1)}, u32[]{:S(2)}, u32[]{:S(2)}) collective-permute-start(bf16[3,608,128]{2,1,0:T(8,128)(2,1)S(1)} %get-tuple-element.54), channel_id=1, source_target_pairs={{2,0},{3,1},{4,2},{5,3},{6,4},{7,5},{10,8},{11,9},{12,10},{13,11},... | collective-permute-start | bytes 1400840 | tf_op jit(solution)/shard_map/ppermute | solution.py:528
  37.3 31.9 %copy-start.11 = (f32[32]{0:T(128)S(1)}, f32[32]{0:T(128)}, u32[]{:S(2)}) copy-start(f32[32]{0:T(128)} %param.19) | copy-start | bytes 388
  37.3 1.0 copy-start.2
  38.3 0.8 copy-start.3
  55.4 22.5 %collective-permute-start.3 = (bf16[4,560,128]{2,1,0:T(8,128)(2,1)}, bf16[4,560,128]{2,1,0:T(8,128)(2,1)S(1)}, u32[]{:S(2)}, u32[]{:S(2)}) collective-permute-start(bf16[4,560,128]{2,1,0:T(8,128)(2,1)} %get-tuple-element.32), channel_id=1, source_target_pairs={{0,2},{1,3},{2,4},{3,5},{4,6},{5,7},{8,10},{9,11},{10,12},{11,13},... | collective-permute-start | bytes 1720328 | tf_op jit(solution)/shard_map/ppermute | solution.py:560
  59.7 18.1 %collective-permute-start.4 = (bf16[4,560,128]{2,1,0:T(8,128)(2,1)}, bf16[4,560,128]{2,1,0:T(8,128)(2,1)S(1)}, u32[]{:S(2)}, u32[]{:S(2)}) collective-permute-start(bf16[4,560,128]{2,1,0:T(8,128)(2,1)} %get-tuple-element.33), channel_id=1, source_target_pairs={{2,0},{3,1},{4,2},{5,3},{6,4},{7,5},{10,8},{11,9},{12,10},{13,11},... | collective-permute-start | bytes 1720328 | tf_op jit(solution)/shard_map/ppermute | solution.py:561
  62.3 15.5 %all-to-all-start = ((f32[8,1,128]{2,1,0:T(1,128)}), f32[8,1,128]{2,1,0:T(1,128)S(1)}, u32[]{:S(2)}, u32[]{:S(2)}) async-start(f32[8,1,128]{2,1,0:T(1,128)} %broadcast_in_dim.44), calls=%async_computation | async-start | bytes 8192 | tf_op jit(solution)/shard_map/all_to_all | solution.py:562
  77.8 0.6 copy-start.10
  77.8 0.8 copy-start
  77.9 1.0 copy-start.1
  105.9 1.8 %copy-start.8 = (f32[3,2048]{1,0:T(4,128)S(1)}, f32[3,2048]{1,0:T(4,128)}, u32[]{:S(2)}) copy-start(f32[3,2048]{1,0:T(4,128)} %get-tuple-element.36) | copy-start | bytes 73732
  129.7 21.7 %all-to-all-start.2 = ((f32[32,34,128]{2,1,0:T(8,128)}), f32[32,34,128]{2,1,0:T(8,128)S(1)}, u32[]{:S(2)}, u32[]{:S(2)}) async-start(f32[32,34,128]{2,1,0:T(8,128)} %broadcast_in_dim.52), calls=%async_computation.2 | async-start | bytes 1310720 | tf_op jit(solution)/shard_map/all_to_all | solution.py:600

commit v2 on v1

v2 whole, which is shorter than its diff:
```python
import functools

import jax
import jax.numpy as jnp
from jax import lax
from jax.experimental import pallas as pl
from jax.experimental.pallas import tpu as pltpu
from jax.sharding import PartitionSpec as P


NXY = 64
resolution = 0.375
f32 = jnp.float32
bf16 = jnp.bfloat16

JB = 16
OWN = 32
RD, RS, R2, R3, RM, RG = 38, 37, 36, 35, 34, 33
BR = 41 * JB
CH = 128
NCH = 5
NT = (((1,), (1,)), ((), ()))
NN = (((1,), (0,)), ((), ()))


def dotf(a, b, dims):
    return lax.dot_general(a, b, dims, preferred_element_type=f32)


def lane_block(shape):
    return lax.broadcasted_iota(jnp.int32, shape, 1) // 32


def spread(block, turn):
    if turn == 1:
        return block
    out = pltpu.roll(block, ((turn - 1) * 32) % 128, 1)
    lanes = lane_block(block.shape)
    if turn == 0:
        return jnp.where(lanes == 3, 0.0, out)
    if turn == 3:
        return jnp.where(lanes == 0, 0.0, out)
    return out


def one_block(block, source, target):
    out = pltpu.roll(block, ((target - source) * 32) % 128, 1)
    return jnp.where(lane_block(block.shape) == target, out, 0.0)


def build_forward(u_ref, conv, flip, w_ref):
    zero = jnp.zeros((32, 128), bf16)

    def body(f, carry):
        fe = jnp.where(flip == 0, f, 2 - f)
        us = [u_ref[conv * 9 + e * 3 + fe] for e in range(3)]
        for jo in range(4):
            rows = [pl.ds(p * 128 + jo * 32, 32) for p in range(2)]
            for e in range(3):
                main = spread(us[e], jo).astype(bf16)
                for p in range(2):
                    w_ref[f, rows[p], pl.ds((p + e) * 128, 128)] = main
            w_ref[f, rows[0], pl.ds(3 * 128, 128)] = zero
            w_ref[f, rows[1], pl.ds(0, 128)] = zero
            for p in range(2):
                for half in range(2):
                    edge = zero
                    if jo in (0, 3):
                        parts = []
                        for q in (2 * half, 2 * half + 1):
                            if 0 <= q - p <= 2:
                                at = 2 * (q % 2)
                                parts.append(one_block(us[q - p], 0, at) if jo == 0 else one_block(us[q - p], 2, at + 1))
                        edge = functools.reduce(jnp.add, parts).astype(bf16)
                    w_ref[f, rows[p], pl.ds(512 + half * 128, 128)] = edge
        return carry

    lax.fori_loop(0, 3, body, 0)


def build_backward(u_ref, conv, flip, w_ref):
    zero = jnp.zeros((32, 128), bf16)

    def body(f, carry):
        fe = jnp.where(flip == 0, 2 - f, f)
        for e in range(3):
            u = u_ref[conv * 9 + (2 - e) * 3 + fe]
            tiles = [spread(u, jc).astype(bf16) for jc in range(4)]
            tiles += [one_block(u, 2, 0).astype(bf16), one_block(u, 0, 3).astype(bf16)]
            for p in range(2):
                q = p + e
                lanes = pl.ds(p * 128, 128)
                for jc in range(6):
                    at = q * 128 + jc * 32 if jc < 4 else 512 + q * 64 + (jc - 4) * 32
                    w_ref[f, pl.ds(at, 32), lanes] = tiles[jc]
        for p, q in ((0, 3), (1, 0)):
            lanes = pl.ds(p * 128, 128)
            for jc in range(6):
                at = q * 128 + jc * 32 if jc < 4 else 512 + q * 64 + (jc - 4) * 32
                w_ref[f, pl.ds(at, 32), lanes] = zero
        return carry

    lax.fori_loop(0, 3, body, 0)


def edges(a, b):
    n = a.shape[0]
    lanes = lane_block((n, 128))
    mixed = jnp.where(lanes < 2, pltpu.roll(a, 32, 1), pltpu.roll(b, 96, 1))
    down = pltpu.roll(mixed, 1, 0)
    up = pltpu.roll(mixed, n - 1, 0)
    jb = lax.broadcasted_iota(jnp.int32, (n, 128), 0) % JB
    low = jnp.where(jb == 0, 0.0, down)
    high = jnp.where(jb == JB - 1, 0.0, up)
    return jnp.where(lanes % 2 == 0, low, high)


def patch(x_ref, e_ref, plane, pair, f, n):
    sl = pl.ds(f * JB, n)
    return [x_ref[plane + k, sl, :] for k in range(4)] + [e_ref[pair + k, sl, :] for k in range(2)]


def conv_pair(x_ref, e_ref, plane, pair, rows, w_ref, acc_ref, dims):
    n = rows * JB
    total = None
    for f in range(3):
        lhs = jnp.concatenate(patch(x_ref, e_ref, plane, pair, f, n), axis=1)
        part = dotf(lhs, w_ref[f], dims)
        total = part if total is None else total + part
    acc_ref[pl.ds(0, n), :] = total


def put_pair(main_ref, e_ref, plane, pair, at, va, vb):
    main_ref[plane, pl.ds(at, va.shape[0]), :] = va.astype(bf16)
    main_ref[plane + 1, pl.ds(at, va.shape[0]), :] = vb.astype(bf16)
    if e_ref is not None:
        e_ref[pair, pl.ds(at, va.shape[0]), :] = edges(va, vb).astype(bf16)


def rounded(v):
    return v.astype(bf16).astype(f32)


def clear_pad(ref):
    for k in range(ref.shape[0]):
        ref[k, pl.ds(0, JB), :] = jnp.zeros((JB, 128), ref.dtype)


WIN = 40 * NXY


def pack_planes(h, source, put):
    row = lax.broadcasted_iota(jnp.int32, (256, 256), 0)
    col = lax.broadcasted_iota(jnp.int32, (256, 256), 1)
    mask = jnp.where((row // 32) % 4 == col % 4, 1.0, 0.0).astype(bf16)
    srow = lax.broadcasted_iota(jnp.int32, (64, 256), 0)
    scol = lax.broadcasted_iota(jnp.int32, (64, 256), 1)
    a = srow // JB
    a = jnp.where(h == 0, a, 3 - a)
    pick = jnp.where((srow % JB == (scol // 4) % JB) & (scol // NXY == a), 1.0, 0.0).astype(bf16)
    for ch in range(10):
        at = pl.multiple_of(jnp.where(h == 0, ch, 9 - ch) * 256, 256)
        x0, x1 = source(at)
        wide = jnp.concatenate([x0] * 4 + [x1] * 4, axis=0) * mask
        out = dotf(pick, wide, NT).astype(bf16)
        n = 64 if ch < 9 else 32
        for p in range(2):
            put(p, pl.ds(ch * 64, n), out[:n, p * 128 : (p + 1) * 128])


def widen(raw_ref, wide_ref, sl):
    for p in range(2):
        wide_ref[p, pl.ds(16, 16), :] = jnp.zeros((16, WIN), bf16)
        wide_ref[p, pl.ds(0, raw_ref.shape[1]), :] = raw_ref[p, :, sl]

    def source(at):
        return [wide_ref[p, :, pl.ds(at, 256)] for p in range(2)]

    return source


def pack_own_kernel(raw_ref, out_ref, wide_ref):
    h = place()[1]
    base = pl.multiple_of(jnp.where(h == 0, 0, NXY * NXY - WIN), 256)

    def put(p, sl, val):
        out_ref[p, sl, :] = val

    pack_planes(h, widen(raw_ref, wide_ref, pl.ds(base, WIN)), put)


def pack_kernel(raw_ref, mine_ref, own_ref, up_ref, dn_ref, wide_ref):
    h = place()[1]

    def put(p, sl, val):
        own_ref[2 * (1 - h) + p, sl, :] = val

    pack_planes(h, widen(raw_ref, wide_ref, pl.ds(0, WIN)), put)
    for p in range(2):
        own_ref[2 * h + p] = mine_ref[p]
    for k in range(3):
        up_ref[k] = own_ref[k + 1]
        dn_ref[k] = own_ref[k]


def weights_kernel(u_ref, wf_ref, wb_ref):
    flip = place()[1]
    for conv in range(3):
        build_forward(u_ref, conv, flip, wf_ref.at[conv])
        build_backward(u_ref, conv, flip, wb_ref.at[conv])


def atom_terms(radii, types):
    radius = jnp.zeros(types.shape, f32)
    for c in range(radii.shape[0]):
        radius = radius + jnp.where(types == c, radii[c], 0.0)
    return 1.0 / (radius * radius)


def centre_rows(n, first, step, half):
    row = lax.broadcasted_iota(jnp.int32, (n, 1), 0)
    return ((first + step * row).astype(f32) + 0.5 - half) * resolution


def bump(centre, place, inv_sq):
    offset = centre - place
    return jnp.exp(-2.0 * offset * offset * inv_sq), offset


def first_row(half):
    return jnp.where(half == 0, 0, NXY - 1), jnp.where(half == 0, 1, -1)


def splat_kernel(depth, count, radii, coords_ref, types_ref, out_ref, z_ref, gy_ref, live_ref, y_ref):
    atoms = types_ref.shape[1]
    types = types_ref[...]
    inv_sq = atom_terms(radii, types)
    group, half = place()
    top, step = first_row(half)
    gx = bump(centre_rows(40, top, step, 0.5 * NXY), coords_ref[0], inv_sq)[0]
    gz = bump(centre_rows(16, 4 * group - 3, 1, 0.5 * depth), coords_ref[2], inv_sq)[0]
    for q in range(10):
        z_ref[pl.ds(q * 40, 40), :] = (gz[q : q + 1, :] * gx).astype(bf16)
    gy_ref[...] = bump(centre_rows(NXY, 0, 1, 0.5 * NXY), coords_ref[1], inv_sq)[0]
    kind = lax.broadcasted_iota(jnp.int32, (32, atoms), 0)
    slot = lax.broadcasted_iota(jnp.int32, (32, atoms), 1)
    live_ref[...] = jnp.where((types == kind) & (slot < count[0]), 1.0, 0.0)

    def body(step8, carry):
        for t in range(8):
            y = gy_ref[pl.ds(step8 * 8 + t, 1), :]
            y_ref[pl.ds(t * 32, 32), :] = (live_ref[...] * y).astype(bf16)
        out = dotf(z_ref[...], y_ref[...], NT)
        out_ref[pl.ds(2 * step8, 400, stride=JB), :] = out[:, :128]
        out_ref[pl.ds(2 * step8 + 1, 400, stride=JB), :] = out[:, 128:]
        return carry

    lax.fori_loop(0, 8, body, 0)


def forward_kernel(
    depth, splat_ref, lo_ref, own_ref, hi_ref, w_ref,
    x_ref, ex_ref, h1_ref, e1_ref, h2_ref, e2_ref, m3_ref, up_ref, dn_ref, pool_ref,
    acc_ref,
):
    first = 4 * place()[0] - 3
    for ref in (x_ref, ex_ref, h1_ref, e1_ref, h2_ref, e2_ref):
        clear_pad(ref)

    def inside(q):
        z = first + q
        return jnp.where((z >= 0) & (z < depth), 1.0, 0.0)

    def receptor(q, sl):
        if q < 3:
            return lo_ref[q, sl, :]
        if q < 7:
            return own_ref[q - 3, sl, :]
        return hi_ref[q - 7, sl, :]

    for m in range(5):
        def density(c, carry):
            at = c * 304
            sl = pl.ds(pl.multiple_of(at, 16), 304)
            vals = []
            for q in (2 * m, 2 * m + 1):
                v = splat_ref[pl.ds(pl.multiple_of(q * 640 + at, 16), 304), :] + receptor(q, sl).astype(f32)
                vals.append(rounded(v * inside(q)))
            put_pair(x_ref, ex_ref, 2 * m, m, pl.multiple_of(JB + at, 16), *vals)
            return carry

        lax.fori_loop(0, 2, density, 0)


    def stem(m, carry):
        conv_pair(x_ref, ex_ref, 2 * m, m, RS, w_ref.at[0], acc_ref, NT)
        ia, ib = inside(2 * m + 1), inside(2 * m + 2)
        for c in range(NCH):
            acc = jnp.maximum(acc_ref[pl.ds(c * CH, CH), :], 0.0)
            put_pair(h1_ref, e1_ref, 2 * m, m, JB + c * CH, rounded(acc[:, :128] * ia), rounded(acc[:, 128:] * ib))
        return carry

    lax.fori_loop(0, 4, stem, 0)

    def second(m, carry):
        conv_pair(h1_ref, e1_ref, 2 * m, m, R2, w_ref.at[1], acc_ref, NT)
        ia, ib = inside(2 * m + 2), inside(2 * m + 3)
        for c in range(NCH):
            acc = jnp.maximum(acc_ref[pl.ds(c * CH, CH), :], 0.0)
            put_pair(h2_ref, e2_ref, 2 * m, m, JB + c * CH, rounded(acc[:, :128] * ia), rounded(acc[:, 128:] * ib))
        return carry

    lax.fori_loop(0, 3, second, 0)

    def third(m, pool):
        conv_pair(h2_ref, e2_ref, 2 * m, m, R3, w_ref.at[2], acc_ref, NT)
        for c in range(7):
            sl = pl.ds(c * 80, 80)
            src = pl.ds(JB + c * 80, 80)
            for k in range(2):
                keep = h1_ref[2 * m + 2 + k, src, :].astype(f32)
                summed = keep + acc_ref[sl, pl.ds(128 * k, 128)]
                top = jnp.maximum(summed, 0.0)
                if (c + 1) * 80 > OWN * JB:
                    row = lax.broadcasted_iota(jnp.int32, (80, 128), 0) + c * 80
                    top = jnp.where(row < OWN * JB, top, 0.0)
                pool = pool + jnp.sum(top, axis=0, keepdims=True)
                m3_ref[2 * m + k, sl, :] = jnp.where(summed > 0.0, 1.0, 0.0).astype(bf16)
        return pool

    pool = lax.fori_loop(0, 2, third, jnp.zeros((1, 128), f32))
    pool = pool + pltpu.roll(pool, 64, 1)
    pool = pool + pltpu.roll(pool, 32, 1)
    pool_ref[...] = jnp.broadcast_to(pool, pool_ref.shape)
    for k in range(3):
        up_ref[k] = m3_ref[k + 1]
        dn_ref[k] = m3_ref[k]
    up_ref[3] = h2_ref[3, pl.ds(JB, R3 * JB), :]
    dn_ref[3] = h2_ref[2, pl.ds(JB, R3 * JB), :]


def weight_grad(x_ref, e_ref, plane, pair, grads, g_ref, first):
    ut = jnp.transpose(grads).astype(bf16)
    for f in range(3):
        rhs = jnp.concatenate(patch(x_ref, e_ref, plane, pair, f, OWN * JB), axis=1)
        part = dotf(ut, rhs, NN)
        g_ref[f] = part if first else g_ref[f] + part


def extract(g_ref, flip, scale, put):
    lanes = lane_block((32, 128))

    def body(f, carry):
        fe = jnp.where(flip == 0, f, 2 - f)
        for e in range(3):
            total = jnp.zeros((32, 128), f32)
            for p in range(2):
                q = p + e
                for jo in range(4):
                    rows = pl.ds(p * 128 + jo * 32, 32)
                    block = g_ref[f, rows, pl.ds(q * 128, 128)]
                    if jo != 1:
                        block = pltpu.roll(block, ((1 - jo) * 32) % 128, 1)
                    if jo == 0:
                        block = jnp.where((lanes == 1) | (lanes == 2), block, 0.0)
                    elif jo == 3:
                        block = jnp.where(lanes < 2, block, 0.0)
                    else:
                        block = jnp.where(lanes < 3, block, 0.0)
                    total = total + block
                    if jo in (0, 3):
                        side = g_ref[f, rows, pl.ds(512 + (q // 2) * 128, 128)]
                        at = 2 * (q % 2)
                        total = total + (one_block(side, at, 0) if jo == 0 else one_block(side, at + 1, 2))
            put(e * 3 + fe, total * scale)
        return carry

    lax.fori_loop(0, 3, body, 0)


def prepare_kernel(m3_ref, h2_ref, e2_ref, gw_ref, g_ref):
    flip = place()[1]
    rows = pl.ds(0, OWN * JB)
    for m in range(2):
        grads = jnp.concatenate([m3_ref[2 * m, rows, :], m3_ref[2 * m + 1, rows, :]], axis=1)
        weight_grad(h2_ref, e2_ref, 2 * m, m, grads, g_ref, m == 0)

    def put(k, val):
        gw_ref[k] = val

    extract(g_ref, flip, 1.0, put)


def backward_kernel(
    depth, label, pool_ref, mine_ref, head_ref,
    x_ref, ex_ref, h1_ref, e1_ref, h2_ref, m3_ref, lo_ref, hi_ref, gw2_ref, w_ref,
    keep_ref, give_ref, score_ref, loss_ref, dk_ref,
    t_ref, et_ref, mg_ref, em_ref, sg_ref, es_ref, hm_ref, acc_ref, g_ref, flat_ref, dg_ref,
):
    flip = place()[1]
    scale = 1.0 / (depth * NXY * NXY)
    head = head_ref[...]
    pooled = pool_ref[0:1, :] * scale
    lane = lax.broadcasted_iota(jnp.int32, (1, 128), 1)
    score = jnp.sum(jnp.where(lane < 32, pooled * head, 0.0), axis=1, keepdims=True)
    sign = (2 * label[0] - 1).astype(f32)
    logit = -sign * score
    score_grad = -sign / (1.0 + jnp.exp(-logit))
    loss = jnp.maximum(logit, 0.0) + jnp.log1p(jnp.exp(-jnp.abs(logit)))
    score_ref[0] = jnp.sum(score)
    loss_ref[0] = jnp.sum(loss)
    tone = rounded(score_grad * head)

    half_rows = keep_ref.shape[0]
    lanes = lane_block((32, 128))
    eye = lax.broadcasted_iota(jnp.int32, (32, 128), 0) == lax.broadcasted_iota(jnp.int32, (32, 128), 1)
    tall = jnp.sum(jnp.where(eye, tone, 0.0), axis=1, keepdims=True) * scale
    for k in range(6):
        tile = gw2_ref[k] * tall
        for g in range(3):
            flat_ref[pl.ds((3 * k + g) * 32, 32), :] = one_block(tile, g, 3)
    for k in range(3):
        flat_ref[pl.ds((18 + k) * 32, 32), :] = gw2_ref[6 + k] * tall
    tail = 2 * half_rows - 672
    flat_ref[pl.ds(672, tail), :] = jnp.where(
        lax.broadcasted_iota(jnp.int32, (tail, 128), 0) == 0, score_grad * mine_ref[0:1, :] * scale, 0.0
    )

    def put_rows(conv):
        def put(k, val):
            rows = pl.ds(pl.multiple_of((conv * 9 + k) * 32, 32), 32)
            flat_ref[rows, :] = jnp.where(lanes < 3, val, flat_ref[rows, :])

        return put

    for ref in (t_ref, et_ref, mg_ref, em_ref, sg_ref, es_ref):
        clear_pad(ref)
    mask_of = lambda q: (lo_ref.at[q] if q < 3 else m3_ref.at[q - 3] if q < 7 else hi_ref.at[q - 7])
    for m in range(5):
        for c in range(5):
            sl = pl.ds(c * 112, 112)
            vals = [jnp.where(mask_of(q)[sl, :].astype(f32) > 0.0, tone, 0.0) for q in (2 * m, 2 * m + 1)]
            put_pair(t_ref, et_ref, 2 * m, m, JB + c * 112, *vals)
    hm_ref[0] = lo_ref[3]
    hm_ref[7] = hi_ref[3]
    for k in range(6):
        hm_ref[k + 1] = h2_ref[k, pl.ds(JB, R3 * JB), :]

    own_rows = pl.ds(JB, OWN * JB)

    def mid(m, carry):
        conv_pair(t_ref, et_ref, 2 * m, m, RM, w_ref.at[2], acc_ref, NN)
        for c in range(NCH):
            sl = pl.ds(c * 112, 112)
            vals = [
                rounded(jnp.where(hm_ref[2 * m + k, sl, :].astype(f32) > 0.0, acc_ref[sl, pl.ds(128 * k, 128)], 0.0))
                for k in range(2)
            ]
            put_pair(mg_ref, em_ref, 2 * m, m, JB + c * 112, *vals)
        return carry

    lax.fori_loop(0, 4, mid, 0)

    for m in range(3):
        ga = mg_ref[1 + 2 * m, own_rows, :]
        gb = mg_ref[2 + 2 * m, own_rows, :]
        if m == 0:
            ga = jnp.zeros_like(ga)
        if m == 2:
            gb = jnp.zeros_like(gb)
        weight_grad(h1_ref, e1_ref, 2 * m, m, jnp.concatenate([ga, gb], axis=1), g_ref, m == 0)
    extract(g_ref, flip, scale, put_rows(1))

    def low(m, carry):
        conv_pair(mg_ref, em_ref, 2 * m, m, RG, w_ref.at[1], acc_ref, NN)
        for c in range(NCH):
            sl = pl.ds(c * 112, 112)
            src = pl.ds(JB + c * 112, 112)
            vals = []
            for k in range(2):
                back = t_ref[2 * m + 2 + k, src, :].astype(f32) + acc_ref[sl, pl.ds(128 * k, 128)]
                vals.append(rounded(jnp.where(h1_ref[2 * m + 1 + k, src, :].astype(f32) > 0.0, back, 0.0)))
            put_pair(sg_ref, es_ref, 2 * m, m, JB + c * 112, *vals)
        return carry

    lax.fori_loop(0, 3, low, 0)

    for m in range(2):
        grads = jnp.concatenate([sg_ref[1 + 2 * m, own_rows, :], sg_ref[2 + 2 * m, own_rows, :]], axis=1)
        weight_grad(x_ref, ex_ref, 2 + 2 * m, 1 + m, grads, g_ref, m == 0)
    extract(g_ref, flip, scale, put_rows(0))
    core = lax.axis_index("core")
    keep_ref[...] = flat_ref[pl.ds(pl.multiple_of(core * half_rows, 16), half_rows), :]
    give_ref[...] = flat_ref[pl.ds(pl.multiple_of((1 - core) * half_rows, 16), half_rows), :]

    def last(m, carry):
        conv_pair(sg_ref, es_ref, 2 * m, m, OWN, w_ref.at[0], acc_ref, NN)
        for k in range(2):
            at = pl.ds(pl.multiple_of((2 * m + k) * OWN * JB, 16), OWN * JB)
            dg_ref[at, :] = rounded(acc_ref[pl.ds(0, OWN * JB), pl.ds(128 * k, 128)])
        return carry

    lax.fori_loop(0, 2, last, 0)
    for jb in range(JB):
        dk_ref[:, pl.ds(jb * 128, 128)] = dg_ref[pl.ds(jb, 4 * OWN, stride=JB), :].astype(bf16)


def atom_kernel(depth, count, radii, coords_ref, types_ref, dk_ref, force_ref, gy_ref, sy_ref, live_ref, y_ref, dy_ref):
    types = types_ref[...]
    inv_sq = atom_terms(radii, types)
    atoms = types.shape[1]
    gy, off = bump(centre_rows(NXY, 0, 1, 0.5 * NXY), coords_ref[1], inv_sq)
    gy_ref[...] = gy
    sy_ref[...] = 4.0 * off * inv_sq * gy
    kind = lax.broadcasted_iota(jnp.int32, (32, atoms), 0)
    slot = lax.broadcasted_iota(jnp.int32, (32, atoms), 1)
    live_ref[...] = jnp.where((types == kind) & (slot < count[0]), 1.0, 0.0)
    group, half = place()
    top, step = first_row(half)
    wide = 256
    for b in range(atoms // wide):
        sl = pl.ds(b * wide, wide)

        def table(j, carry):
            live = live_ref[:, sl]
            at = pl.ds(pl.multiple_of(j * 32, 32), 32)
            y_ref[at, :] = (live * gy_ref[pl.ds(j, 1), sl]).astype(bf16)
            dy_ref[at, :] = (live * sy_ref[pl.ds(j, 1), sl]).astype(bf16)
            return carry

        lax.fori_loop(0, NXY, table, 0, unroll=4)
        plain = dotf(dk_ref[...], y_ref[...], NN)
        slope = dotf(dk_ref[...], dy_ref[...], NN)
        inv = inv_sq[:, b * wide : (b + 1) * wide]
        gx, off_x = bump(centre_rows(OWN, top, step, 0.5 * NXY), coords_ref[0, :, sl], inv)
        dgx = 4.0 * off_x * inv * gx
        gz, off_z = bump(centre_rows(8, 4 * group, 1, 0.5 * depth), coords_ref[2, :, sl], inv)
        dgz = 4.0 * off_z * inv * gz
        fx = jnp.zeros((1, wide), f32)
        fy = jnp.zeros((1, wide), f32)
        fz = jnp.zeros((1, wide), f32)
        for k in range(4):
            pk = plain[k * OWN : (k + 1) * OWN, :]
            sk = slope[k * OWN : (k + 1) * OWN, :]
            fx = fx + gz[k : k + 1, :] * jnp.sum(pk * dgx, axis=0, keepdims=True)
            fy = fy + gz[k : k + 1, :] * jnp.sum(sk * gx, axis=0, keepdims=True)
            fz = fz + dgz[k : k + 1, :] * jnp.sum(pk * gx, axis=0, keepdims=True)
        force_ref[0:1, sl] = fx
        force_ref[1:2, sl] = fy
        force_ref[2:3, sl] = fz


def place():
    s = lax.axis_index("slab")
    return s // 2, s % 2


def smem():
    return pl.BlockSpec(memory_space=pltpu.SMEM)


def vmem():
    return pl.BlockSpec(memory_space=pltpu.VMEM)


def lane_rows(w):
    o, c = w.shape[:2]
    moved = jnp.transpose(w, (2, 3, 0, 4, 1)).astype(f32)
    moved = jnp.pad(moved, ((0, 0), (0, 0), (0, 0), (0, 1), (0, 32 - c)))
    return moved.reshape(9, o, 128)


def finish_kernel(mine_ref, other_ref, fa_ref, fb_ref, stem_ref, one_ref, two_ref, head_ref, force_ref, both_ref):
    core = lax.axis_index("core")
    both_ref[core] = mine_ref[...]
    both_ref[1 - core] = other_ref[...]
    half_rows = mine_ref.shape[0]

    def tile(t):
        return both_ref[t * 32 // half_rows, pl.ds(t * 32 % half_rows, 32), :]

    for t in range(27):
        conv, k = divmod(t, 9)
        ref = (stem_ref, one_ref, two_ref)[conv]
        for g in range(3):
            if conv < 2:
                block, at = tile(t), g
            elif k < 6:
                block, at = tile(3 * k + g), 3
            else:
                block, at = tile(12 + k), g
            val = pltpu.roll(block, 128 - 32 * at, 1) if at else block
            ref[3 * k + g] = val[:, : ref.shape[2]]
    head_ref[...] = both_ref[672 // half_rows, pl.ds(672 % half_rows, 8), :][:1, :32]
    total = fa_ref[...] + fb_ref[...]
    for k in range(3):
        force_ref[k] = total[k : k + 1, :]


def call(kernel, limit, flops, **kwargs):
    return pl.pallas_call(
        kernel,
        compiler_params=pltpu.CompilerParams(vmem_limit_bytes=limit << 20),
        cost_estimate=pl.CostEstimate(flops=int(flops), bytes_accessed=4_000_000, transcendentals=0),
        **kwargs,
    )


def local(coords, atom_types, counts, labels, receptor, radii, w_stem, w_one, w_two, w_head):
    slab_count = lax.axis_size("slab")
    y_count = lax.axis_size("y")
    atoms = coords.shape[2]
    half = lax.axis_index("slab") % 2
    depth = receptor.shape[2] * slab_count
    bh = (RD * JB, 128)
    places = coords.reshape(3, 1, atoms)

    raw = jnp.transpose(receptor[0], (1, 0, 2))
    theirs = lax.dynamic_slice_in_dim(raw, jnp.where(half == 1, 0, NXY * NXY - WIN), WIN, 2)
    other = lax.ppermute(theirs, "slab", [(i, i ^ 1) for i in range(slab_count)])
    mine = call(
        pack_own_kernel, 6, 2e9,
        out_shape=jax.ShapeDtypeStruct((2,) + bh, bf16),
        in_specs=[vmem()],
        out_specs=vmem(),
        scratch_shapes=[pltpu.VMEM((2, 32, WIN), bf16)],
    )(raw)
    u = jnp.concatenate([lane_rows(w_stem), lane_rows(w_one), lane_rows(w_two)], axis=0)
    head = jnp.tile(w_head, 4)[None, :]
    wf, wb = call(
        weights_kernel, 6, 3e9,
        out_shape=[jax.ShapeDtypeStruct((3, 3, 256, 768), bf16), jax.ShapeDtypeStruct((3, 3, 768, 256), bf16)],
        in_specs=[vmem()],
        out_specs=[vmem()] * 2,
    )(u)
    other, mine, wf, wb, head = lax.optimization_barrier((other, mine, wf, wb, head))
    own, own_up, own_dn = call(
        pack_kernel, 6, 2e9,
        out_shape=[jax.ShapeDtypeStruct((n,) + bh, bf16) for n in (4, 3, 3)],
        in_specs=[vmem(), vmem()],
        out_specs=[vmem()] * 3,
        scratch_shapes=[pltpu.VMEM((2, 32, WIN), bf16)],
    )(other, mine)
    ups = [(i, i + 2) for i in range(slab_count - 2)]
    downs = [(i + 2, i) for i in range(slab_count - 2)]
    lo = lax.ppermute(own_up, "slab", ups)
    hi = lax.ppermute(own_dn, "slab", downs)

    splat = call(
        functools.partial(splat_kernel, depth), 10, 8e9,
        out_shape=jax.ShapeDtypeStruct((6400, 128), f32),
        in_specs=[smem(), smem(), vmem(), vmem()],
        out_specs=vmem(),
        scratch_shapes=[
            pltpu.VMEM((400, atoms), bf16),
            pltpu.VMEM((NXY, atoms), f32),
            pltpu.VMEM((32, atoms), f32),
            pltpu.VMEM((256, atoms), bf16),
        ],
    )(counts, radii, places, atom_types)

    big = lambda n: jax.ShapeDtypeStruct((n, BR, 128), bf16)
    thin = lambda n: jax.ShapeDtypeStruct((n, R3 * JB, 128), bf16)
    x, ex, h1, e1, h2, e2, m3, up, dn, pool = call(
        functools.partial(forward_kernel, depth), 8, 1.4e10,
        out_shape=[big(10), big(5), big(8), big(4), big(6), big(3), thin(4), thin(4), thin(4),
                   jax.ShapeDtypeStruct((8, 128), f32)],
        in_specs=[vmem()] * 5,
        out_specs=[vmem()] * 10,
        scratch_shapes=[pltpu.VMEM((BR, 256), f32)],
    )(splat, lo, own, hi, wf)

    def over_slab(value, rounds):
        step = 1
        while step < rounds:
            value = value + lax.ppermute(value, "slab", [(i, i ^ step) for i in range(slab_count)])
            step *= 2
        return value

    from_lo = lax.ppermute(up, "slab", ups)
    from_hi = lax.ppermute(dn, "slab", downs)
    pool_sum = over_slab(pool, slab_count)
    gw2 = call(
        prepare_kernel, 8, 3e9,
        out_shape=jax.ShapeDtypeStruct((9, 32, 128), f32),
        in_specs=[vmem()] * 3,
        out_specs=vmem(),
        scratch_shapes=[pltpu.VMEM((3, 256, 768), f32)],
    )(m3, h2, e2)

    ranks = y_count * slab_count
    each = -(-680 // (2 * ranks))
    if each > 8:
        each = -(-each // 8) * 8
    half_rows = each * ranks
    keep, give, scores, pose_loss, dk = call(
        functools.partial(backward_kernel, depth), 18, 1.4e10,
        out_shape=[
            jax.ShapeDtypeStruct((half_rows, 128), f32), jax.ShapeDtypeStruct((half_rows, 128), f32),
            jax.ShapeDtypeStruct((1,), f32), jax.ShapeDtypeStruct((1,), f32),
            jax.ShapeDtypeStruct((4 * OWN, 2048), bf16),
        ],
        in_specs=[smem()] + [vmem()] * 13,
        out_specs=[vmem(), vmem(), smem(), smem(), vmem()],
        scratch_shapes=[
            pltpu.VMEM((10, BR, 128), bf16), pltpu.VMEM((5, BR, 128), bf16),
            pltpu.VMEM((8, BR, 128), bf16), pltpu.VMEM((4, BR, 128), bf16),
            pltpu.VMEM((6, BR, 128), bf16), pltpu.VMEM((3, BR, 128), bf16),
            pltpu.VMEM((8, R3 * JB, 128), bf16),
            pltpu.VMEM((BR, 256), f32), pltpu.VMEM((3, 256, 768), f32),
            pltpu.VMEM((2 * half_rows, 128), f32), pltpu.VMEM((4 * OWN * JB, 128), f32),
        ],
    )(labels, pool_sum, pool, head, x, ex, h1, e1, h2, m3, from_lo, from_hi, gw2, wb)

    swap = [(0, 1), (1, 0)]
    chip = keep + lax.ppermute(give, "core", swap)
    got = lax.all_to_all(chip.reshape(ranks, each, 128), ("y", "slab"), 0, 0)
    force = call(
        functools.partial(atom_kernel, depth), 12, 1e10,
        out_shape=jax.ShapeDtypeStruct((3, atoms), f32),
        in_specs=[smem(), smem(), vmem(), vmem(), vmem()],
        out_specs=vmem(),
        scratch_shapes=[
            pltpu.VMEM((NXY, atoms), f32), pltpu.VMEM((NXY, atoms), f32), pltpu.VMEM((32, atoms), f32),
            pltpu.VMEM((2048, 256), bf16), pltpu.VMEM((2048, 256), bf16),
        ],
    )(counts, radii, places, atom_types, dk)
    total = jnp.sum(got, axis=0)
    total, force = lax.optimization_barrier((total, force))
    spread_total = jnp.broadcast_to(total[None], (ranks, each, 128))
    gathered = lax.all_to_all(spread_total, ("y", "slab"), 0, 0)
    gathered = gathered.reshape(half_rows, 128)
    gathered_other = lax.ppermute(gathered, "core", swap)
    last_step = slab_count // 2
    force = over_slab(force, last_step)
    force_other = lax.ppermute(force, "slab", [(i, i ^ last_step) for i in range(slab_count)])

    grid = lambda c: jax.ShapeDtypeStruct((27, 32, c), f32)
    stem, one, two, grad_head, atom_grad = call(
        finish_kernel, 6, 1e8,
        out_shape=[grid(w_stem.shape[1]), grid(32), grid(32), jax.ShapeDtypeStruct((1, 32), f32),
                   jax.ShapeDtypeStruct((3, 1, atoms), f32)],
        in_specs=[vmem()] * 4,
        out_specs=[vmem()] * 5,
        scratch_shapes=[pltpu.VMEM((2, half_rows, 128), f32)],
    )(gathered, gathered_other, force, force_other)
    shaped = lambda v: v.reshape(3, 3, 3, 32, v.shape[2]).transpose(3, 4, 0, 1, 2)
    return (scores, pose_loss, atom_grad.reshape(1, 3, atoms), shaped(stem), shaped(one), shaped(two),
            grad_head.reshape(32))


def solution(mesh):
    pose_count, slab_count = mesh.shape["pose"], mesh.shape["slab"]
    fine = jax.sharding.Mesh(mesh.devices.reshape(pose_count // 2, 2, slab_count), ("y", "core", "slab"))
    pose = ("y", "core")

    return jax.shard_map(
        local,
        mesh=fine,
        in_specs=(
            P(pose, None, None),
            P(pose, None),
            P(pose),
            P(pose),
            P(pose, None, "slab", None),
            P(),
            P(),
            P(),
            P(),
            P(),
        ),
        out_specs=(P(pose), P(pose), P(pose, None, None), P(), P(), P(), P()),
        check_vma=False,
    )
```

time: 158 us -> 121 us (0.77)
  Pallas kernels: 57.8 us -> 44.8 us
  local copies, waits for them, and re-layouts: 16.2 us -> 5.13 us
  blocking collectives: 20.8 us -> 13.6 us
  waiting for transfers between devices: 32 us -> 27.3 us
  starting transfers between devices: 23.1 us -> 26.5 us
  other arithmetic: 3.07 us -> 0.8 us
  between operations: 4.19 us -> 2.23 us
    ppermute x2 -> x10, waiting for transfers between devices: 1.02 us -> 25.4 us  [the longest x5 15 us: over_slab(): lax.ppermute(value, 'slab', [(i, i ^ step) for i in range(slab_count)])]
    all_to_all x2 -> x1, waiting for transfers between devices: 25 us -> 1.33 us  [local(): got = lax.all_to_all(chip.reshape(ranks, each, 128), ('y', 'slab'), 0, 0)]
    pallas_call x4 -> x9, Pallas kernels: 57.8 us -> 44.8 us  [the longest x1 14 us: local(): call(functools.partial(backward_kernel, depth), 18, 14000000000.0, out_sh...]
    ppermute x2 -> x10, starting transfers between devices: 5.05 us -> 13.9 us  [the longest x5 7.75 us: over_slab(): lax.ppermute(value, 'slab', [(i, i ^ step) for i in range(slab_count)])]
    all_to_all x1, blocking collectives: 20.8 us -> 13.6 us  [local(): gathered = lax.all_to_all(spread_total, ('y', 'slab'), 0, 0)]
    ppermute x1, waiting for transfers between devices: 5.97 us -> 0.6 us  [local(): lax.ppermute(theirs, 'slab', [(i, i ^ 1) for i in range(slab_count)])]
    all_to_all x2 -> x1, starting transfers between devices: 9.49 us -> 4.58 us  [local(): got = lax.all_to_all(chip.reshape(ranks, each, 128), ('y', 'slab'), 0, 0)]
    unnamed x32 -> x16, local copies, waits for them, and re-layouts: 6.64 us -> 2.76 us
  transfers between devices with their start and end apart: 7 -> 14, of which waited for: 4 -> 11; matrix products, arithmetic and copies ran while one was open for 4% -> 3% of each run, Pallas kernels for 5% -> 15%
where the time goes in v2:
time: 121 us; the launch traced here: 120 us
  Pallas kernels  44.8 us (37%)
  waiting for transfers between devices  27.3 us (23%)
  starting transfers between devices  26.5 us (22%)
  blocking collectives  13.6 us (11%)
  local copies, waits for them, and re-layouts  5.13 us (4%)
  between operations  2.23 us (2%)
    ppermute x5, waiting for transfers between devices, over_slab(): lax.ppermute(value, 'slab', [(i, i ^ step) for i in range(slab_count)])  15 us
    pallas_call x1, Pallas kernels, local(): call(functools.partial(backward_kernel, depth), 18, 14000000000.0, out_sh...  14 us
    all_to_all x1, blocking collectives, local(): gathered = lax.all_to_all(spread_total, ('y', 'slab'), 0, 0)  13.6 us
    pallas_call x1, Pallas kernels, local(): call(functools.partial(forward_kernel, depth), 8, 14000000000.0, out_shap...  10.4 us
    ppermute x5, starting transfers between devices, over_slab(): lax.ppermute(value, 'slab', [(i, i ^ step) for i in range(slab_count)])  7.75 us
    pallas_call x1, Pallas kernels, local(): call(functools.partial(atom_kernel, depth), 12, 10000000000.0, out_shape=...  7.35 us
    pallas_call x1, Pallas kernels, local(): call(functools.partial(splat_kernel, depth), 10, 8000000000.0, out_shape=...  6.64 us
    all_to_all x1, starting transfers between devices, local(): got = lax.all_to_all(chip.reshape(ranks, each, 128), ('y', 'slab'), 0, 0)  4.58 us
  transfers between devices with their start and end apart: 14, of which 11 were waited for; matrix products, arithmetic and copies ran while one was open for 3% of the time, Pallas kernels for 15%

profile of v2, /device:TPU:0, one launch (start us, length us, event | category | flops | bytes accessed | tf_op | source)
XLA Modules:
  0.0 120.4 jit_solution(3798471688785801858)
XLA Ops:
  0.7 1.2 %constant_dynamic-slice_fusion = bf16[1,28,2,2560]{3,2,1,0:T(2,128)(2,1)S(1)} fusion(bf16[1,28,2,4096]{3,2,1,0:T(2,128)(2,1)} %param.14, s32[]{:T(128)S(6)} %select_n.13), kind=kLoop, calls=%fused_computation.3 | loop fusion | bytes 573444 | tf_op jit(solution)/shard_map/dynamic-slice.1
  1.9 3.0 %collective-permute-start = (bf16[2,28,2560]{2,1,0:T(8,128)(2,1)S(1)}, bf16[2,28,2560]{2,1,0:T(8,128)(2,1)S(1)}, u32[]{:S(2)}, u32[]{:S(2)}) collective-permute-start(bf16[2,28,2560]{2,1,0:T(8,128)(2,1)S(1)} %bitcast.32), channel_id=1, source_target_pairs={{0,1},{1,0},{2,3},{3,2},{4,5},{5,4},{6,7},{7,6},{8,9},{9,8},{10,11... | collective-permute-start | bytes 860168 | tf_op jit(solution)/shard_map/ppermute | solution.py:620
  5.0 1.3 %copy.27 = bf16[1,28,2,4096]{3,1,2,0:T(8,128)(2,1)S(1)} copy(bf16[1,28,2,4096]{3,2,1,0:T(2,128)(2,1)} %param.14) | data formatting | bytes 917504 | tf_op args[4]
  6.2 1.1 copy.22
  10.1 1.9 %shard_map.155 = (bf16[3,3,256,768]{3,2,1,0:T(8,128)(2,1)S(1)}, bf16[3,3,768,256]{3,2,1,0:T(8,128)(2,1)S(1)}) custom-call(f32[27,32,128]{2,1,0:T(8,128)S(1)} %maximum_convert_fusion.u_ref), custom_call_target="tpu_custom_call" | custom-call | flops 3000000000 | bytes 4000000 | tf_op jit(solution)/shard_map/pallas_call | solution.py:630
  13.3 3.8 %collective-permute-start.1 = (bf16[3,608,128]{2,1,0:T(8,128)(2,1)S(1)}, bf16[3,608,128]{2,1,0:T(8,128)(2,1)S(1)}, u32[]{:S(2)}, u32[]{:S(2)}) collective-permute-start(bf16[3,608,128]{2,1,0:T(8,128)(2,1)S(1)} %get-tuple-element.43), channel_id=1, source_target_pairs={{0,2},{1,3},{2,4},{3,5},{4,6},{5,7},{8,10},{9,11},{10,12},{11,13},... | collective-permute-start | bytes 1400840 | tf_op jit(solution)/shard_map/ppermute | solution.py:646
  17.1 1.3 %collective-permute-start.2 = (bf16[3,608,128]{2,1,0:T(8,128)(2,1)S(1)}, bf16[3,608,128]{2,1,0:T(8,128)(2,1)S(1)}, u32[]{:S(2)}, u32[]{:S(2)}) collective-permute-start(bf16[3,608,128]{2,1,0:T(8,128)(2,1)S(1)} %get-tuple-element.45), channel_id=1, source_target_pairs={{2,0},{3,1},{4,2},{5,3},{6,4},{7,5},{10,8},{11,9},{12,10},{13,11},... | collective-permute-start | bytes 1400840 | tf_op jit(solution)/shard_map/ppermute | solution.py:647
  18.4 6.6 %shard_map.153.splat_ref = f32[6400,128]{1,0:T(8,128)S(1)} custom-call(s32[1]{0:T(128)S(6)} %copy.29.count, f32[28]{0:T(128)S(1)} %copy-done.2, f32[3,1,2048]{2,1,0:T(1,128)S(1)} %bitcast.30, s32[1,2048]{1,0:T(1,128)S(1)} %copy-done.1), custom_call_target="tpu_custom_call" | custom-call | flops 8000000000 | bytes 4000000 | tf_op jit(solution)/shard_map/pallas_call | solution.py:649
  25.1 1.1 collective-permute-done.1.lo_ref
  26.1 4.1 %collective-permute-done.2.hi_ref = bf16[3,608,128]{2,1,0:T(8,128)(2,1)S(1)} collective-permute-done((bf16[3,608,128]{2,1,0:T(8,128)(2,1)S(1)}, bf16[3,608,128]{2,1,0:T(8,128)(2,1)S(1)}, u32[]{:S(2)}, u32[]{:S(2)}) %collective-permute-start.2) | collective-permute-done | bytes 466976 | tf_op jit(solution)/shard_map/ppermute | solution.py:647
  30.3 10.4 %shard_map.157 = (bf16[10,656,128]{2,1,0:T(8,128)(2,1)S(1)}, bf16[5,656,128]{2,1,0:T(8,128)(2,1)S(1)}, bf16[8,656,128]{2,1,0:T(8,128)(2,1)S(1)}, bf16[4,656,128]...) custom-call(f32[6400,128]{1,0:T(8,128)S(1)} %shard_map.153.splat_ref, ...), custom_call_target="tpu_custom_call" | custom-call | flops 14000000000 | bytes 4000000 | tf_op jit(solution)/shard_map/pallas_call | solution.py:664
  40.7 3.5 %collective-permute-start.6 = (bf16[4,560,128]{2,1,0:T(8,128)(2,1)S(1)}, bf16[4,560,128]{2,1,0:T(8,128)(2,1)S(1)}, u32[]{:S(2)}, u32[]{:S(2)}) collective-permute-start(bf16[4,560,128]{2,1,0:T(8,128)(2,1)S(1)} %get-tuple-element.55), channel_id=1, source_target_pairs={{0,2},{1,3},{2,4},{3,5},{4,6},{5,7},{8,10},{9,11},{10,12},{11,13},... | collective-permute-start | bytes 1720328 | tf_op jit(solution)/shard_map/ppermute | solution.py:680
  44.2 1.5 %collective-permute-start.7 = (bf16[4,560,128]{2,1,0:T(8,128)(2,1)S(1)}, bf16[4,560,128]{2,1,0:T(8,128)(2,1)S(1)}, u32[]{:S(2)}, u32[]{:S(2)}) collective-permute-start(bf16[4,560,128]{2,1,0:T(8,128)(2,1)S(1)} %get-tuple-element.56), channel_id=1, source_target_pairs={{2,0},{3,1},{4,2},{5,3},{6,4},{7,5},{10,8},{11,9},{12,10},{13,11},... | collective-permute-start | bytes 1720328 | tf_op jit(solution)/shard_map/ppermute | solution.py:681
  45.6 1.5 %collective-permute-start.3 = (f32[8,128]{1,0:T(8,128)S(1)}, f32[8,128]{1,0:T(8,128)S(1)}, u32[]{:S(2)}, u32[]{:S(2)}) collective-permute-start(f32[8,128]{1,0:T(8,128)S(1)} %get-tuple-element.47.mine_ref), channel_id=1, source_target_pairs={{0,1},{1,0},{2,3},{3,2},{4,5},{5,4},{6,7},{7,6},{8,9},{9,8},{10,11... | collective-permute-start | bytes 12296 | tf_op jit(solution)/shard_map/ppermute | solution.py:676
  47.2 2.1 %collective-permute-done.3 = f32[8,128]{1,0:T(8,128)S(1)} collective-permute-done((f32[8,128]{1,0:T(8,128)S(1)}, f32[8,128]{1,0:T(8,128)S(1)}, u32[]{:S(2)}, u32[]{:S(2)}) %collective-permute-start.3) | collective-permute-done | bytes 4128 | tf_op jit(solution)/shard_map/ppermute | solution.py:676
  49.3 2.6 %collective-permute-start.4 = (f32[8,128]{1,0:T(8,128)S(1)}, f32[8,128]{1,0:T(8,128)S(1)}, u32[]{:S(2)}, u32[]{:S(2)}) collective-permute-start(f32[8,128]{1,0:T(8,128)S(1)} %add.30), channel_id=1, source_target_pairs={{0,2},{1,3},{2,0},{3,1},{4,6},{5,7},{6,4},{7,5},{8,10},{9,11},{10,... | collective-permute-start | bytes 12296 | tf_op jit(solution)/shard_map/ppermute | solution.py:676
  52.6 6.0 %collective-permute-done.4 = f32[8,128]{1,0:T(8,128)S(1)} collective-permute-done((f32[8,128]{1,0:T(8,128)S(1)}, f32[8,128]{1,0:T(8,128)S(1)}, u32[]{:S(2)}, u32[]{:S(2)}) %collective-permute-start.4) | collective-permute-done | bytes 4128 | tf_op jit(solution)/shard_map/ppermute | solution.py:676
  58.6 1.3 %collective-permute-start.5 = (f32[8,128]{1,0:T(8,128)S(1)}, f32[8,128]{1,0:T(8,128)S(1)}, u32[]{:S(2)}, u32[]{:S(2)}) collective-permute-start(f32[8,128]{1,0:T(8,128)S(1)} %add.31), channel_id=1, source_target_pairs={{0,4},{1,5},{2,6},{3,7},{4,0},{5,1},{6,2},{7,3},{8,12},{9,13},{10,... | collective-permute-start | bytes 12296 | tf_op jit(solution)/shard_map/ppermute | solution.py:676
  59.9 2.0 %shard_map.158.gw2_ref = f32[9,32,128]{2,1,0:T(8,128)S(1)} custom-call(bf16[4,560,128]{2,1,0:T(8,128)(2,1)S(1)} %get-tuple-element.54.m3_ref, bf16[6,656,128]{2,1,0:T(8,128)(2,1)S(1)} %get-tuple-element.53.h2_ref, bf16[3,656,128]{2,1,0:T(8,128)(2,1)S(1)} %get-tuple-element.57.e2_ref), custom_call_target="tpu_custom_call" | custom-call | flops 3000000000 | bytes 4000000 | tf_op jit(solution)/shard_map/pallas_call | solution.py:683
  61.9 1.2 %collective-permute-done.5 = f32[8,128]{1,0:T(8,128)S(1)} collective-permute-done((f32[8,128]{1,0:T(8,128)S(1)}, f32[8,128]{1,0:T(8,128)S(1)}, u32[]{:S(2)}, u32[]{:S(2)}) %collective-permute-start.5) | collective-permute-done | bytes 4128 | tf_op jit(solution)/shard_map/ppermute | solution.py:676
  63.1 14.0 %shard_map.159 = (f32[384,128]{1,0:T(8,128)S(1)}, f32[384,128]{1,0:T(8,128)S(1)}, f32[1]{0:T(128)}, f32[1]{0:T(128)}, bf16[128,2048]{1,0:T(8,128)(2,1)S(1)}) custom-call(s32[1]{0:T(128)S(6)} %copy.30.label, f32[8,128]{1,0:T(8,128)S(1)} %add.32.pool_ref, f32[8,128]{1,0:T(8,128)S(1)} %get-tuple-element.47.mine_ref, ...), custom_call_target="tpu_custom_call" | custom-call | flops 14000000000 | bytes 4000000 | tf_op jit(solution)/shard_map/pallas_call | solution.py:696
  77.2 1.4 %collective-permute-done.8 = f32[384,128]{1,0:T(8,128)S(1)} collective-permute-done((f32[384,128]{1,0:T(8,128)S(1)}, f32[384,128]{1,0:T(8,128)S(1)}, u32[]{:S(2)}, u32[]{:S(2)}) %collective-permute-start.8) | collective-permute-done | bytes 196640 | tf_op jit(solution)/shard_map/ppermute | solution.py:716
  79.4 4.6 %all-to-all-start = ((f32[16,24,128]{2,1,0:T(8,128)}), f32[16,24,128]{2,1,0:T(8,128)S(1)}, u32[]{:S(2)}, u32[]{:S(2)}) async-start(f32[16,24,128]{2,1,0:T(8,128)} %bitcast.8), calls=%async_computation | async-start | bytes 393216 | tf_op jit(solution)/shard_map/all_to_all | solution.py:717
  83.9 7.3 %shard_map.160 = f32[3,2048]{1,0:T(4,128)S(1)} custom-call(s32[1]{0:T(128)S(6)} %copy.29.count, f32[28]{0:T(128)S(1)} %copy-done.2, f32[3,1,2048]{2,1,0:T(1,128)S(1)} %bitcast.31, s32[1,2048]{1,0:T(1,128)S(1)} %copy-done.1, bf16[128,2048]{1,0:T(8,128)(2,1)S(1)} %get-tuple-element.63.dk_ref), custom_call_target="tpu_custom_call" | custom-call | flops 10000000000 | bytes 4000000 | tf_op jit(solution)/shard_map/pallas_call | solution.py:718
  91.3 1.3 %all-to-all-done = f32[16,24,128]{2,1,0:T(8,128)S(1)} async-done(((f32[16,24,128]{2,1,0:T(8,128)}), f32[16,24,128]{2,1,0:T(8,128)S(1)}, u32[]{:S(2)}, u32[]{:S(2)}) %all-to-all-start) | async-done | bytes 196640 | tf_op jit(solution)/shard_map/all_to_all | solution.py:717
  92.7 13.6 %all_to_all.10 = f32[16,24,128]{2,1,0:T(8,128)S(1)} all-to-all(f32[16,24,128]{2,1,0:T(8,128)S(1)} %broadcast_in_dim.2), channel_id=1, replica_groups=mesh['y'=2,'core'=2,'slab'=8] {'y','slab'}, dimensions={0} | all-to-all | bytes 393216 | tf_op jit(solution)/shard_map/all_to_all | solution.py:731
  106.3 1.2 %collective-permute-start.10 = (f32[3,2048]{1,0:T(4,128)S(1)}, f32[3,2048]{1,0:T(4,128)S(1)}, u32[]{:S(2)}, u32[]{:S(2)}) collective-permute-start(f32[3,2048]{1,0:T(4,128)S(1)} %shard_map.160), channel_id=1, source_target_pairs={{0,1},{1,0},{2,3},{3,2},{4,5},{5,4},{6,7},{7,6},{8,9},{9,8},{10,11... | collective-permute-start | bytes 73736 | tf_op jit(solution)/shard_map/ppermute | solution.py:676
  107.5 2.7 %collective-permute-done.10 = f32[3,2048]{1,0:T(4,128)S(1)} collective-permute-done((f32[3,2048]{1,0:T(4,128)S(1)}, f32[3,2048]{1,0:T(4,128)S(1)}, u32[]{:S(2)}, u32[]{:S(2)}) %collective-permute-start.10) | collective-permute-done | bytes 24608 | tf_op jit(solution)/shard_map/ppermute | solution.py:676
  111.2 3.0 %collective-permute-done.11 = f32[3,2048]{1,0:T(4,128)S(1)} collective-permute-done((f32[3,2048]{1,0:T(4,128)S(1)}, f32[3,2048]{1,0:T(4,128)S(1)}, u32[]{:S(2)}, u32[]{:S(2)}) %collective-permute-start.11) | collective-permute-done | bytes 24608 | tf_op jit(solution)/shard_map/ppermute | solution.py:676
  114.2 1.1 collective-permute-start.12
  115.3 3.8 %collective-permute-done.12.fb_ref = f32[3,2048]{1,0:T(4,128)S(1)} collective-permute-done((f32[3,2048]{1,0:T(4,128)S(1)}, f32[3,2048]{1,0:T(4,128)S(1)}, u32[]{:S(2)}, u32[]{:S(2)}) %collective-permute-start.12) | collective-permute-done | bytes 24608 | tf_op jit(solution)/shard_map/ppermute | solution.py:736
  119.1 1.3 %shard_map.161 = (f32[27,32,28]{2,1,0:T(8,128)}, f32[27,32,32]{2,1,0:T(8,128)}, f32[27,32,32]{2,1,0:T(8,128)}, f32[1,32]{1,0:T(1,128)}, f32[3,1,2048]{2,1,0:T(1,128)}) custom-call(f32[384,128]{1,0:T(8,128)S(1)} %bitcast.28, f32[384,128]{1,0:T(8,128)S(1)} %collective-permute-done.9.other_ref, f32[3,2048]{1,0:T(4,128)S(1)} %add.35.fa_ref, ...), custom_call_target="tpu_custom_call" | custom-call | flops 100000000 | bytes 4000000 | tf_op jit(solution)/shard_map/pallas_call | solution.py:739
  (41 shorter events, 5.2 us)
Async XLA Ops:
  0.6 7.1 %copy-start.3 = (bf16[32,32,3,3,3]{1,0,4,3,2:T(8,128)(2,1)S(1)}, bf16[32,32,3,3,3]{1,0,4,3,2:T(8,128)(2,1)}, u32[]{:S(2)}) copy-start(bf16[32,32,3,3,3]{1,0,4,3,2:T(8,128)(2,1)} %param.17) | copy-start | bytes 165892
  0.6 7.6 %copy-start.4 = (bf16[32,32,3,3,3]{1,0,4,3,2:T(8,128)(2,1)S(1)}, bf16[32,32,3,3,3]{1,0,4,3,2:T(8,128)(2,1)}, u32[]{:S(2)}) copy-start(bf16[32,32,3,3,3]{1,0,4,3,2:T(8,128)(2,1)} %param.18) | copy-start | bytes 165892
  1.9 10.7 %collective-permute-start = (bf16[2,28,2560]{2,1,0:T(8,128)(2,1)S(1)}, bf16[2,28,2560]{2,1,0:T(8,128)(2,1)S(1)}, u32[]{:S(2)}, u32[]{:S(2)}) collective-permute-start(bf16[2,28,2560]{2,1,0:T(8,128)(2,1)S(1)} %bitcast.32), channel_id=1, source_target_pairs={{0,1},{1,0},{2,3},{3,2},{4,5},{5,4},{6,7},{7,6},{8,9},{9,8},{10,11... | collective-permute-start | bytes 860168 | tf_op jit(solution)/shard_map/ppermute | solution.py:620
  8.7 0.7 copy-start.5
  12.7 5.7 %copy-start = (f32[1,3,2048]{2,0,1:T(1,128)S(1)}, f32[1,3,2048]{2,0,1:T(1,128)}, u32[]{:S(2)}) copy-start(f32[1,3,2048]{2,0,1:T(1,128)} %param.10) | copy-start | bytes 73732
  12.7 5.7 %copy-start.1 = (s32[1,2048]{1,0:T(1,128)S(1)}, s32[1,2048]{1,0:T(1,128)}, u32[]{:S(2)}) copy-start(s32[1,2048]{1,0:T(1,128)} %types_ref.3) | copy-start | bytes 24580
  12.7 5.7 %copy-start.2 = (f32[28]{0:T(128)S(1)}, f32[28]{0:T(128)}, u32[]{:S(2)}) copy-start(f32[28]{0:T(128)} %radii.3) | copy-start | bytes 340
  13.3 12.8 %collective-permute-start.1 = (bf16[3,608,128]{2,1,0:T(8,128)(2,1)S(1)}, bf16[3,608,128]{2,1,0:T(8,128)(2,1)S(1)}, u32[]{:S(2)}, u32[]{:S(2)}) collective-permute-start(bf16[3,608,128]{2,1,0:T(8,128)(2,1)S(1)} %get-tuple-element.43), channel_id=1, source_target_pairs={{0,2},{1,3},{2,4},{3,5},{4,6},{5,7},{8,10},{9,11},{10,12},{11,13},... | collective-permute-start | bytes 1400840 | tf_op jit(solution)/shard_map/ppermute | solution.py:646
  17.1 13.2 %collective-permute-start.2 = (bf16[3,608,128]{2,1,0:T(8,128)(2,1)S(1)}, bf16[3,608,128]{2,1,0:T(8,128)(2,1)S(1)}, u32[]{:S(2)}, u32[]{:S(2)}) collective-permute-start(bf16[3,608,128]{2,1,0:T(8,128)(2,1)S(1)} %get-tuple-element.45), channel_id=1, source_target_pairs={{2,0},{3,1},{4,2},{5,3},{6,4},{7,5},{10,8},{11,9},{12,10},{13,11},... | collective-permute-start | bytes 1400840 | tf_op jit(solution)/shard_map/ppermute | solution.py:647
  40.7 22.4 %collective-permute-start.6 = (bf16[4,560,128]{2,1,0:T(8,128)(2,1)S(1)}, bf16[4,560,128]{2,1,0:T(8,128)(2,1)S(1)}, u32[]{:S(2)}, u32[]{:S(2)}) collective-permute-start(bf16[4,560,128]{2,1,0:T(8,128)(2,1)S(1)} %get-tuple-element.55), channel_id=1, source_target_pairs={{0,2},{1,3},{2,4},{3,5},{4,6},{5,7},{8,10},{9,11},{10,12},{11,13},... | collective-permute-start | bytes 1720328 | tf_op jit(solution)/shard_map/ppermute | solution.py:680
  44.2 18.9 %collective-permute-start.7 = (bf16[4,560,128]{2,1,0:T(8,128)(2,1)S(1)}, bf16[4,560,128]{2,1,0:T(8,128)(2,1)S(1)}, u32[]{:S(2)}, u32[]{:S(2)}) collective-permute-start(bf16[4,560,128]{2,1,0:T(8,128)(2,1)S(1)} %get-tuple-element.56), channel_id=1, source_target_pairs={{2,0},{3,1},{4,2},{5,3},{6,4},{7,5},{10,8},{11,9},{12,10},{13,11},... | collective-permute-start | bytes 1720328 | tf_op jit(solution)/shard_map/ppermute | solution.py:681
  45.6 3.7 %collective-permute-start.3 = (f32[8,128]{1,0:T(8,128)S(1)}, f32[8,128]{1,0:T(8,128)S(1)}, u32[]{:S(2)}, u32[]{:S(2)}) collective-permute-start(f32[8,128]{1,0:T(8,128)S(1)} %get-tuple-element.47.mine_ref), channel_id=1, source_target_pairs={{0,1},{1,0},{2,3},{3,2},{4,5},{5,4},{6,7},{7,6},{8,9},{9,8},{10,11... | collective-permute-start | bytes 12296 | tf_op jit(solution)/shard_map/ppermute | solution.py:676
  49.3 9.3 %collective-permute-start.4 = (f32[8,128]{1,0:T(8,128)S(1)}, f32[8,128]{1,0:T(8,128)S(1)}, u32[]{:S(2)}, u32[]{:S(2)}) collective-permute-start(f32[8,128]{1,0:T(8,128)S(1)} %add.30), channel_id=1, source_target_pairs={{0,2},{1,3},{2,0},{3,1},{4,6},{5,7},{6,4},{7,5},{8,10},{9,11},{10,... | collective-permute-start | bytes 12296 | tf_op jit(solution)/shard_map/ppermute | solution.py:676
  58.6 4.5 %collective-permute-start.5 = (f32[8,128]{1,0:T(8,128)S(1)}, f32[8,128]{1,0:T(8,128)S(1)}, u32[]{:S(2)}, u32[]{:S(2)}) collective-permute-start(f32[8,128]{1,0:T(8,128)S(1)} %add.31), channel_id=1, source_target_pairs={{0,4},{1,5},{2,6},{3,7},{4,0},{5,1},{6,2},{7,3},{8,12},{9,13},{10,... | collective-permute-start | bytes 12296 | tf_op jit(solution)/shard_map/ppermute | solution.py:676
  77.1 1.5 %collective-permute-start.8 = (f32[384,128]{1,0:T(8,128)S(1)}, f32[384,128]{1,0:T(8,128)S(1)}, u32[]{:S(2)}, u32[]{:S(2)}) collective-permute-start(f32[384,128]{1,0:T(8,128)S(1)} %get-tuple-element.62), channel_id=1, source_target_pairs={{0,8},{8,0},{1,9},{9,1},{2,10},{10,2},{3,11},{11,3},{4,12},{12,4},... | collective-permute-start | bytes 589832 | tf_op jit(solution)/shard_map/ppermute | solution.py:716
  79.4 13.3 %all-to-all-start = ((f32[16,24,128]{2,1,0:T(8,128)}), f32[16,24,128]{2,1,0:T(8,128)S(1)}, u32[]{:S(2)}, u32[]{:S(2)}) async-start(f32[16,24,128]{2,1,0:T(8,128)} %bitcast.8), calls=%async_computation | async-start | bytes 393216 | tf_op jit(solution)/shard_map/all_to_all | solution.py:717
  106.3 12.8 %collective-permute-start.9 = (f32[384,128]{1,0:T(8,128)S(1)}, f32[384,128]{1,0:T(8,128)S(1)}, u32[]{:S(2)}, u32[]{:S(2)}) collective-permute-start(f32[384,128]{1,0:T(8,128)S(1)} %bitcast.27), channel_id=1, source_target_pairs={{0,8},{8,0},{1,9},{9,1},{2,10},{10,2},{3,11},{11,3},{4,12},{12,4},... | collective-permute-start | bytes 589832 | tf_op jit(solution)/shard_map/ppermute | solution.py:733
  106.3 3.9 %collective-permute-start.10 = (f32[3,2048]{1,0:T(4,128)S(1)}, f32[3,2048]{1,0:T(4,128)S(1)}, u32[]{:S(2)}, u32[]{:S(2)}) collective-permute-start(f32[3,2048]{1,0:T(4,128)S(1)} %shard_map.160), channel_id=1, source_target_pairs={{0,1},{1,0},{2,3},{3,2},{4,5},{5,4},{6,7},{7,6},{8,9},{9,8},{10,11... | collective-permute-start | bytes 73736 | tf_op jit(solution)/shard_map/ppermute | solution.py:676
  110.2 4.0 %collective-permute-start.11 = (f32[3,2048]{1,0:T(4,128)S(1)}, f32[3,2048]{1,0:T(4,128)S(1)}, u32[]{:S(2)}, u32[]{:S(2)}) collective-permute-start(f32[3,2048]{1,0:T(4,128)S(1)} %add.34), channel_id=1, source_target_pairs={{0,2},{1,3},{2,0},{3,1},{4,6},{5,7},{6,4},{7,5},{8,10},{9,11},{10,... | collective-permute-start | bytes 73736 | tf_op jit(solution)/shard_map/ppermute | solution.py:676
  114.2 4.9 %collective-permute-start.12 = (f32[3,2048]{1,0:T(4,128)S(1)}, f32[3,2048]{1,0:T(4,128)S(1)}, u32[]{:S(2)}, u32[]{:S(2)}) collective-permute-start(f32[3,2048]{1,0:T(4,128)S(1)} %add.35.fa_ref), channel_id=1, source_target_pairs={{0,4},{1,5},{2,6},{3,7},{4,0},{5,1},{6,2},{7,3},{8,12},{9,13},{10,... | collective-permute-start | bytes 73736 | tf_op jit(solution)/shard_map/ppermute | solution.py:736

commit v3 on v2

--- a/solution.py
+++ b/solution.py
@@ -53,15 +53,16 @@
 
     def body(f, carry):
         fe = jnp.where(flip == 0, f, 2 - f)
+        at_f = pl.multiple_of(f * 768, 128)
         us = [u_ref[conv * 9 + e * 3 + fe] for e in range(3)]
         for jo in range(4):
             rows = [pl.ds(p * 128 + jo * 32, 32) for p in range(2)]
             for e in range(3):
                 main = spread(us[e], jo).astype(bf16)
                 for p in range(2):
-                    w_ref[f, rows[p], pl.ds((p + e) * 128, 128)] = main
-            w_ref[f, rows[0], pl.ds(3 * 128, 128)] = zero
-            w_ref[f, rows[1], pl.ds(0, 128)] = zero
+                    w_ref[rows[p], pl.ds(at_f + (p + e) * 128, 128)] = main
+            w_ref[rows[0], pl.ds(at_f + 3 * 128, 128)] = zero
+            w_ref[rows[1], pl.ds(at_f, 128)] = zero
             for p in range(2):
                 for half in range(2):
                     edge = zero
@@ -72,7 +73,7 @@
                                 at = 2 * (q % 2)
                                 parts.append(one_block(us[q - p], 0, at) if jo == 0 else one_block(us[q - p], 2, at + 1))
                         edge = functools.reduce(jnp.add, parts).astype(bf16)
-                    w_ref[f, rows[p], pl.ds(512 + half * 128, 128)] = edge
+                    w_ref[rows[p], pl.ds(at_f + 512 + half * 128, 128)] = edge
         return carry
 
     lax.fori_loop(0, 3, body, 0)
@@ -83,6 +84,7 @@
 
     def body(f, carry):
         fe = jnp.where(flip == 0, 2 - f, f)
+        at_f = pl.multiple_of(f * 768, 128)
         for e in range(3):
             u = u_ref[conv * 9 + (2 - e) * 3 + fe]
             tiles = [spread(u, jc).astype(bf16) for jc in range(4)]
@@ -92,12 +94,12 @@
                 lanes = pl.ds(p * 128, 128)
                 for jc in range(6):
                     at = q * 128 + jc * 32 if jc < 4 else 512 + q * 64 + (jc - 4) * 32
-                    w_ref[f, pl.ds(at, 32), lanes] = tiles[jc]
+                    w_ref[pl.ds(at_f + at, 32), lanes] = tiles[jc]
         for p, q in ((0, 3), (1, 0)):
             lanes = pl.ds(p * 128, 128)
             for jc in range(6):
                 at = q * 128 + jc * 32 if jc < 4 else 512 + q * 64 + (jc - 4) * 32
-                w_ref[f, pl.ds(at, 32), lanes] = zero
+                w_ref[pl.ds(at_f + at, 32), lanes] = zero
         return carry
 
     lax.fori_loop(0, 3, body, 0)
@@ -122,12 +124,8 @@
 
 def conv_pair(x_ref, e_ref, plane, pair, rows, w_ref, acc_ref, dims):
     n = rows * JB
-    total = None
-    for f in range(3):
-        lhs = jnp.concatenate(patch(x_ref, e_ref, plane, pair, f, n), axis=1)
-        part = dotf(lhs, w_ref[f], dims)
-        total = part if total is None else total + part
-    acc_ref[pl.ds(0, n), :] = total
+    lhs = jnp.concatenate([p for f in range(3) for p in patch(x_ref, e_ref, plane, pair, f, n)], axis=1)
+    acc_ref[pl.ds(0, n), :] = dotf(lhs, w_ref[...], dims)
 
 
 def put_pair(main_ref, e_ref, plane, pair, at, va, vb):
@@ -179,33 +177,41 @@
     return source
 
 
-def pack_own_kernel(raw_ref, out_ref, wide_ref):
+def pack_own_kernel(raw_ref, low_ref, high_ref, wide_ref):
     h = place()[1]
     base = pl.multiple_of(jnp.where(h == 0, 0, NXY * NXY - WIN), 256)
 
     def put(p, sl, val):
-        out_ref[p, sl, :] = val
+        (low_ref, high_ref)[p][sl, :] = val
 
     pack_planes(h, widen(raw_ref, wide_ref, pl.ds(base, WIN)), put)
 
 
-def pack_kernel(raw_ref, mine_ref, own_ref, up_ref, dn_ref, wide_ref):
+def pack_kernel(raw_ref, low_ref, high_ref, own_ref, up_ref, dn_ref, wide_ref):
     h = place()[1]
 
     def put(p, sl, val):
         own_ref[2 * (1 - h) + p, sl, :] = val
 
     pack_planes(h, widen(raw_ref, wide_ref, pl.ds(0, WIN)), put)
-    for p in range(2):
-        own_ref[2 * h + p] = mine_ref[p]
-    for k in range(3):
-        up_ref[k] = own_ref[k + 1]
-        dn_ref[k] = own_ref[k]
-
-
-def weights_kernel(u_ref, wf_ref, wb_ref):
+    own_ref[2 * h] = low_ref[...]
+    own_ref[2 * h + 1] = high_ref[...]
+    for k in range(2):
+        up_ref[k] = own_ref[2 - h + k]
+        dn_ref[k] = own_ref[1 - h + k]
+
+
+def weights_kernel(stem_ref, one_ref, two_ref, wf_ref, wb_ref, u_ref):
     flip = place()[1]
-    for conv in range(3):
+    for conv, ref in enumerate((stem_ref, one_ref, two_ref)):
+        channels = ref.shape[2]
+        blank = jnp.zeros((32, 128 - channels), f32)
+        for k in range(9):
+            tile = jnp.zeros((32, 128), f32)
+            for g in range(3):
+                block = jnp.concatenate([ref[3 * k + g].astype(f32), blank], axis=1)
+                tile = tile + (pltpu.roll(block, 32 * g, 1) if g else block)
+            u_ref[conv * 9 + k] = tile
         build_forward(u_ref, conv, flip, wf_ref.at[conv])
         build_backward(u_ref, conv, flip, wb_ref.at[conv])
 
@@ -259,11 +265,16 @@
 
 
 def forward_kernel(
-    depth, splat_ref, lo_ref, own_ref, hi_ref, w_ref,
-    x_ref, ex_ref, h1_ref, e1_ref, h2_ref, e2_ref, m3_ref, up_ref, dn_ref, pool_ref,
-    acc_ref,
+    depth, splat_ref, lo_one, lo_two, own_ref, hi_one, hi_two, w_ref,
+    x_ref, ex_ref, h1_ref, h2_ref, e2_ref, m3_ref, up_ref, dn_ref, pool_ref,
+    accs_ref, rim_ref, e1_ref,
 ):
-    first = 4 * place()[0] - 3
+    group, half = place()
+    first = 4 * group - 3
+    for k, (one, two) in enumerate(((lo_one, lo_two), (hi_one, hi_two))):
+        rim_ref[k, 2 * half] = one[...]
+        rim_ref[k, 1 - half] = two[0]
+        rim_ref[k, 2 - half] = two[1]
     for ref in (x_ref, ex_ref, h1_ref, e1_ref, h2_ref, e2_ref):
         clear_pad(ref)
 
@@ -273,10 +284,10 @@
 
     def receptor(q, sl):
         if q < 3:
-            return lo_ref[q, sl, :]
+            return rim_ref[0, q, sl, :]
         if q < 7:
             return own_ref[q - 3, sl, :]
-        return hi_ref[q - 7, sl, :]
+        return rim_ref[1, q - 7, sl, :]
 
     for m in range(5):
         def density(c, carry):
@@ -293,6 +304,7 @@
 
 
     def stem(m, carry):
+        acc_ref = accs_ref.at[m % 2]
         conv_pair(x_ref, ex_ref, 2 * m, m, RS, w_ref.at[0], acc_ref, NT)
         ia, ib = inside(2 * m + 1), inside(2 * m + 2)
         for c in range(NCH):
@@ -300,9 +312,11 @@
             put_pair(h1_ref, e1_ref, 2 * m, m, JB + c * CH, rounded(acc[:, :128] * ia), rounded(acc[:, 128:] * ib))
         return carry
 
-    lax.fori_loop(0, 4, stem, 0)
+    for m in range(4):
+        stem(m, 0)
 
     def second(m, carry):
+        acc_ref = accs_ref.at[m % 2]
         conv_pair(h1_ref, e1_ref, 2 * m, m, R2, w_ref.at[1], acc_ref, NT)
         ia, ib = inside(2 * m + 2), inside(2 * m + 3)
         for c in range(NCH):
@@ -310,9 +324,11 @@
             put_pair(h2_ref, e2_ref, 2 * m, m, JB + c * CH, rounded(acc[:, :128] * ia), rounded(acc[:, 128:] * ib))
         return carry
 
-    lax.fori_loop(0, 3, second, 0)
+    for m in range(3):
+        second(m, 0)
 
     def third(m, pool):
+        acc_ref = accs_ref.at[m % 2]
         conv_pair(h2_ref, e2_ref, 2 * m, m, R3, w_ref.at[2], acc_ref, NT)
         for c in range(7):
             sl = pl.ds(c * 80, 80)
@@ -328,7 +344,9 @@
                 m3_ref[2 * m + k, sl, :] = jnp.where(summed > 0.0, 1.0, 0.0).astype(bf16)
         return pool
 
-    pool = lax.fori_loop(0, 2, third, jnp.zeros((1, 128), f32))
+    pool = jnp.zeros((1, 128), f32)
+    for m in range(2):
+        pool = third(m, pool)
     pool = pool + pltpu.roll(pool, 64, 1)
     pool = pool + pltpu.roll(pool, 32, 1)
     pool_ref[...] = jnp.broadcast_to(pool, pool_ref.shape)
@@ -378,8 +396,14 @@
     lax.fori_loop(0, 3, body, 0)
 
 
-def prepare_kernel(m3_ref, h2_ref, e2_ref, gw_ref, g_ref):
+def prepare_kernel(m3_ref, h2_ref, e2_ref, h1_ref, gw_ref, e1_ref, g_ref):
     flip = place()[1]
+    clear_pad(e1_ref)
+    for m in range(3):
+        for c in range(5):
+            sl = pl.ds(JB + c * CH, CH)
+            sides = [h1_ref[2 * m + 1 + k, sl, :].astype(f32) for k in range(2)]
+            e1_ref[m, sl, :] = edges(*sides).astype(bf16)
     rows = pl.ds(0, OWN * JB)
     for m in range(2):
         grads = jnp.concatenate([m3_ref[2 * m, rows, :], m3_ref[2 * m + 1, rows, :]], axis=1)
@@ -392,15 +416,16 @@
 
 
 def backward_kernel(
-    depth, label, pool_ref, mine_ref, head_ref,
-    x_ref, ex_ref, h1_ref, e1_ref, h2_ref, m3_ref, lo_ref, hi_ref, gw2_ref, w_ref,
-    keep_ref, give_ref, score_ref, loss_ref, dk_ref,
-    t_ref, et_ref, mg_ref, em_ref, sg_ref, es_ref, hm_ref, acc_ref, g_ref, flat_ref, dg_ref,
+    depth, terms, label, *refs,
 ):
+    pool_refs, refs = refs[:terms], refs[terms:]
+    mine_ref, head_ref, x_ref, ex_ref, h1_ref, e1_ref, h2_ref, m3_ref, lo_ref, hi_ref, gw2_ref, w_ref = refs[:12]
+    keep_ref, give_ref, score_ref, loss_ref, dk_ref = refs[12:17]
+    t_ref, et_ref, mg_ref, em_ref, sg_ref, es_ref, hm_ref, accs_ref, g_ref, flat_ref, dg_ref = refs[17:]
     flip = place()[1]
     scale = 1.0 / (depth * NXY * NXY)
     head = head_ref[...]
-    pooled = pool_ref[0:1, :] * scale
+    pooled = terms_sum([ref[0:1, :] for ref in pool_refs]) * scale
     lane = lax.broadcasted_iota(jnp.int32, (1, 128), 1)
     score = jnp.sum(jnp.where(lane < 32, pooled * head, 0.0), axis=1, keepdims=True)
     sign = (2 * label[0] - 1).astype(f32)
@@ -449,6 +474,7 @@
     own_rows = pl.ds(JB, OWN * JB)
 
     def mid(m, carry):
+        acc_ref = accs_ref.at[m % 2]
         conv_pair(t_ref, et_ref, 2 * m, m, RM, w_ref.at[2], acc_ref, NN)
         for c in range(NCH):
             sl = pl.ds(c * 112, 112)
@@ -459,19 +485,16 @@
             put_pair(mg_ref, em_ref, 2 * m, m, JB + c * 112, *vals)
         return carry
 
-    lax.fori_loop(0, 4, mid, 0)
-
-    for m in range(3):
-        ga = mg_ref[1 + 2 * m, own_rows, :]
-        gb = mg_ref[2 + 2 * m, own_rows, :]
-        if m == 0:
-            ga = jnp.zeros_like(ga)
-        if m == 2:
-            gb = jnp.zeros_like(gb)
-        weight_grad(h1_ref, e1_ref, 2 * m, m, jnp.concatenate([ga, gb], axis=1), g_ref, m == 0)
+    for m in range(4):
+        mid(m, 0)
+
+    for m in range(2):
+        grads = jnp.concatenate([mg_ref[2 + 2 * m, own_rows, :], mg_ref[3 + 2 * m, own_rows, :]], axis=1)
+        weight_grad(h1_ref, e1_ref, 1 + 2 * m, m, grads, g_ref, m == 0)
     extract(g_ref, flip, scale, put_rows(1))
 
     def low(m, carry):
+        acc_ref = accs_ref.at[m % 2]
         conv_pair(mg_ref, em_ref, 2 * m, m, RG, w_ref.at[1], acc_ref, NN)
         for c in range(NCH):
             sl = pl.ds(c * 112, 112)
@@ -483,7 +506,8 @@
             put_pair(sg_ref, es_ref, 2 * m, m, JB + c * 112, *vals)
         return carry
 
-    lax.fori_loop(0, 3, low, 0)
+    for m in range(3):
+        low(m, 0)
 
     for m in range(2):
         grads = jnp.concatenate([sg_ref[1 + 2 * m, own_rows, :], sg_ref[2 + 2 * m, own_rows, :]], axis=1)
@@ -494,13 +518,15 @@
     give_ref[...] = flat_ref[pl.ds(pl.multiple_of((1 - core) * half_rows, 16), half_rows), :]
 
     def last(m, carry):
+        acc_ref = accs_ref.at[m % 2]
         conv_pair(sg_ref, es_ref, 2 * m, m, OWN, w_ref.at[0], acc_ref, NN)
         for k in range(2):
             at = pl.ds(pl.multiple_of((2 * m + k) * OWN * JB, 16), OWN * JB)
             dg_ref[at, :] = rounded(acc_ref[pl.ds(0, OWN * JB), pl.ds(128 * k, 128)])
         return carry
 
-    lax.fori_loop(0, 2, last, 0)
+    for m in range(2):
+        last(m, 0)
     for jb in range(JB):
         dk_ref[:, pl.ds(jb * 128, 128)] = dg_ref[pl.ds(jb, 4 * OWN, stride=JB), :].astype(bf16)
 
@@ -550,6 +576,13 @@
         force_ref[2:3, sl] = fz
 
 
+def terms_sum(terms):
+    if len(terms) == 1:
+        return terms[0]
+    half = len(terms) // 2
+    return terms_sum([a + b for a, b in zip(terms[:half], terms[half:])])
+
+
 def place():
     s = lax.axis_index("slab")
     return s // 2, s % 2
@@ -563,14 +596,7 @@
     return pl.BlockSpec(memory_space=pltpu.VMEM)
 
 
-def lane_rows(w):
-    o, c = w.shape[:2]
-    moved = jnp.transpose(w, (2, 3, 0, 4, 1)).astype(f32)
-    moved = jnp.pad(moved, ((0, 0), (0, 0), (0, 0), (0, 1), (0, 32 - c)))
-    return moved.reshape(9, o, 128)
-
-
-def finish_kernel(mine_ref, other_ref, fa_ref, fb_ref, stem_ref, one_ref, two_ref, head_ref, force_ref, both_ref):
+def finish_kernel(mine_ref, other_ref, sum_ref, stem_ref, one_ref, two_ref, head_ref, force_ref, both_ref):
     core = lax.axis_index("core")
     both_ref[core] = mine_ref[...]
     both_ref[1 - core] = other_ref[...]
@@ -592,9 +618,8 @@
             val = pltpu.roll(block, 128 - 32 * at, 1) if at else block
             ref[3 * k + g] = val[:, : ref.shape[2]]
     head_ref[...] = both_ref[672 // half_rows, pl.ds(672 % half_rows, 8), :][:1, :32]
-    total = fa_ref[...] + fb_ref[...]
     for k in range(3):
-        force_ref[k] = total[k : k + 1, :]
+        force_ref[k] = sum_ref[k : k + 1, :]
 
 
 def call(kernel, limit, flops, **kwargs):
@@ -618,33 +643,36 @@
     raw = jnp.transpose(receptor[0], (1, 0, 2))
     theirs = lax.dynamic_slice_in_dim(raw, jnp.where(half == 1, 0, NXY * NXY - WIN), WIN, 2)
     other = lax.ppermute(theirs, "slab", [(i, i ^ 1) for i in range(slab_count)])
-    mine = call(
+    low, high = call(
         pack_own_kernel, 6, 2e9,
-        out_shape=jax.ShapeDtypeStruct((2,) + bh, bf16),
+        out_shape=[jax.ShapeDtypeStruct(bh, bf16)] * 2,
         in_specs=[vmem()],
-        out_specs=vmem(),
+        out_specs=[vmem()] * 2,
         scratch_shapes=[pltpu.VMEM((2, 32, WIN), bf16)],
     )(raw)
-    u = jnp.concatenate([lane_rows(w_stem), lane_rows(w_one), lane_rows(w_two)], axis=0)
+    offsets = lambda w: jnp.transpose(w, (2, 3, 4, 0, 1)).reshape(27, 32, w.shape[1])
     head = jnp.tile(w_head, 4)[None, :]
+    ups = [(i, i + 2) for i in range(slab_count - 2)]
+    downs = [(i + 2, i) for i in range(slab_count - 2)]
+    lo_one = lax.ppermute(high, "slab", ups)
+    hi_one = lax.ppermute(low, "slab", downs)
     wf, wb = call(
         weights_kernel, 6, 3e9,
-        out_shape=[jax.ShapeDtypeStruct((3, 3, 256, 768), bf16), jax.ShapeDtypeStruct((3, 3, 768, 256), bf16)],
-        in_specs=[vmem()],
+        out_shape=[jax.ShapeDtypeStruct((3, 256, 2304), bf16), jax.ShapeDtypeStruct((3, 2304, 256), bf16)],
+        in_specs=[vmem()] * 3,
         out_specs=[vmem()] * 2,
-    )(u)
-    other, mine, wf, wb, head = lax.optimization_barrier((other, mine, wf, wb, head))
+        scratch_shapes=[pltpu.VMEM((27, 32, 128), f32)],
+    )(offsets(w_stem), offsets(w_one), offsets(w_two))
+    other, wf, wb, head = lax.optimization_barrier((other, wf, wb, head))
     own, own_up, own_dn = call(
         pack_kernel, 6, 2e9,
-        out_shape=[jax.ShapeDtypeStruct((n,) + bh, bf16) for n in (4, 3, 3)],
-        in_specs=[vmem(), vmem()],
+        out_shape=[jax.ShapeDtypeStruct((n,) + bh, bf16) for n in (4, 2, 2)],
+        in_specs=[vmem()] * 3,
         out_specs=[vmem()] * 3,
         scratch_shapes=[pltpu.VMEM((2, 32, WIN), bf16)],
-    )(other, mine)
-    ups = [(i, i + 2) for i in range(slab_count - 2)]
-    downs = [(i + 2, i) for i in range(slab_count - 2)]
-    lo = lax.ppermute(own_up, "slab", ups)
-    hi = lax.ppermute(own_dn, "slab", downs)
+    )(other, low, high)
+    lo_two = lax.ppermute(own_up, "slab", ups)
+    hi_two = lax.ppermute(own_dn, "slab", downs)
 
     splat = call(
         functools.partial(splat_kernel, depth), 10, 8e9,
@@ -661,32 +689,39 @@
 
     big = lambda n: jax.ShapeDtypeStruct((n, BR, 128), bf16)
     thin = lambda n: jax.ShapeDtypeStruct((n, R3 * JB, 128), bf16)
-    x, ex, h1, e1, h2, e2, m3, up, dn, pool = call(
+    x, ex, h1, h2, e2, m3, up, dn, pool = call(
         functools.partial(forward_kernel, depth), 8, 1.4e10,
-        out_shape=[big(10), big(5), big(8), big(4), big(6), big(3), thin(4), thin(4), thin(4),
+        out_shape=[big(10), big(5), big(8), big(6), big(3), thin(4), thin(4), thin(4),
                    jax.ShapeDtypeStruct((8, 128), f32)],
-        in_specs=[vmem()] * 5,
-        out_specs=[vmem()] * 10,
-        scratch_shapes=[pltpu.VMEM((BR, 256), f32)],
-    )(splat, lo, own, hi, wf)
-
-    def over_slab(value, rounds):
-        step = 1
-        while step < rounds:
-            value = value + lax.ppermute(value, "slab", [(i, i ^ step) for i in range(slab_count)])
-            step *= 2
-        return value
+        in_specs=[vmem()] * 7,
+        out_specs=[vmem()] * 9,
+        scratch_shapes=[
+            pltpu.VMEM((2, BR, 256), f32), pltpu.VMEM((2, 3) + bh, bf16), pltpu.VMEM((4, BR, 128), bf16),
+        ],
+    )(splat, lo_one, lo_two, own, hi_one, hi_two, wf)
+
+    def swapped(value, bits):
+        return lax.ppermute(value, "slab", [(i, i ^ bits) for i in range(slab_count)])
+
+    def slab_terms(value):
+        other = swapped(value, 1)
+        value = value + other
+        bits = 2
+        while slab_count // bits > 4:
+            value = value + swapped(value, bits)
+            bits *= 2
+        return [value] + [swapped(value, k) for k in range(bits, slab_count, bits)]
 
     from_lo = lax.ppermute(up, "slab", ups)
     from_hi = lax.ppermute(dn, "slab", downs)
-    pool_sum = over_slab(pool, slab_count)
-    gw2 = call(
+    pools = slab_terms(pool)
+    gw2, e1 = call(
         prepare_kernel, 8, 3e9,
-        out_shape=jax.ShapeDtypeStruct((9, 32, 128), f32),
-        in_specs=[vmem()] * 3,
-        out_specs=vmem(),
+        out_shape=[jax.ShapeDtypeStruct((9, 32, 128), f32), big(3)],
+        in_specs=[vmem()] * 4,
+        out_specs=[vmem()] * 2,
         scratch_shapes=[pltpu.VMEM((3, 256, 768), f32)],
-    )(m3, h2, e2)
+    )(m3, h2, e2, h1)
 
     ranks = y_count * slab_count
     each = -(-680 // (2 * ranks))
@@ -694,23 +729,23 @@
         each = -(-each // 8) * 8
     half_rows = each * ranks
     keep, give, scores, pose_loss, dk = call(
-        functools.partial(backward_kernel, depth), 18, 1.4e10,
+        functools.partial(backward_kernel, depth, len(pools)), 18, 1.4e10,
         out_shape=[
             jax.ShapeDtypeStruct((half_rows, 128), f32), jax.ShapeDtypeStruct((half_rows, 128), f32),
             jax.ShapeDtypeStruct((1,), f32), jax.ShapeDtypeStruct((1,), f32),
             jax.ShapeDtypeStruct((4 * OWN, 2048), bf16),
         ],
-        in_specs=[smem()] + [vmem()] * 13,
+        in_specs=[smem()] + [vmem()] * (12 + len(pools)),
         out_specs=[vmem(), vmem(), smem(), smem(), vmem()],
         scratch_shapes=[
             pltpu.VMEM((10, BR, 128), bf16), pltpu.VMEM((5, BR, 128), bf16),
             pltpu.VMEM((8, BR, 128), bf16), pltpu.VMEM((4, BR, 128), bf16),
             pltpu.VMEM((6, BR, 128), bf16), pltpu.VMEM((3, BR, 128), bf16),
             pltpu.VMEM((8, R3 * JB, 128), bf16),
-            pltpu.VMEM((BR, 256), f32), pltpu.VMEM((3, 256, 768), f32),
+            pltpu.VMEM((2, BR, 256), f32), pltpu.VMEM((3, 256, 768), f32),
             pltpu.VMEM((2 * half_rows, 128), f32), pltpu.VMEM((4 * OWN * JB, 128), f32),
         ],
-    )(labels, pool_sum, pool, head, x, ex, h1, e1, h2, m3, from_lo, from_hi, gw2, wb)
+    )(labels, *pools, pool, head, x, ex, h1, e1, h2, m3, from_lo, from_hi, gw2, wb)
 
     swap = [(0, 1), (1, 0)]
     chip = keep + lax.ppermute(give, "core", swap)
@@ -731,19 +766,18 @@
     gathered = lax.all_to_all(spread_total, ("y", "slab"), 0, 0)
     gathered = gathered.reshape(half_rows, 128)
     gathered_other = lax.ppermute(gathered, "core", swap)
-    last_step = slab_count // 2
-    force = over_slab(force, last_step)
-    force_other = lax.ppermute(force, "slab", [(i, i ^ last_step) for i in range(slab_count)])
+    forces = slab_terms(force)
+    force = terms_sum(forces)
 
     grid = lambda c: jax.ShapeDtypeStruct((27, 32, c), f32)
     stem, one, two, grad_head, atom_grad = call(
         finish_kernel, 6, 1e8,
         out_shape=[grid(w_stem.shape[1]), grid(32), grid(32), jax.ShapeDtypeStruct((1, 32), f32),
                    jax.ShapeDtypeStruct((3, 1, atoms), f32)],
-        in_specs=[vmem()] * 4,
+        in_specs=[vmem()] * 3,
         out_specs=[vmem()] * 5,
         scratch_shapes=[pltpu.VMEM((2, half_rows, 128), f32)],
-    )(gathered, gathered_other, force, force_other)
+    )(gathered, gathered_other, force)
     shaped = lambda v: v.reshape(3, 3, 3, 32, v.shape[2]).transpose(3, 4, 0, 1, 2)
     return (scores, pose_loss, atom_grad.reshape(1, 3, atoms), shaped(stem), shaped(one), shaped(two),
             grad_head.reshape(32))

time: 121 us -> 108 us (0.89)
  starting transfers between devices: 26.5 us -> 42 us
  blocking collectives: 13.6 us -> 0 us
  waiting for transfers between devices: 27.3 us -> 16.5 us
  local copies, waits for them, and re-layouts: 5.13 us -> 3.3 us
  Pallas kernels: 44.8 us -> 43.1 us
    all_to_all x1 -> x0, blocking collectives: 13.6 us -> none  [local(): gathered = lax.all_to_all(spread_total, ('y', 'slab'), 0, 0)]
    ppermute x8 -> x12, waiting for transfers between devices: 24 us -> 13.7 us  [the longest x8 11.8 us: swapped(): lax.ppermute(value, 'slab', [(i, i ^ bits) for i in range(slab_count)])]
    ppermute x8 -> x12, starting transfers between devices: 13.9 us -> 22 us  [the longest x8 11.4 us: swapped(): lax.ppermute(value, 'slab', [(i, i ^ bits) for i in range(slab_count)])]
    all_to_all x0 -> x1, starting transfers between devices: none -> 5.59 us  [local(): gathered = lax.all_to_all(spread_total, ('y', 'slab'), 0, 0)]
    pallas_call x3, Pallas kernels: 16.5 us -> 14.7 us  [the longest x1 12 us: local(): call(functools.partial(backward_kernel, depth, len(pools)), 18, 140000000...]
    unnamed x16 -> x15, local copies, waits for them, and re-layouts: 2.76 us -> 1.32 us
    ppermute x1, starting transfers between devices: 3.49 us -> 4.76 us  [local(): from_lo = lax.ppermute(up, 'slab', ups)]
  transfers between devices with their start and end apart: 14 -> 19, of which waited for: 11 -> 9; matrix products, arithmetic and copies ran while one was open for 3% -> 1% of each run, Pallas kernels for 15% -> 18%
where the time goes in v3:
time: 108 us
  Pallas kernels  43.1 us (40%)
  starting transfers between devices  42 us (39%)
  waiting for transfers between devices  16.5 us (15%)
  local copies, waits for them, and re-layouts  3.3 us (3%)
  between operations  2.28 us (2%)
    pallas_call x1, Pallas kernels, local(): call(functools.partial(backward_kernel, depth, len(pools)), 18, 140000000...  12 us
    ppermute x8, waiting for transfers between devices, swapped(): lax.ppermute(value, 'slab', [(i, i ^ bits) for i in range(slab_count)])  11.8 us
    ppermute x8, starting transfers between devices, swapped(): lax.ppermute(value, 'slab', [(i, i ^ bits) for i in range(slab_count)])  11.4 us
    pallas_call x1, Pallas kernels, local(): call(functools.partial(forward_kernel, depth), 8, 14000000000.0, out_shap...  9.95 us
    pallas_call x1, Pallas kernels, local(): call(functools.partial(atom_kernel, depth), 12, 10000000000.0, out_shape=...  7.35 us
    pallas_call x1, Pallas kernels, local(): call(functools.partial(splat_kernel, depth), 10, 8000000000.0, out_shape=...  6.64 us
    all_to_all x1, starting transfers between devices, local(): gathered = lax.all_to_all(spread_total, ('y', 'slab'), 0, 0)  5.59 us
    all_to_all x1, starting transfers between devices, local(): got = lax.all_to_all(chip.reshape(ranks, each, 128), ('y', 'slab'), 0, 0)  5.23 us
  transfers between devices with their start and end apart: 19, of which 9 were waited for; matrix products, arithmetic and copies ran while one was open for 1% of the time, Pallas kernels for 18%

profile of v3, /device:TPU:0, one launch (start us, length us, event | category | flops | bytes accessed | tf_op | source)
XLA Modules:
  0.0 107.9 jit_solution(17402197655520978372)
XLA Ops:
  0.6 1.2 %constant_dynamic-slice_fusion = bf16[1,28,2,2560]{3,2,1,0:T(2,128)(2,1)S(1)} fusion(bf16[1,28,2,4096]{3,2,1,0:T(2,128)(2,1)} %param.14, s32[]{:T(128)S(6)} %select_n.13), kind=kLoop, calls=%fused_computation.3 | loop fusion | bytes 573444 | tf_op jit(solution)/shard_map/dynamic-slice.1
  1.9 3.0 %collective-permute-start.1 = (bf16[2,28,2560]{2,1,0:T(8,128)(2,1)S(1)}, bf16[2,28,2560]{2,1,0:T(8,128)(2,1)S(1)}, u32[]{:S(2)}, u32[]{:S(2)}) collective-permute-start(bf16[2,28,2560]{2,1,0:T(8,128)(2,1)S(1)} %bitcast.41), channel_id=1, source_target_pairs={{0,1},{1,0},{2,3},{3,2},{4,5},{5,4},{6,7},{7,6},{8,9},{9,8},{10,11... | collective-permute-start | bytes 860168 | tf_op jit(solution)/shard_map/ppermute | solution.py:645
  4.9 1.3 %copy.21 = bf16[1,28,2,4096]{3,1,2,0:T(8,128)(2,1)S(1)} copy(bf16[1,28,2,4096]{3,2,1,0:T(2,128)(2,1)} %param.14) | data formatting | bytes 917504 | tf_op args[4]
  6.8 3.5 %collective-permute-start = (bf16[608,128]{1,0:T(8,128)(2,1)S(1)}, bf16[608,128]{1,0:T(8,128)(2,1)S(1)}, u32[]{:S(2)}, u32[]{:S(2)}) collective-permute-start(bf16[608,128]{1,0:T(8,128)(2,1)S(1)} %get-tuple-element.41.high_ref), channel_id=1, source_target_pairs={{0,2},{1,3},{2,4},{3,5},{4,6},{5,7},{8,10},{9,11},{10,12},{11,13},... | collective-permute-start | bytes 466952 | tf_op jit(solution)/shard_map/ppermute | solution.py:657
  10.3 1.3 %collective-permute-start.3 = (bf16[608,128]{1,0:T(8,128)(2,1)S(1)}, bf16[608,128]{1,0:T(8,128)(2,1)S(1)}, u32[]{:S(2)}, u32[]{:S(2)}) collective-permute-start(bf16[608,128]{1,0:T(8,128)(2,1)S(1)} %get-tuple-element.45.low_ref), channel_id=1, source_target_pairs={{2,0},{3,1},{4,2},{5,3},{6,4},{7,5},{10,8},{11,9},{12,10},{13,11},... | collective-permute-start | bytes 466952 | tf_op jit(solution)/shard_map/ppermute | solution.py:658
  12.3 2.6 %shard_map.155 = (bf16[3,256,2304]{2,1,0:T(8,128)(2,1)S(1)}, bf16[3,2304,256]{2,1,0:T(8,128)(2,1)S(1)}) custom-call(bf16[27,32,28]{2,1,0:T(8,128)(2,1)S(1)} %bitcast.36, bf16[27,32,32]{2,1,0:T(8,128)(2,1)S(1)} %bitcast.37, bf16[27,32,32]{2,1,0:T(8,128)(2,1)S(1)} %bitcast.38), custom_call_target="tpu_custom_call" | custom-call | flops 3000000000 | bytes 4000000 | tf_op jit(solution)/shard_map/pallas_call | solution.py:659
  15.6 4.6 %collective-permute-start.2 = (bf16[2,608,128]{2,1,0:T(8,128)(2,1)S(1)}, bf16[2,608,128]{2,1,0:T(8,128)(2,1)S(1)}, u32[]{:S(2)}, u32[]{:S(2)}) collective-permute-start(bf16[2,608,128]{2,1,0:T(8,128)(2,1)S(1)} %get-tuple-element.46), channel_id=1, source_target_pairs={{0,2},{1,3},{2,4},{3,5},{4,6},{5,7},{8,10},{9,11},{10,12},{11,13},... | collective-permute-start | bytes 933896 | tf_op jit(solution)/shard_map/ppermute | solution.py:674
  20.2 1.3 %collective-permute-start.4 = (bf16[2,608,128]{2,1,0:T(8,128)(2,1)S(1)}, bf16[2,608,128]{2,1,0:T(8,128)(2,1)S(1)}, u32[]{:S(2)}, u32[]{:S(2)}) collective-permute-start(bf16[2,608,128]{2,1,0:T(8,128)(2,1)S(1)} %get-tuple-element.48), channel_id=1, source_target_pairs={{2,0},{3,1},{4,2},{5,3},{6,4},{7,5},{10,8},{11,9},{12,10},{13,11},... | collective-permute-start | bytes 933896 | tf_op jit(solution)/shard_map/ppermute | solution.py:675
  21.5 6.6 %shard_map.153.splat_ref = f32[6400,128]{1,0:T(8,128)S(1)} custom-call(s32[1]{0:T(128)S(6)} %copy.23.count, f32[28]{0:T(128)S(1)} %copy-done.5, f32[3,1,2048]{2,1,0:T(1,128)S(1)} %bitcast.39, s32[1,2048]{1,0:T(1,128)S(1)} %copy-done.4), custom_call_target="tpu_custom_call" | custom-call | flops 8000000000 | bytes 4000000 | tf_op jit(solution)/shard_map/pallas_call | solution.py:677
  28.2 1.9 %collective-permute-done.4.hi_two = bf16[2,608,128]{2,1,0:T(8,128)(2,1)S(1)} collective-permute-done((bf16[2,608,128]{2,1,0:T(8,128)(2,1)S(1)}, bf16[2,608,128]{2,1,0:T(8,128)(2,1)S(1)}, u32[]{:S(2)}, u32[]{:S(2)}) %collective-permute-start.4) | collective-permute-done | bytes 311328 | tf_op jit(solution)/shard_map/ppermute | solution.py:675
  30.1 9.9 %shard_map.157 = (bf16[10,656,128]{2,1,0:T(8,128)(2,1)S(1)}, bf16[5,656,128]{2,1,0:T(8,128)(2,1)S(1)}, bf16[8,656,128]{2,1,0:T(8,128)(2,1)S(1)}, bf16[6,656,128]...) custom-call(f32[6400,128]{1,0:T(8,128)S(1)} %shard_map.153.splat_ref, ...), custom_call_target="tpu_custom_call" | custom-call | flops 14000000000 | bytes 4000000 | tf_op jit(solution)/shard_map/pallas_call | solution.py:692
  40.0 1.3 %collective-permute-start.10 = (bf16[4,560,128]{2,1,0:T(8,128)(2,1)S(1)}, bf16[4,560,128]{2,1,0:T(8,128)(2,1)S(1)}, u32[]{:S(2)}, u32[]{:S(2)}) collective-permute-start(bf16[4,560,128]{2,1,0:T(8,128)(2,1)S(1)} %get-tuple-element.60), channel_id=1, source_target_pairs={{2,0},{3,1},{4,2},{5,3},{6,4},{7,5},{10,8},{11,9},{12,10},{13,11},... | collective-permute-start | bytes 1720328 | tf_op jit(solution)/shard_map/ppermute | solution.py:716
  41.3 4.8 %collective-permute-start.9 = (bf16[4,560,128]{2,1,0:T(8,128)(2,1)S(1)}, bf16[4,560,128]{2,1,0:T(8,128)(2,1)S(1)}, u32[]{:S(2)}, u32[]{:S(2)}) collective-permute-start(bf16[4,560,128]{2,1,0:T(8,128)(2,1)S(1)} %get-tuple-element.59), channel_id=1, source_target_pairs={{0,2},{1,3},{2,4},{3,5},{4,6},{5,7},{8,10},{9,11},{10,12},{11,13},... | collective-permute-start | bytes 1720328 | tf_op jit(solution)/shard_map/ppermute | solution.py:715
  47.3 2.4 %collective-permute-done.5 = f32[8,128]{1,0:T(8,128)S(1)} collective-permute-done((f32[8,128]{1,0:T(8,128)S(1)}, f32[8,128]{1,0:T(8,128)S(1)}, u32[]{:S(2)}, u32[]{:S(2)}) %collective-permute-start.5) | collective-permute-done | bytes 4128 | tf_op jit(solution)/shard_map/ppermute | solution.py:704
  49.7 1.5 %collective-permute-start.6 = (f32[8,128]{1,0:T(8,128)S(1)}, f32[8,128]{1,0:T(8,128)S(1)}, u32[]{:S(2)}, u32[]{:S(2)}) collective-permute-start(f32[8,128]{1,0:T(8,128)S(1)} %add.24.refs_0_), channel_id=1, source_target_pairs={{0,2},{1,3},{2,0},{3,1},{4,6},{5,7},{6,4},{7,5},{8,10},{9,11},{10,... | collective-permute-start | bytes 12296 | tf_op jit(solution)/shard_map/ppermute | solution.py:704
  51.3 1.0 collective-permute-start.7
  52.3 1.8 %collective-permute-start.8 = (f32[8,128]{1,0:T(8,128)S(1)}, f32[8,128]{1,0:T(8,128)S(1)}, u32[]{:S(2)}, u32[]{:S(2)}) collective-permute-start(f32[8,128]{1,0:T(8,128)S(1)} %add.24.refs_0_), channel_id=1, source_target_pairs={{0,6},{1,7},{2,4},{3,5},{4,2},{5,3},{6,0},{7,1},{8,14},{9,15},{10,... | collective-permute-start | bytes 12296 | tf_op jit(solution)/shard_map/ppermute | solution.py:704
  54.1 2.1 %shard_map.158 = (f32[9,32,128]{2,1,0:T(8,128)S(1)}, bf16[3,656,128]{2,1,0:T(8,128)(2,1)S(1)}) custom-call(bf16[4,560,128]{2,1,0:T(8,128)(2,1)S(1)} %get-tuple-element.55.m3_ref.refs_11_, bf16[6,656,128]{2,1,0:T(8,128)(2,1)S(1)} %get-tuple-element.56.h2_ref.refs_10_, bf16[3,656,128]{2,1,0:T(8,128)(2,1)S(1)} %get-tuple-element.57.e2_ref, ...), custom_call_target="tpu_custom_call" | custom-call | flops 3000000000 | bytes 4000000 | tf_op jit(solution)/shard_map/pallas_call | solution.py:718
  56.3 1.4 %collective-permute-done.8.refs_3_ = f32[8,128]{1,0:T(8,128)S(1)} collective-permute-done((f32[8,128]{1,0:T(8,128)S(1)}, f32[8,128]{1,0:T(8,128)S(1)}, u32[]{:S(2)}, u32[]{:S(2)}) %collective-permute-start.8) | collective-permute-done | bytes 4128 | tf_op jit(solution)/shard_map/ppermute | solution.py:704
  57.7 12.0 %shard_map.159 = (f32[384,128]{1,0:T(8,128)S(1)}, f32[384,128]{1,0:T(8,128)S(1)}, f32[1]{0:T(128)}, f32[1]{0:T(128)}, bf16[128,2048]{1,0:T(8,128)(2,1)S(1)}) custom-call(s32[1]{0:T(128)S(6)} %copy.24.label, f32[8,128]{1,0:T(8,128)S(1)} %add.24.refs_0_, f32[8,128]{1,0:T(8,128)S(1)} %collective-permute-done.6.refs_1_, ...), custom_call_target="tpu_custom_call" | custom-call | flops 14000000000 | bytes 4000000 | tf_op jit(solution)/shard_map/pallas_call | solution.py:731
  69.9 1.4 %collective-permute-done.11 = f32[384,128]{1,0:T(8,128)S(1)} collective-permute-done((f32[384,128]{1,0:T(8,128)S(1)}, f32[384,128]{1,0:T(8,128)S(1)}, u32[]{:S(2)}, u32[]{:S(2)}) %collective-permute-start.11) | collective-permute-done | bytes 196640 | tf_op jit(solution)/shard_map/ppermute | solution.py:751
  72.0 5.2 %all-to-all-start = ((f32[16,24,128]{2,1,0:T(8,128)}), f32[16,24,128]{2,1,0:T(8,128)S(1)}, u32[]{:S(2)}, u32[]{:S(2)}) async-start(f32[16,24,128]{2,1,0:T(8,128)} %bitcast.11), calls=%async_computation | async-start | bytes 393216 | tf_op jit(solution)/shard_map/all_to_all | solution.py:752
  77.2 7.3 %shard_map.160 = f32[3,2048]{1,0:T(4,128)S(1)} custom-call(s32[1]{0:T(128)S(6)} %copy.23.count, f32[28]{0:T(128)S(1)} %copy-done.5, f32[3,1,2048]{2,1,0:T(1,128)S(1)} %bitcast.40, s32[1,2048]{1,0:T(1,128)S(1)} %copy-done.4, bf16[128,2048]{1,0:T(8,128)(2,1)S(1)} %get-tuple-element.67.dk_ref), custom_call_target="tpu_custom_call" | custom-call | flops 10000000000 | bytes 4000000 | tf_op jit(solution)/shard_map/pallas_call | solution.py:753
  84.6 1.3 %all-to-all-done = f32[16,24,128]{2,1,0:T(8,128)S(1)} async-done(((f32[16,24,128]{2,1,0:T(8,128)}), f32[16,24,128]{2,1,0:T(8,128)S(1)}, u32[]{:S(2)}, u32[]{:S(2)}) %all-to-all-start) | async-done | bytes 196640 | tf_op jit(solution)/shard_map/all_to_all | solution.py:752
  86.6 5.6 %all-to-all-start.1 = ((f32[16,24,128]{2,1,0:T(8,128)}), f32[16,24,128]{2,1,0:T(8,128)S(1)}, u32[]{:S(2)}, u32[]{:S(2)}) async-start(f32[16,24,128]{2,1,0:T(8,128)} %broadcast_in_dim.2), calls=%async_computation.1 | async-start | bytes 393216 | tf_op jit(solution)/shard_map/all_to_all | solution.py:766
  92.2 1.9 %collective-permute-start.13 = (f32[3,2048]{1,0:T(4,128)S(1)}, f32[3,2048]{1,0:T(4,128)S(1)}, u32[]{:S(2)}, u32[]{:S(2)}) collective-permute-start(f32[3,2048]{1,0:T(4,128)S(1)} %shard_map.160), channel_id=1, source_target_pairs={{0,1},{1,0},{2,3},{3,2},{4,5},{5,4},{6,7},{7,6},{8,9},{9,8},{10,11... | collective-permute-start | bytes 73736 | tf_op jit(solution)/shard_map/ppermute | solution.py:704
  94.1 2.4 %collective-permute-done.13 = f32[3,2048]{1,0:T(4,128)S(1)} collective-permute-done((f32[3,2048]{1,0:T(4,128)S(1)}, f32[3,2048]{1,0:T(4,128)S(1)}, u32[]{:S(2)}, u32[]{:S(2)}) %collective-permute-start.13) | collective-permute-done | bytes 24608 | tf_op jit(solution)/shard_map/ppermute | solution.py:704
  96.5 3.0 %collective-permute-start.14 = (f32[3,2048]{1,0:T(4,128)S(1)}, f32[3,2048]{1,0:T(4,128)S(1)}, u32[]{:S(2)}, u32[]{:S(2)}) collective-permute-start(f32[3,2048]{1,0:T(4,128)S(1)} %add.26), channel_id=1, source_target_pairs={{0,4},{1,5},{2,6},{3,7},{4,0},{5,1},{6,2},{7,3},{8,12},{9,13},{10,... | collective-permute-start | bytes 73736 | tf_op jit(solution)/shard_map/ppermute | solution.py:704
  99.5 1.4 %collective-permute-start.15 = (f32[3,2048]{1,0:T(4,128)S(1)}, f32[3,2048]{1,0:T(4,128)S(1)}, u32[]{:S(2)}, u32[]{:S(2)}) collective-permute-start(f32[3,2048]{1,0:T(4,128)S(1)} %add.26), channel_id=1, source_target_pairs={{0,2},{1,3},{2,0},{3,1},{4,6},{5,7},{6,4},{7,5},{8,10},{9,11},{10,... | collective-permute-start | bytes 73736 | tf_op jit(solution)/shard_map/ppermute | solution.py:704
  101.6 2.1 %collective-permute-done.15 = f32[3,2048]{1,0:T(4,128)S(1)} collective-permute-done((f32[3,2048]{1,0:T(4,128)S(1)}, f32[3,2048]{1,0:T(4,128)S(1)}, u32[]{:S(2)}, u32[]{:S(2)}) %collective-permute-start.15) | collective-permute-done | bytes 24608 | tf_op jit(solution)/shard_map/ppermute | solution.py:704
  103.6 3.0 %collective-permute-done.16 = f32[3,2048]{1,0:T(4,128)S(1)} collective-permute-done((f32[3,2048]{1,0:T(4,128)S(1)}, f32[3,2048]{1,0:T(4,128)S(1)}, u32[]{:S(2)}, u32[]{:S(2)}) %collective-permute-start.16) | collective-permute-done | bytes 24608 | tf_op jit(solution)/shard_map/ppermute | solution.py:704
  106.6 1.3 %shard_map.161 = (f32[27,32,28]{2,1,0:T(8,128)}, f32[27,32,32]{2,1,0:T(8,128)}, f32[27,32,32]{2,1,0:T(8,128)}, f32[1,32]{1,0:T(1,128)}, f32[3,1,2048]{2,1,0:T(1,128)}) custom-call(f32[384,128]{1,0:T(8,128)S(1)} %bitcast.34, f32[384,128]{1,0:T(8,128)S(1)} %collective-permute-done.12.other_ref, f32[3,2048]{1,0:T(4,128)S(1)} %add_add_fusion.sum_ref), custom_call_target="tpu_custom_call" | custom-call | flops 100000000 | bytes 4000000 | tf_op jit(solution)/shard_map/pallas_call | solution.py:773
  (40 shorter events, 4.1 us)
Async XLA Ops:
  1.9 13.1 %collective-permute-start.1 = (bf16[2,28,2560]{2,1,0:T(8,128)(2,1)S(1)}, bf16[2,28,2560]{2,1,0:T(8,128)(2,1)S(1)}, u32[]{:S(2)}, u32[]{:S(2)}) collective-permute-start(bf16[2,28,2560]{2,1,0:T(8,128)(2,1)S(1)} %bitcast.41), channel_id=1, source_target_pairs={{0,1},{1,0},{2,3},{3,2},{4,5},{5,4},{6,7},{7,6},{8,9},{9,8},{10,11... | collective-permute-start | bytes 860168 | tf_op jit(solution)/shard_map/ppermute | solution.py:645
  6.2 5.4 %copy-start.6 = (f32[32]{0:T(128)S(1)}, f32[32]{0:T(128)}, u32[]{:S(2)}) copy-start(f32[32]{0:T(128)} %param.19) | copy-start | bytes 388
  6.2 6.1 %copy-start = (bf16[32,28,3,3,3]{1,0,4,3,2:T(8,128)(2,1)S(1)}, bf16[32,28,3,3,3]{1,0,4,3,2:T(8,128)(2,1)}, u32[]{:S(2)}) copy-start(bf16[32,28,3,3,3]{1,0,4,3,2:T(8,128)(2,1)} %param.16) | copy-start | bytes 145156
  6.2 6.1 %copy-start.1 = (bf16[32,32,3,3,3]{1,0,4,3,2:T(8,128)(2,1)S(1)}, bf16[32,32,3,3,3]{1,0,4,3,2:T(8,128)(2,1)}, u32[]{:S(2)}) copy-start(bf16[32,32,3,3,3]{1,0,4,3,2:T(8,128)(2,1)} %param.17) | copy-start | bytes 165892
  6.2 6.1 %copy-start.2 = (bf16[32,32,3,3,3]{1,0,4,3,2:T(8,128)(2,1)S(1)}, bf16[32,32,3,3,3]{1,0,4,3,2:T(8,128)(2,1)}, u32[]{:S(2)}) copy-start(bf16[32,32,3,3,3]{1,0,4,3,2:T(8,128)(2,1)} %param.18) | copy-start | bytes 165892
  6.8 21.4 %collective-permute-start = (bf16[608,128]{1,0:T(8,128)(2,1)S(1)}, bf16[608,128]{1,0:T(8,128)(2,1)S(1)}, u32[]{:S(2)}, u32[]{:S(2)}) collective-permute-start(bf16[608,128]{1,0:T(8,128)(2,1)S(1)} %get-tuple-element.41.high_ref), channel_id=1, source_target_pairs={{0,2},{1,3},{2,4},{3,5},{4,6},{5,7},{8,10},{9,11},{10,12},{11,13},... | collective-permute-start | bytes 466952 | tf_op jit(solution)/shard_map/ppermute | solution.py:657
  10.3 17.9 %collective-permute-start.3 = (bf16[608,128]{1,0:T(8,128)(2,1)S(1)}, bf16[608,128]{1,0:T(8,128)(2,1)S(1)}, u32[]{:S(2)}, u32[]{:S(2)}) collective-permute-start(bf16[608,128]{1,0:T(8,128)(2,1)S(1)} %get-tuple-element.45.low_ref), channel_id=1, source_target_pairs={{2,0},{3,1},{4,2},{5,3},{6,4},{7,5},{10,8},{11,9},{12,10},{13,11},... | collective-permute-start | bytes 466952 | tf_op jit(solution)/shard_map/ppermute | solution.py:658
  15.0 6.5 %copy-start.3 = (f32[1,3,2048]{2,0,1:T(1,128)S(1)}, f32[1,3,2048]{2,0,1:T(1,128)}, u32[]{:S(2)}) copy-start(f32[1,3,2048]{2,0,1:T(1,128)} %param.10) | copy-start | bytes 73732
  15.0 6.5 %copy-start.4 = (s32[1,2048]{1,0:T(1,128)S(1)}, s32[1,2048]{1,0:T(1,128)}, u32[]{:S(2)}) copy-start(s32[1,2048]{1,0:T(1,128)} %types_ref.3) | copy-start | bytes 24580
  15.0 6.5 %copy-start.5 = (f32[28]{0:T(128)S(1)}, f32[28]{0:T(128)}, u32[]{:S(2)}) copy-start(f32[28]{0:T(128)} %radii.3) | copy-start | bytes 340
  15.6 12.6 %collective-permute-start.2 = (bf16[2,608,128]{2,1,0:T(8,128)(2,1)S(1)}, bf16[2,608,128]{2,1,0:T(8,128)(2,1)S(1)}, u32[]{:S(2)}, u32[]{:S(2)}) collective-permute-start(bf16[2,608,128]{2,1,0:T(8,128)(2,1)S(1)} %get-tuple-element.46), channel_id=1, source_target_pairs={{0,2},{1,3},{2,4},{3,5},{4,6},{5,7},{8,10},{9,11},{10,12},{11,13},... | collective-permute-start | bytes 933896 | tf_op jit(solution)/shard_map/ppermute | solution.py:674
  20.2 9.9 %collective-permute-start.4 = (bf16[2,608,128]{2,1,0:T(8,128)(2,1)S(1)}, bf16[2,608,128]{2,1,0:T(8,128)(2,1)S(1)}, u32[]{:S(2)}, u32[]{:S(2)}) collective-permute-start(bf16[2,608,128]{2,1,0:T(8,128)(2,1)S(1)} %get-tuple-element.48), channel_id=1, source_target_pairs={{2,0},{3,1},{4,2},{5,3},{6,4},{7,5},{10,8},{11,9},{12,10},{13,11},... | collective-permute-start | bytes 933896 | tf_op jit(solution)/shard_map/ppermute | solution.py:675
  40.0 17.7 %collective-permute-start.10 = (bf16[4,560,128]{2,1,0:T(8,128)(2,1)S(1)}, bf16[4,560,128]{2,1,0:T(8,128)(2,1)S(1)}, u32[]{:S(2)}, u32[]{:S(2)}) collective-permute-start(bf16[4,560,128]{2,1,0:T(8,128)(2,1)S(1)} %get-tuple-element.60), channel_id=1, source_target_pairs={{2,0},{3,1},{4,2},{5,3},{6,4},{7,5},{10,8},{11,9},{12,10},{13,11},... | collective-permute-start | bytes 1720328 | tf_op jit(solution)/shard_map/ppermute | solution.py:716
  41.3 16.4 %collective-permute-start.9 = (bf16[4,560,128]{2,1,0:T(8,128)(2,1)S(1)}, bf16[4,560,128]{2,1,0:T(8,128)(2,1)S(1)}, u32[]{:S(2)}, u32[]{:S(2)}) collective-permute-start(bf16[4,560,128]{2,1,0:T(8,128)(2,1)S(1)} %get-tuple-element.59), channel_id=1, source_target_pairs={{0,2},{1,3},{2,4},{3,5},{4,6},{5,7},{8,10},{9,11},{10,12},{11,13},... | collective-permute-start | bytes 1720328 | tf_op jit(solution)/shard_map/ppermute | solution.py:715
  46.1 3.7 %collective-permute-start.5 = (f32[8,128]{1,0:T(8,128)S(1)}, f32[8,128]{1,0:T(8,128)S(1)}, u32[]{:S(2)}, u32[]{:S(2)}) collective-permute-start(f32[8,128]{1,0:T(8,128)S(1)} %get-tuple-element.50.refs_4_), channel_id=1, source_target_pairs={{0,1},{1,0},{2,3},{3,2},{4,5},{5,4},{6,7},{7,6},{8,9},{9,8},{10,11... | collective-permute-start | bytes 12296 | tf_op jit(solution)/shard_map/ppermute | solution.py:704
  49.7 6.5 %collective-permute-start.6 = (f32[8,128]{1,0:T(8,128)S(1)}, f32[8,128]{1,0:T(8,128)S(1)}, u32[]{:S(2)}, u32[]{:S(2)}) collective-permute-start(f32[8,128]{1,0:T(8,128)S(1)} %add.24.refs_0_), channel_id=1, source_target_pairs={{0,2},{1,3},{2,0},{3,1},{4,6},{5,7},{6,4},{7,5},{8,10},{9,11},{10,... | collective-permute-start | bytes 12296 | tf_op jit(solution)/shard_map/ppermute | solution.py:704
  51.3 5.0 %collective-permute-start.7 = (f32[8,128]{1,0:T(8,128)S(1)}, f32[8,128]{1,0:T(8,128)S(1)}, u32[]{:S(2)}, u32[]{:S(2)}) collective-permute-start(f32[8,128]{1,0:T(8,128)S(1)} %add.24.refs_0_), channel_id=1, source_target_pairs={{0,4},{1,5},{2,6},{3,7},{4,0},{5,1},{6,2},{7,3},{8,12},{9,13},{10,... | collective-permute-start | bytes 12296 | tf_op jit(solution)/shard_map/ppermute | solution.py:704
  52.3 5.4 %collective-permute-start.8 = (f32[8,128]{1,0:T(8,128)S(1)}, f32[8,128]{1,0:T(8,128)S(1)}, u32[]{:S(2)}, u32[]{:S(2)}) collective-permute-start(f32[8,128]{1,0:T(8,128)S(1)} %add.24.refs_0_), channel_id=1, source_target_pairs={{0,6},{1,7},{2,4},{3,5},{4,2},{5,3},{6,0},{7,1},{8,14},{9,15},{10,... | collective-permute-start | bytes 12296 | tf_op jit(solution)/shard_map/ppermute | solution.py:704
  69.8 1.5 %collective-permute-start.11 = (f32[384,128]{1,0:T(8,128)S(1)}, f32[384,128]{1,0:T(8,128)S(1)}, u32[]{:S(2)}, u32[]{:S(2)}) collective-permute-start(f32[384,128]{1,0:T(8,128)S(1)} %get-tuple-element.66), channel_id=1, source_target_pairs={{0,8},{8,0},{1,9},{9,1},{2,10},{10,2},{3,11},{11,3},{4,12},{12,4},... | collective-permute-start | bytes 589832 | tf_op jit(solution)/shard_map/ppermute | solution.py:751
  72.0 13.9 %all-to-all-start = ((f32[16,24,128]{2,1,0:T(8,128)}), f32[16,24,128]{2,1,0:T(8,128)S(1)}, u32[]{:S(2)}, u32[]{:S(2)}) async-start(f32[16,24,128]{2,1,0:T(8,128)} %bitcast.11), calls=%async_computation | async-start | bytes 393216 | tf_op jit(solution)/shard_map/all_to_all | solution.py:752
  86.6 14.4 %all-to-all-start.1 = ((f32[16,24,128]{2,1,0:T(8,128)}), f32[16,24,128]{2,1,0:T(8,128)S(1)}, u32[]{:S(2)}, u32[]{:S(2)}) async-start(f32[16,24,128]{2,1,0:T(8,128)} %broadcast_in_dim.2), calls=%async_computation.1 | async-start | bytes 393216 | tf_op jit(solution)/shard_map/all_to_all | solution.py:766
  92.2 4.3 %collective-permute-start.13 = (f32[3,2048]{1,0:T(4,128)S(1)}, f32[3,2048]{1,0:T(4,128)S(1)}, u32[]{:S(2)}, u32[]{:S(2)}) collective-permute-start(f32[3,2048]{1,0:T(4,128)S(1)} %shard_map.160), channel_id=1, source_target_pairs={{0,1},{1,0},{2,3},{3,2},{4,5},{5,4},{6,7},{7,6},{8,9},{9,8},{10,11... | collective-permute-start | bytes 73736 | tf_op jit(solution)/shard_map/ppermute | solution.py:704
  96.5 5.1 %collective-permute-start.14 = (f32[3,2048]{1,0:T(4,128)S(1)}, f32[3,2048]{1,0:T(4,128)S(1)}, u32[]{:S(2)}, u32[]{:S(2)}) collective-permute-start(f32[3,2048]{1,0:T(4,128)S(1)} %add.26), channel_id=1, source_target_pairs={{0,4},{1,5},{2,6},{3,7},{4,0},{5,1},{6,2},{7,3},{8,12},{9,13},{10,... | collective-permute-start | bytes 73736 | tf_op jit(solution)/shard_map/ppermute | solution.py:704
  99.5 4.2 %collective-permute-start.15 = (f32[3,2048]{1,0:T(4,128)S(1)}, f32[3,2048]{1,0:T(4,128)S(1)}, u32[]{:S(2)}, u32[]{:S(2)}) collective-permute-start(f32[3,2048]{1,0:T(4,128)S(1)} %add.26), channel_id=1, source_target_pairs={{0,2},{1,3},{2,0},{3,1},{4,6},{5,7},{6,4},{7,5},{8,10},{9,11},{10,... | collective-permute-start | bytes 73736 | tf_op jit(solution)/shard_map/ppermute | solution.py:704
  100.9 5.7 %collective-permute-start.16 = (f32[3,2048]{1,0:T(4,128)S(1)}, f32[3,2048]{1,0:T(4,128)S(1)}, u32[]{:S(2)}, u32[]{:S(2)}) collective-permute-start(f32[3,2048]{1,0:T(4,128)S(1)} %add.26), channel_id=1, source_target_pairs={{0,6},{1,7},{2,4},{3,5},{4,2},{5,3},{6,0},{7,1},{8,14},{9,15},{10,... | collective-permute-start | bytes 73736 | tf_op jit(solution)/shard_map/ppermute | solution.py:704
  101.0 5.6 %collective-permute-start.12 = (f32[384,128]{1,0:T(8,128)S(1)}, f32[384,128]{1,0:T(8,128)S(1)}, u32[]{:S(2)}, u32[]{:S(2)}) collective-permute-start(f32[384,128]{1,0:T(8,128)S(1)} %bitcast.33), channel_id=1, source_target_pairs={{0,8},{8,0},{1,9},{9,1},{2,10},{10,2},{3,11},{11,3},{4,12},{12,4},... | collective-permute-start | bytes 589832 | tf_op jit(solution)/shard_map/ppermute | solution.py:768

commit v4 on v3

--- a/solution.py
+++ b/solution.py
@@ -201,7 +201,7 @@
         dn_ref[k] = own_ref[1 - h + k]
 
 
-def weights_kernel(stem_ref, one_ref, two_ref, wf_ref, wb_ref, u_ref):
+def weights_kernel(stem_ref, one_ref, two_ref, wf_ref, u_ref):
     flip = place()[1]
     for conv, ref in enumerate((stem_ref, one_ref, two_ref)):
         channels = ref.shape[2]
@@ -213,7 +213,6 @@
                 tile = tile + (pltpu.roll(block, 32 * g, 1) if g else block)
             u_ref[conv * 9 + k] = tile
         build_forward(u_ref, conv, flip, wf_ref.at[conv])
-        build_backward(u_ref, conv, flip, wb_ref.at[conv])
 
 
 def atom_terms(radii, types):
@@ -282,6 +281,10 @@
         z = first + q
         return jnp.where((z >= 0) & (z < depth), 1.0, 0.0)
 
+    def kept(acc, q):
+        parts = acc[:, :128], acc[:, 128:]
+        return [v if 3 <= q + k < 7 else v * inside(q + k) for k, v in enumerate(parts)]
+
     def receptor(q, sl):
         if q < 3:
             return rim_ref[0, q, sl, :]
@@ -296,7 +299,7 @@
             vals = []
             for q in (2 * m, 2 * m + 1):
                 v = splat_ref[pl.ds(pl.multiple_of(q * 640 + at, 16), 304), :] + receptor(q, sl).astype(f32)
-                vals.append(rounded(v * inside(q)))
+                vals.append(v if 3 <= q < 7 else v * inside(q))
             put_pair(x_ref, ex_ref, 2 * m, m, pl.multiple_of(JB + at, 16), *vals)
             return carry
 
@@ -306,10 +309,9 @@
     def stem(m, carry):
         acc_ref = accs_ref.at[m % 2]
         conv_pair(x_ref, ex_ref, 2 * m, m, RS, w_ref.at[0], acc_ref, NT)
-        ia, ib = inside(2 * m + 1), inside(2 * m + 2)
         for c in range(NCH):
             acc = jnp.maximum(acc_ref[pl.ds(c * CH, CH), :], 0.0)
-            put_pair(h1_ref, e1_ref, 2 * m, m, JB + c * CH, rounded(acc[:, :128] * ia), rounded(acc[:, 128:] * ib))
+            put_pair(h1_ref, e1_ref, 2 * m, m, JB + c * CH, *kept(acc, 2 * m + 1))
         return carry
 
     for m in range(4):
@@ -318,10 +320,9 @@
     def second(m, carry):
         acc_ref = accs_ref.at[m % 2]
         conv_pair(h1_ref, e1_ref, 2 * m, m, R2, w_ref.at[1], acc_ref, NT)
-        ia, ib = inside(2 * m + 2), inside(2 * m + 3)
         for c in range(NCH):
             acc = jnp.maximum(acc_ref[pl.ds(c * CH, CH), :], 0.0)
-            put_pair(h2_ref, e2_ref, 2 * m, m, JB + c * CH, rounded(acc[:, :128] * ia), rounded(acc[:, 128:] * ib))
+            put_pair(h2_ref, e2_ref, 2 * m, m, JB + c * CH, *kept(acc, 2 * m + 2))
         return carry
 
     for m in range(3):
@@ -396,8 +397,10 @@
     lax.fori_loop(0, 3, body, 0)
 
 
-def prepare_kernel(m3_ref, h2_ref, e2_ref, h1_ref, gw_ref, e1_ref, g_ref):
+def prepare_kernel(m3_ref, h2_ref, e2_ref, h1_ref, u_ref, gw_ref, e1_ref, wb_ref, g_ref):
     flip = place()[1]
+    for conv in range(3):
+        build_backward(u_ref, conv, flip, wb_ref.at[conv])
     clear_pad(e1_ref)
     for m in range(3):
         for c in range(5):
@@ -479,7 +482,7 @@
         for c in range(NCH):
             sl = pl.ds(c * 112, 112)
             vals = [
-                rounded(jnp.where(hm_ref[2 * m + k, sl, :].astype(f32) > 0.0, acc_ref[sl, pl.ds(128 * k, 128)], 0.0))
+                jnp.where(hm_ref[2 * m + k, sl, :].astype(f32) > 0.0, acc_ref[sl, pl.ds(128 * k, 128)], 0.0)
                 for k in range(2)
             ]
             put_pair(mg_ref, em_ref, 2 * m, m, JB + c * 112, *vals)
@@ -502,7 +505,7 @@
             vals = []
             for k in range(2):
                 back = t_ref[2 * m + 2 + k, src, :].astype(f32) + acc_ref[sl, pl.ds(128 * k, 128)]
-                vals.append(rounded(jnp.where(h1_ref[2 * m + 1 + k, src, :].astype(f32) > 0.0, back, 0.0)))
+                vals.append(jnp.where(h1_ref[2 * m + 1 + k, src, :].astype(f32) > 0.0, back, 0.0))
             put_pair(sg_ref, es_ref, 2 * m, m, JB + c * 112, *vals)
         return carry
 
@@ -522,7 +525,7 @@
         conv_pair(sg_ref, es_ref, 2 * m, m, OWN, w_ref.at[0], acc_ref, NN)
         for k in range(2):
             at = pl.ds(pl.multiple_of((2 * m + k) * OWN * JB, 16), OWN * JB)
-            dg_ref[at, :] = rounded(acc_ref[pl.ds(0, OWN * JB), pl.ds(128 * k, 128)])
+            dg_ref[at, :] = acc_ref[pl.ds(0, OWN * JB), pl.ds(128 * k, 128)]
         return carry
 
     for m in range(2):
@@ -656,14 +659,7 @@
     downs = [(i + 2, i) for i in range(slab_count - 2)]
     lo_one = lax.ppermute(high, "slab", ups)
     hi_one = lax.ppermute(low, "slab", downs)
-    wf, wb = call(
-        weights_kernel, 6, 3e9,
-        out_shape=[jax.ShapeDtypeStruct((3, 256, 2304), bf16), jax.ShapeDtypeStruct((3, 2304, 256), bf16)],
-        in_specs=[vmem()] * 3,
-        out_specs=[vmem()] * 2,
-        scratch_shapes=[pltpu.VMEM((27, 32, 128), f32)],
-    )(offsets(w_stem), offsets(w_one), offsets(w_two))
-    other, wf, wb, head = lax.optimization_barrier((other, wf, wb, head))
+    other, head = lax.optimization_barrier((other, head))
     own, own_up, own_dn = call(
         pack_kernel, 6, 2e9,
         out_shape=[jax.ShapeDtypeStruct((n,) + bh, bf16) for n in (4, 2, 2)],
@@ -674,6 +670,13 @@
     lo_two = lax.ppermute(own_up, "slab", ups)
     hi_two = lax.ppermute(own_dn, "slab", downs)
 
+    own, w_stem, w_one, w_two = lax.optimization_barrier((own, w_stem, w_one, w_two))
+    wf, u = call(
+        weights_kernel, 6, 3e9,
+        out_shape=[jax.ShapeDtypeStruct((3, 256, 2304), bf16), jax.ShapeDtypeStruct((27, 32, 128), f32)],
+        in_specs=[vmem()] * 3,
+        out_specs=[vmem()] * 2,
+    )(offsets(w_stem), offsets(w_one), offsets(w_two))
     splat = call(
         functools.partial(splat_kernel, depth), 10, 8e9,
         out_shape=jax.ShapeDtypeStruct((6400, 128), f32),
@@ -715,13 +718,13 @@
     from_lo = lax.ppermute(up, "slab", ups)
     from_hi = lax.ppermute(dn, "slab", downs)
     pools = slab_terms(pool)
-    gw2, e1 = call(
+    gw2, e1, wb = call(
         prepare_kernel, 8, 3e9,
-        out_shape=[jax.ShapeDtypeStruct((9, 32, 128), f32), big(3)],
-        in_specs=[vmem()] * 4,
-        out_specs=[vmem()] * 2,
+        out_shape=[jax.ShapeDtypeStruct((9, 32, 128), f32), big(3), jax.ShapeDtypeStruct((3, 2304, 256), bf16)],
+        in_specs=[vmem()] * 5,
+        out_specs=[vmem()] * 3,
         scratch_shapes=[pltpu.VMEM((3, 256, 768), f32)],
-    )(m3, h2, e2, h1)
+    )(m3, h2, e2, h1, u)
 
     ranks = y_count * slab_count
     each = -(-680 // (2 * ranks))

time: 108 us -> 107 us (level)
  waiting for transfers between devices: 16.5 us -> 14.2 us
  starting transfers between devices: 42 us -> 43.4 us
    ppermute x1, waiting for transfers between devices: 1.86 us -> 0.31 us  [local(): hi_two = lax.ppermute(own_dn, 'slab', downs)]
    ppermute x8, waiting for transfers between devices: 11.8 us -> 10.7 us  [swapped(): lax.ppermute(value, 'slab', [(i, i ^ bits) for i in range(slab_count)])]
    pallas_call x1, Pallas kernels: 2.6 us -> 1.48 us  [local(): call(weights_kernel, 6, 3000000000.0, out_shape=[jax.ShapeDtypeStruct((3,...]
  transfers between devices with their start and end apart: 19 -> 19, of which waited for: 9 -> 10; matrix products, arithmetic and copies ran while one was open for 1% -> 1% of each run, Pallas kernels for 18% -> 18%
where the time goes in v4:
time: 107 us
  starting transfers between devices  43.4 us (41%)
  Pallas kernels  43 us (40%)
  waiting for transfers between devices  14.2 us (13%)
  local copies, waits for them, and re-layouts  3.3 us (3%)
  between operations  2.27 us (2%)
    pallas_call x1, Pallas kernels, local(): call(functools.partial(backward_kernel, depth, len(pools)), 18, 140000000...  12 us
    ppermute x8, starting transfers between devices, swapped(): lax.ppermute(value, 'slab', [(i, i ^ bits) for i in range(slab_count)])  11.9 us
    ppermute x8, waiting for transfers between devices, swapped(): lax.ppermute(value, 'slab', [(i, i ^ bits) for i in range(slab_count)])  10.7 us
    pallas_call x1, Pallas kernels, local(): call(functools.partial(forward_kernel, depth), 8, 14000000000.0, out_shap...  9.96 us
    pallas_call x1, Pallas kernels, local(): call(functools.partial(atom_kernel, depth), 12, 10000000000.0, out_shape=...  7.21 us
    pallas_call x1, Pallas kernels, local(): call(functools.partial(splat_kernel, depth), 10, 8000000000.0, out_shape=...  6.64 us
    all_to_all x1, starting transfers between devices, local(): got = lax.all_to_all(chip.reshape(ranks, each, 128), ('y', 'slab'), 0, 0)  6.2 us
    all_to_all x1, starting transfers between devices, local(): gathered = lax.all_to_all(spread_total, ('y', 'slab'), 0, 0)  5.46 us
  transfers between devices with their start and end apart: 19, of which 10 were waited for; matrix products, arithmetic and copies ran while one was open for 1% of the time, Pallas kernels for 18%

profile of v4, /device:TPU:0, one launch (start us, length us, event | category | flops | bytes accessed | tf_op | source)
XLA Modules:
  0.0 106.9 jit_solution(10177782686520966973)
XLA Ops:
  0.6 1.2 %constant_dynamic-slice_fusion = bf16[1,28,2,2560]{3,2,1,0:T(2,128)(2,1)S(1)} fusion(bf16[1,28,2,4096]{3,2,1,0:T(2,128)(2,1)} %param.14, s32[]{:T(128)S(6)} %select_n.13), kind=kLoop, calls=%fused_computation.3 | loop fusion | bytes 573444 | tf_op jit(solution)/shard_map/dynamic-slice.1
  1.9 3.0 %collective-permute-start.1 = (bf16[2,28,2560]{2,1,0:T(8,128)(2,1)S(1)}, bf16[2,28,2560]{2,1,0:T(8,128)(2,1)S(1)}, u32[]{:S(2)}, u32[]{:S(2)}) collective-permute-start(bf16[2,28,2560]{2,1,0:T(8,128)(2,1)S(1)} %bitcast.41), channel_id=1, source_target_pairs={{0,1},{1,0},{2,3},{3,2},{4,5},{5,4},{6,7},{7,6},{8,9},{9,8},{10,11... | collective-permute-start | bytes 860168 | tf_op jit(solution)/shard_map/ppermute | solution.py:648
  4.9 1.3 %copy.21 = bf16[1,28,2,4096]{3,1,2,0:T(8,128)(2,1)S(1)} copy(bf16[1,28,2,4096]{3,2,1,0:T(2,128)(2,1)} %param.14) | data formatting | bytes 917504 | tf_op args[4]
  6.7 3.5 %collective-permute-start = (bf16[608,128]{1,0:T(8,128)(2,1)S(1)}, bf16[608,128]{1,0:T(8,128)(2,1)S(1)}, u32[]{:S(2)}, u32[]{:S(2)}) collective-permute-start(bf16[608,128]{1,0:T(8,128)(2,1)S(1)} %get-tuple-element.44.high_ref), channel_id=1, source_target_pairs={{0,2},{1,3},{2,4},{3,5},{4,6},{5,7},{8,10},{9,11},{10,12},{11,13},... | collective-permute-start | bytes 466952 | tf_op jit(solution)/shard_map/ppermute | solution.py:660
  10.2 1.3 %collective-permute-start.3 = (bf16[608,128]{1,0:T(8,128)(2,1)S(1)}, bf16[608,128]{1,0:T(8,128)(2,1)S(1)}, u32[]{:S(2)}, u32[]{:S(2)}) collective-permute-start(bf16[608,128]{1,0:T(8,128)(2,1)S(1)} %get-tuple-element.46.low_ref), channel_id=1, source_target_pairs={{2,0},{3,1},{4,2},{5,3},{6,4},{7,5},{10,8},{11,9},{12,10},{13,11},... | collective-permute-start | bytes 466952 | tf_op jit(solution)/shard_map/ppermute | solution.py:661
  13.2 4.3 %collective-permute-start.2 = (bf16[2,608,128]{2,1,0:T(8,128)(2,1)S(1)}, bf16[2,608,128]{2,1,0:T(8,128)(2,1)S(1)}, u32[]{:S(2)}, u32[]{:S(2)}) collective-permute-start(bf16[2,608,128]{2,1,0:T(8,128)(2,1)S(1)} %get-tuple-element.47), channel_id=1, source_target_pairs={{0,2},{1,3},{2,4},{3,5},{4,6},{5,7},{8,10},{9,11},{10,12},{11,13},... | collective-permute-start | bytes 933896 | tf_op jit(solution)/shard_map/ppermute | solution.py:670
  17.5 1.3 %collective-permute-start.4 = (bf16[2,608,128]{2,1,0:T(8,128)(2,1)S(1)}, bf16[2,608,128]{2,1,0:T(8,128)(2,1)S(1)}, u32[]{:S(2)}, u32[]{:S(2)}) collective-permute-start(bf16[2,608,128]{2,1,0:T(8,128)(2,1)S(1)} %get-tuple-element.50), channel_id=1, source_target_pairs={{2,0},{3,1},{4,2},{5,3},{6,4},{7,5},{10,8},{11,9},{12,10},{13,11},... | collective-permute-start | bytes 933896 | tf_op jit(solution)/shard_map/ppermute | solution.py:671
  18.9 6.6 %shard_map.153.splat_ref = f32[6400,128]{1,0:T(8,128)S(1)} custom-call(s32[1]{0:T(128)S(6)} %copy.23.count, f32[28]{0:T(128)S(1)} %copy-done.5, f32[3,1,2048]{2,1,0:T(1,128)S(1)} %bitcast.39, s32[1,2048]{1,0:T(1,128)S(1)} %copy-done.4), custom_call_target="tpu_custom_call" | custom-call | flops 8000000000 | bytes 4000000 | tf_op jit(solution)/shard_map/pallas_call | solution.py:680
  25.6 1.5 %shard_map.156 = (bf16[3,256,2304]{2,1,0:T(8,128)(2,1)S(1)}, f32[27,32,128]{2,1,0:T(8,128)S(1)}) custom-call(bf16[27,32,28]{2,1,0:T(8,128)(2,1)S(1)} %bitcast.36, bf16[27,32,32]{2,1,0:T(8,128)(2,1)S(1)} %bitcast.37, bf16[27,32,32]{2,1,0:T(8,128)(2,1)S(1)} %bitcast.38), custom_call_target="tpu_custom_call" | custom-call | flops 3000000000 | bytes 4000000 | tf_op jit(solution)/shard_map/pallas_call | solution.py:674
  27.4 10.0 %shard_map.157 = (bf16[10,656,128]{2,1,0:T(8,128)(2,1)S(1)}, bf16[5,656,128]{2,1,0:T(8,128)(2,1)S(1)}, bf16[8,656,128]{2,1,0:T(8,128)(2,1)S(1)}, bf16[6,656,128]...) custom-call(f32[6400,128]{1,0:T(8,128)S(1)} %shard_map.153.splat_ref, ...), custom_call_target="tpu_custom_call" | custom-call | flops 14000000000 | bytes 4000000 | tf_op jit(solution)/shard_map/pallas_call | solution.py:695
  37.3 1.3 %collective-permute-start.10 = (bf16[4,560,128]{2,1,0:T(8,128)(2,1)S(1)}, bf16[4,560,128]{2,1,0:T(8,128)(2,1)S(1)}, u32[]{:S(2)}, u32[]{:S(2)}) collective-permute-start(bf16[4,560,128]{2,1,0:T(8,128)(2,1)S(1)} %get-tuple-element.66), channel_id=1, source_target_pairs={{2,0},{3,1},{4,2},{5,3},{6,4},{7,5},{10,8},{11,9},{12,10},{13,11},... | collective-permute-start | bytes 1720328 | tf_op jit(solution)/shard_map/ppermute | solution.py:719
  38.6 5.1 %collective-permute-start.9 = (bf16[4,560,128]{2,1,0:T(8,128)(2,1)S(1)}, bf16[4,560,128]{2,1,0:T(8,128)(2,1)S(1)}, u32[]{:S(2)}, u32[]{:S(2)}) collective-permute-start(bf16[4,560,128]{2,1,0:T(8,128)(2,1)S(1)} %get-tuple-element.65), channel_id=1, source_target_pairs={{0,2},{1,3},{2,4},{3,5},{4,6},{5,7},{8,10},{9,11},{10,12},{11,13},... | collective-permute-start | bytes 1720328 | tf_op jit(solution)/shard_map/ppermute | solution.py:718
  43.7 1.0 collective-permute-start.5
  45.4 2.0 %collective-permute-done.5 = f32[8,128]{1,0:T(8,128)S(1)} collective-permute-done((f32[8,128]{1,0:T(8,128)S(1)}, f32[8,128]{1,0:T(8,128)S(1)}, u32[]{:S(2)}, u32[]{:S(2)}) %collective-permute-start.5) | collective-permute-done | bytes 4128 | tf_op jit(solution)/shard_map/ppermute | solution.py:707
  47.4 2.0 %collective-permute-start.6 = (f32[8,128]{1,0:T(8,128)S(1)}, f32[8,128]{1,0:T(8,128)S(1)}, u32[]{:S(2)}, u32[]{:S(2)}) collective-permute-start(f32[8,128]{1,0:T(8,128)S(1)} %add.24.refs_0_), channel_id=1, source_target_pairs={{0,2},{1,3},{2,0},{3,1},{4,6},{5,7},{6,4},{7,5},{8,10},{9,11},{10,... | collective-permute-start | bytes 12296 | tf_op jit(solution)/shard_map/ppermute | solution.py:707
  49.4 1.0 collective-permute-start.7
  50.4 1.5 %collective-permute-start.8 = (f32[8,128]{1,0:T(8,128)S(1)}, f32[8,128]{1,0:T(8,128)S(1)}, u32[]{:S(2)}, u32[]{:S(2)}) collective-permute-start(f32[8,128]{1,0:T(8,128)S(1)} %add.24.refs_0_), channel_id=1, source_target_pairs={{0,6},{1,7},{2,4},{3,5},{4,2},{5,3},{6,0},{7,1},{8,14},{9,15},{10,... | collective-permute-start | bytes 12296 | tf_op jit(solution)/shard_map/ppermute | solution.py:707
  51.9 3.2 %shard_map.158 = (f32[9,32,128]{2,1,0:T(8,128)S(1)}, bf16[3,656,128]{2,1,0:T(8,128)(2,1)S(1)}, bf16[3,2304,256]{2,1,0:T(8,128)(2,1)S(1)}) custom-call(bf16[4,560,128]{2,1,0:T(8,128)(2,1)S(1)} %get-tuple-element.60.m3_ref.refs_11_, bf16[6,656,128]{2,1,0:T(8,128)(2,1)S(1)} %get-tuple-element.61.h2_ref.refs_10_, ...), custom_call_target="tpu_custom_call" | custom-call | flops 3000000000 | bytes 4000000 | tf_op jit(solution)/shard_map/pallas_call | solution.py:721
  55.1 0.7 collective-permute-done.8.refs_3_
  55.8 12.0 %shard_map.159 = (f32[384,128]{1,0:T(8,128)S(1)}, f32[384,128]{1,0:T(8,128)S(1)}, f32[1]{0:T(128)}, f32[1]{0:T(128)}, bf16[128,2048]{1,0:T(8,128)(2,1)S(1)}) custom-call(s32[1]{0:T(128)S(6)} %copy.24.label, f32[8,128]{1,0:T(8,128)S(1)} %add.24.refs_0_, f32[8,128]{1,0:T(8,128)S(1)} %collective-permute-done.6.refs_1_, ...), custom_call_target="tpu_custom_call" | custom-call | flops 14000000000 | bytes 4000000 | tf_op jit(solution)/shard_map/pallas_call | solution.py:734
  67.9 1.4 %collective-permute-done.11 = f32[384,128]{1,0:T(8,128)S(1)} collective-permute-done((f32[384,128]{1,0:T(8,128)S(1)}, f32[384,128]{1,0:T(8,128)S(1)}, u32[]{:S(2)}, u32[]{:S(2)}) %collective-permute-start.11) | collective-permute-done | bytes 196640 | tf_op jit(solution)/shard_map/ppermute | solution.py:754
  70.1 6.2 %all-to-all-start = ((f32[16,24,128]{2,1,0:T(8,128)}), f32[16,24,128]{2,1,0:T(8,128)S(1)}, u32[]{:S(2)}, u32[]{:S(2)}) async-start(f32[16,24,128]{2,1,0:T(8,128)} %bitcast.11), calls=%async_computation | async-start | bytes 393216 | tf_op jit(solution)/shard_map/all_to_all | solution.py:755
  76.3 7.2 %shard_map.160 = f32[3,2048]{1,0:T(4,128)S(1)} custom-call(s32[1]{0:T(128)S(6)} %copy.23.count, f32[28]{0:T(128)S(1)} %copy-done.5, f32[3,1,2048]{2,1,0:T(1,128)S(1)} %bitcast.40, s32[1,2048]{1,0:T(1,128)S(1)} %copy-done.4, bf16[128,2048]{1,0:T(8,128)(2,1)S(1)} %get-tuple-element.73.dk_ref), custom_call_target="tpu_custom_call" | custom-call | flops 10000000000 | bytes 4000000 | tf_op jit(solution)/shard_map/pallas_call | solution.py:756
  83.5 1.5 %all-to-all-done = f32[16,24,128]{2,1,0:T(8,128)S(1)} async-done(((f32[16,24,128]{2,1,0:T(8,128)}), f32[16,24,128]{2,1,0:T(8,128)S(1)}, u32[]{:S(2)}, u32[]{:S(2)}) %all-to-all-start) | async-done | bytes 196640 | tf_op jit(solution)/shard_map/all_to_all | solution.py:755
  85.7 5.5 %all-to-all-start.1 = ((f32[16,24,128]{2,1,0:T(8,128)}), f32[16,24,128]{2,1,0:T(8,128)S(1)}, u32[]{:S(2)}, u32[]{:S(2)}) async-start(f32[16,24,128]{2,1,0:T(8,128)} %broadcast_in_dim.2), calls=%async_computation.1 | async-start | bytes 393216 | tf_op jit(solution)/shard_map/all_to_all | solution.py:769
  91.1 1.9 %collective-permute-start.13 = (f32[3,2048]{1,0:T(4,128)S(1)}, f32[3,2048]{1,0:T(4,128)S(1)}, u32[]{:S(2)}, u32[]{:S(2)}) collective-permute-start(f32[3,2048]{1,0:T(4,128)S(1)} %shard_map.160), channel_id=1, source_target_pairs={{0,1},{1,0},{2,3},{3,2},{4,5},{5,4},{6,7},{7,6},{8,9},{9,8},{10,11... | collective-permute-start | bytes 73736 | tf_op jit(solution)/shard_map/ppermute | solution.py:707
  93.1 2.4 %collective-permute-done.13 = f32[3,2048]{1,0:T(4,128)S(1)} collective-permute-done((f32[3,2048]{1,0:T(4,128)S(1)}, f32[3,2048]{1,0:T(4,128)S(1)}, u32[]{:S(2)}, u32[]{:S(2)}) %collective-permute-start.13) | collective-permute-done | bytes 24608 | tf_op jit(solution)/shard_map/ppermute | solution.py:707
  95.4 3.0 %collective-permute-start.14 = (f32[3,2048]{1,0:T(4,128)S(1)}, f32[3,2048]{1,0:T(4,128)S(1)}, u32[]{:S(2)}, u32[]{:S(2)}) collective-permute-start(f32[3,2048]{1,0:T(4,128)S(1)} %add.26), channel_id=1, source_target_pairs={{0,4},{1,5},{2,6},{3,7},{4,0},{5,1},{6,2},{7,3},{8,12},{9,13},{10,... | collective-permute-start | bytes 73736 | tf_op jit(solution)/shard_map/ppermute | solution.py:707
  98.4 1.4 %collective-permute-start.15 = (f32[3,2048]{1,0:T(4,128)S(1)}, f32[3,2048]{1,0:T(4,128)S(1)}, u32[]{:S(2)}, u32[]{:S(2)}) collective-permute-start(f32[3,2048]{1,0:T(4,128)S(1)} %add.26), channel_id=1, source_target_pairs={{0,2},{1,3},{2,0},{3,1},{4,6},{5,7},{6,4},{7,5},{8,10},{9,11},{10,... | collective-permute-start | bytes 73736 | tf_op jit(solution)/shard_map/ppermute | solution.py:707
  100.5 2.1 %collective-permute-done.15 = f32[3,2048]{1,0:T(4,128)S(1)} collective-permute-done((f32[3,2048]{1,0:T(4,128)S(1)}, f32[3,2048]{1,0:T(4,128)S(1)}, u32[]{:S(2)}, u32[]{:S(2)}) %collective-permute-start.15) | collective-permute-done | bytes 24608 | tf_op jit(solution)/shard_map/ppermute | solution.py:707
  102.6 2.9 %collective-permute-done.16 = f32[3,2048]{1,0:T(4,128)S(1)} collective-permute-done((f32[3,2048]{1,0:T(4,128)S(1)}, f32[3,2048]{1,0:T(4,128)S(1)}, u32[]{:S(2)}, u32[]{:S(2)}) %collective-permute-start.16) | collective-permute-done | bytes 24608 | tf_op jit(solution)/shard_map/ppermute | solution.py:707
  105.6 1.3 %shard_map.161 = (f32[27,32,28]{2,1,0:T(8,128)}, f32[27,32,32]{2,1,0:T(8,128)}, f32[27,32,32]{2,1,0:T(8,128)}, f32[1,32]{1,0:T(1,128)}, f32[3,1,2048]{2,1,0:T(1,128)}) custom-call(f32[384,128]{1,0:T(8,128)S(1)} %bitcast.34, f32[384,128]{1,0:T(8,128)S(1)} %collective-permute-done.12.other_ref, f32[3,2048]{1,0:T(4,128)S(1)} %add_add_fusion.sum_ref), custom_call_target="tpu_custom_call" | custom-call | flops 100000000 | bytes 4000000 | tf_op jit(solution)/shard_map/pallas_call | solution.py:776
  (40 shorter events, 4.1 us)
Async XLA Ops:
  1.9 10.7 %collective-permute-start.1 = (bf16[2,28,2560]{2,1,0:T(8,128)(2,1)S(1)}, bf16[2,28,2560]{2,1,0:T(8,128)(2,1)S(1)}, u32[]{:S(2)}, u32[]{:S(2)}) collective-permute-start(bf16[2,28,2560]{2,1,0:T(8,128)(2,1)S(1)} %bitcast.41), channel_id=1, source_target_pairs={{0,1},{1,0},{2,3},{3,2},{4,5},{5,4},{6,7},{7,6},{8,9},{9,8},{10,11... | collective-permute-start | bytes 860168 | tf_op jit(solution)/shard_map/ppermute | solution.py:648
  6.2 5.4 %copy-start.6 = (f32[32]{0:T(128)S(1)}, f32[32]{0:T(128)}, u32[]{:S(2)}) copy-start(f32[32]{0:T(128)} %param.19) | copy-start | bytes 388
  6.7 20.3 %collective-permute-start = (bf16[608,128]{1,0:T(8,128)(2,1)S(1)}, bf16[608,128]{1,0:T(8,128)(2,1)S(1)}, u32[]{:S(2)}, u32[]{:S(2)}) collective-permute-start(bf16[608,128]{1,0:T(8,128)(2,1)S(1)} %get-tuple-element.44.high_ref), channel_id=1, source_target_pairs={{0,2},{1,3},{2,4},{3,5},{4,6},{5,7},{8,10},{9,11},{10,12},{11,13},... | collective-permute-start | bytes 466952 | tf_op jit(solution)/shard_map/ppermute | solution.py:660
  10.2 16.8 %collective-permute-start.3 = (bf16[608,128]{1,0:T(8,128)(2,1)S(1)}, bf16[608,128]{1,0:T(8,128)(2,1)S(1)}, u32[]{:S(2)}, u32[]{:S(2)}) collective-permute-start(bf16[608,128]{1,0:T(8,128)(2,1)S(1)} %get-tuple-element.46.low_ref), channel_id=1, source_target_pairs={{2,0},{3,1},{4,2},{5,3},{6,4},{7,5},{10,8},{11,9},{12,10},{13,11},... | collective-permute-start | bytes 466952 | tf_op jit(solution)/shard_map/ppermute | solution.py:661
  12.3 6.5 %copy-start.3 = (f32[1,3,2048]{2,0,1:T(1,128)S(1)}, f32[1,3,2048]{2,0,1:T(1,128)}, u32[]{:S(2)}) copy-start(f32[1,3,2048]{2,0,1:T(1,128)} %param.10) | copy-start | bytes 73732
  12.3 6.5 %copy-start.4 = (s32[1,2048]{1,0:T(1,128)S(1)}, s32[1,2048]{1,0:T(1,128)}, u32[]{:S(2)}) copy-start(s32[1,2048]{1,0:T(1,128)} %types_ref.3) | copy-start | bytes 24580
  12.3 6.5 %copy-start.5 = (f32[28]{0:T(128)S(1)}, f32[28]{0:T(128)}, u32[]{:S(2)}) copy-start(f32[28]{0:T(128)} %radii.3) | copy-start | bytes 340
  13.2 13.9 %collective-permute-start.2 = (bf16[2,608,128]{2,1,0:T(8,128)(2,1)S(1)}, bf16[2,608,128]{2,1,0:T(8,128)(2,1)S(1)}, u32[]{:S(2)}, u32[]{:S(2)}) collective-permute-start(bf16[2,608,128]{2,1,0:T(8,128)(2,1)S(1)} %get-tuple-element.47), channel_id=1, source_target_pairs={{0,2},{1,3},{2,4},{3,5},{4,6},{5,7},{8,10},{9,11},{10,12},{11,13},... | collective-permute-start | bytes 933896 | tf_op jit(solution)/shard_map/ppermute | solution.py:670
  17.5 9.9 %collective-permute-start.4 = (bf16[2,608,128]{2,1,0:T(8,128)(2,1)S(1)}, bf16[2,608,128]{2,1,0:T(8,128)(2,1)S(1)}, u32[]{:S(2)}, u32[]{:S(2)}) collective-permute-start(bf16[2,608,128]{2,1,0:T(8,128)(2,1)S(1)} %get-tuple-element.50), channel_id=1, source_target_pairs={{2,0},{3,1},{4,2},{5,3},{6,4},{7,5},{10,8},{11,9},{12,10},{13,11},... | collective-permute-start | bytes 933896 | tf_op jit(solution)/shard_map/ppermute | solution.py:671
  18.8 6.7 %copy-start = (bf16[32,28,3,3,3]{1,0,4,3,2:T(8,128)(2,1)S(1)}, bf16[32,28,3,3,3]{1,0,4,3,2:T(8,128)(2,1)}, u32[]{:S(2)}) copy-start(bf16[32,28,3,3,3]{1,0,4,3,2:T(8,128)(2,1)} %param.16) | copy-start | bytes 145156
  18.9 6.7 %copy-start.1 = (bf16[32,32,3,3,3]{1,0,4,3,2:T(8,128)(2,1)S(1)}, bf16[32,32,3,3,3]{1,0,4,3,2:T(8,128)(2,1)}, u32[]{:S(2)}) copy-start(bf16[32,32,3,3,3]{1,0,4,3,2:T(8,128)(2,1)} %param.17) | copy-start | bytes 165892
  18.9 6.7 %copy-start.2 = (bf16[32,32,3,3,3]{1,0,4,3,2:T(8,128)(2,1)S(1)}, bf16[32,32,3,3,3]{1,0,4,3,2:T(8,128)(2,1)}, u32[]{:S(2)}) copy-start(bf16[32,32,3,3,3]{1,0,4,3,2:T(8,128)(2,1)} %param.18) | copy-start | bytes 165892
  37.3 18.5 %collective-permute-start.10 = (bf16[4,560,128]{2,1,0:T(8,128)(2,1)S(1)}, bf16[4,560,128]{2,1,0:T(8,128)(2,1)S(1)}, u32[]{:S(2)}, u32[]{:S(2)}) collective-permute-start(bf16[4,560,128]{2,1,0:T(8,128)(2,1)S(1)} %get-tuple-element.66), channel_id=1, source_target_pairs={{2,0},{3,1},{4,2},{5,3},{6,4},{7,5},{10,8},{11,9},{12,10},{13,11},... | collective-permute-start | bytes 1720328 | tf_op jit(solution)/shard_map/ppermute | solution.py:719
  38.6 17.2 %collective-permute-start.9 = (bf16[4,560,128]{2,1,0:T(8,128)(2,1)S(1)}, bf16[4,560,128]{2,1,0:T(8,128)(2,1)S(1)}, u32[]{:S(2)}, u32[]{:S(2)}) collective-permute-start(bf16[4,560,128]{2,1,0:T(8,128)(2,1)S(1)} %get-tuple-element.65), channel_id=1, source_target_pairs={{0,2},{1,3},{2,4},{3,5},{4,6},{5,7},{8,10},{9,11},{10,12},{11,13},... | collective-permute-start | bytes 1720328 | tf_op jit(solution)/shard_map/ppermute | solution.py:718
  43.7 3.7 %collective-permute-start.5 = (f32[8,128]{1,0:T(8,128)S(1)}, f32[8,128]{1,0:T(8,128)S(1)}, u32[]{:S(2)}, u32[]{:S(2)}) collective-permute-start(f32[8,128]{1,0:T(8,128)S(1)} %get-tuple-element.55.refs_4_), channel_id=1, source_target_pairs={{0,1},{1,0},{2,3},{3,2},{4,5},{5,4},{6,7},{7,6},{8,9},{9,8},{10,11... | collective-permute-start | bytes 12296 | tf_op jit(solution)/shard_map/ppermute | solution.py:707
  47.4 7.7 %collective-permute-start.6 = (f32[8,128]{1,0:T(8,128)S(1)}, f32[8,128]{1,0:T(8,128)S(1)}, u32[]{:S(2)}, u32[]{:S(2)}) collective-permute-start(f32[8,128]{1,0:T(8,128)S(1)} %add.24.refs_0_), channel_id=1, source_target_pairs={{0,2},{1,3},{2,0},{3,1},{4,6},{5,7},{6,4},{7,5},{8,10},{9,11},{10,... | collective-permute-start | bytes 12296 | tf_op jit(solution)/shard_map/ppermute | solution.py:707
  49.4 5.7 %collective-permute-start.7 = (f32[8,128]{1,0:T(8,128)S(1)}, f32[8,128]{1,0:T(8,128)S(1)}, u32[]{:S(2)}, u32[]{:S(2)}) collective-permute-start(f32[8,128]{1,0:T(8,128)S(1)} %add.24.refs_0_), channel_id=1, source_target_pairs={{0,4},{1,5},{2,6},{3,7},{4,0},{5,1},{6,2},{7,3},{8,12},{9,13},{10,... | collective-permute-start | bytes 12296 | tf_op jit(solution)/shard_map/ppermute | solution.py:707
  50.4 5.4 %collective-permute-start.8 = (f32[8,128]{1,0:T(8,128)S(1)}, f32[8,128]{1,0:T(8,128)S(1)}, u32[]{:S(2)}, u32[]{:S(2)}) collective-permute-start(f32[8,128]{1,0:T(8,128)S(1)} %add.24.refs_0_), channel_id=1, source_target_pairs={{0,6},{1,7},{2,4},{3,5},{4,2},{5,3},{6,0},{7,1},{8,14},{9,15},{10,... | collective-permute-start | bytes 12296 | tf_op jit(solution)/shard_map/ppermute | solution.py:707
  67.9 1.5 %collective-permute-start.11 = (f32[384,128]{1,0:T(8,128)S(1)}, f32[384,128]{1,0:T(8,128)S(1)}, u32[]{:S(2)}, u32[]{:S(2)}) collective-permute-start(f32[384,128]{1,0:T(8,128)S(1)} %get-tuple-element.72), channel_id=1, source_target_pairs={{0,8},{8,0},{1,9},{9,1},{2,10},{10,2},{3,11},{11,3},{4,12},{12,4},... | collective-permute-start | bytes 589832 | tf_op jit(solution)/shard_map/ppermute | solution.py:754
  70.1 14.9 %all-to-all-start = ((f32[16,24,128]{2,1,0:T(8,128)}), f32[16,24,128]{2,1,0:T(8,128)S(1)}, u32[]{:S(2)}, u32[]{:S(2)}) async-start(f32[16,24,128]{2,1,0:T(8,128)} %bitcast.11), calls=%async_computation | async-start | bytes 393216 | tf_op jit(solution)/shard_map/all_to_all | solution.py:755
  85.7 14.3 %all-to-all-start.1 = ((f32[16,24,128]{2,1,0:T(8,128)}), f32[16,24,128]{2,1,0:T(8,128)S(1)}, u32[]{:S(2)}, u32[]{:S(2)}) async-start(f32[16,24,128]{2,1,0:T(8,128)} %broadcast_in_dim.2), calls=%async_computation.1 | async-start | bytes 393216 | tf_op jit(solution)/shard_map/all_to_all | solution.py:769
  91.1 4.3 %collective-permute-start.13 = (f32[3,2048]{1,0:T(4,128)S(1)}, f32[3,2048]{1,0:T(4,128)S(1)}, u32[]{:S(2)}, u32[]{:S(2)}) collective-permute-start(f32[3,2048]{1,0:T(4,128)S(1)} %shard_map.160), channel_id=1, source_target_pairs={{0,1},{1,0},{2,3},{3,2},{4,5},{5,4},{6,7},{7,6},{8,9},{9,8},{10,11... | collective-permute-start | bytes 73736 | tf_op jit(solution)/shard_map/ppermute | solution.py:707
  95.4 5.1 %collective-permute-start.14 = (f32[3,2048]{1,0:T(4,128)S(1)}, f32[3,2048]{1,0:T(4,128)S(1)}, u32[]{:S(2)}, u32[]{:S(2)}) collective-permute-start(f32[3,2048]{1,0:T(4,128)S(1)} %add.26), channel_id=1, source_target_pairs={{0,4},{1,5},{2,6},{3,7},{4,0},{5,1},{6,2},{7,3},{8,12},{9,13},{10,... | collective-permute-start | bytes 73736 | tf_op jit(solution)/shard_map/ppermute | solution.py:707
  98.4 4.2 %collective-permute-start.15 = (f32[3,2048]{1,0:T(4,128)S(1)}, f32[3,2048]{1,0:T(4,128)S(1)}, u32[]{:S(2)}, u32[]{:S(2)}) collective-permute-start(f32[3,2048]{1,0:T(4,128)S(1)} %add.26), channel_id=1, source_target_pairs={{0,2},{1,3},{2,0},{3,1},{4,6},{5,7},{6,4},{7,5},{8,10},{9,11},{10,... | collective-permute-start | bytes 73736 | tf_op jit(solution)/shard_map/ppermute | solution.py:707
  99.8 5.7 %collective-permute-start.16 = (f32[3,2048]{1,0:T(4,128)S(1)}, f32[3,2048]{1,0:T(4,128)S(1)}, u32[]{:S(2)}, u32[]{:S(2)}) collective-permute-start(f32[3,2048]{1,0:T(4,128)S(1)} %add.26), channel_id=1, source_target_pairs={{0,6},{1,7},{2,4},{3,5},{4,2},{5,3},{6,0},{7,1},{8,14},{9,15},{10,... | collective-permute-start | bytes 73736 | tf_op jit(solution)/shard_map/ppermute | solution.py:707
  99.9 5.6 %collective-permute-start.12 = (f32[384,128]{1,0:T(8,128)S(1)}, f32[384,128]{1,0:T(8,128)S(1)}, u32[]{:S(2)}, u32[]{:S(2)}) collective-permute-start(f32[384,128]{1,0:T(8,128)S(1)} %bitcast.33), channel_id=1, source_target_pairs={{0,8},{8,0},{1,9},{9,1},{2,10},{10,2},{3,11},{11,3},{4,12},{12,4},... | collective-permute-start | bytes 589832 | tf_op jit(solution)/shard_map/ppermute | solution.py:771
